TPU v7x, 32 devices: a whole 2x2x4 slice. The times are simulated.
32 devices in a mesh: dp: 4 (over y, x), fsdp: 8 (over z, core).
Axes of the slice: x: 2, y: 2, z: 4, core: 2. Of those that a mesh axis runs over, the one named last changes fastest.
Arguments:
- segment_input: bfloat16 [128, 32, 32, 512], P(('dp', 'fsdp')), may hold values from -256 to 256
- cotangent: bfloat16 [128, 16, 16, 1024], P(('dp', 'fsdp')), may hold values from -6 to 6
- tile_centres: int32 [128, 2], P(('dp', 'fsdp')), may hold values from 4 to 28
- valid_mask: int32 [128, 16, 16], P(('dp', 'fsdp')), may hold values from 0 to 1, as said below
- w_down: bfloat16 [512, 9, 1024], P('fsdp'), may hold values from -0.09375 to 0.09375
- w_split: bfloat16 [1024, 1, 1024], P('fsdp'), may hold values from -0.1875 to 0.1875
- w_reduce: bfloat16 [2, 512, 1, 512], P(None, 'fsdp'), may hold values from -0.25 to 0.25
- w_spread: bfloat16 [2, 512, 9, 512], P(None, 'fsdp'), may hold values from -0.09375 to 0.09375
- w_trans: bfloat16 [512, 1, 512], P('fsdp'), may hold values from -0.25 to 0.25
- w_unite: bfloat16 [1024, 1, 1024], P('fsdp'), may hold values from -0.1875 to 0.1875
- bn_gain: float32 [5632], replicated, may hold values from 0.1 to 1.9
- bn_bias: float32 [5632], replicated, may hold values from -3 to 3
- running_mean: float32 [5632], replicated, may hold values from -3 to 3
- running_var: float32 [5632], replicated, may hold values from 0.5 to 2
Outputs:
- output: bfloat16 [128, 16, 16, 1024], P(('dp', 'fsdp'))
- input_grad: bfloat16 [128, 32, 32, 512], P(('dp', 'fsdp'))
- grad_down: float32 [512, 9, 1024], P('fsdp')
- grad_split: float32 [1024, 1, 1024], P('fsdp')
- grad_reduce: float32 [2, 512, 1, 512], P(None, 'fsdp')
- grad_spread: float32 [2, 512, 9, 512], P(None, 'fsdp')
- grad_trans: float32 [512, 1, 512], P('fsdp')
- grad_unite: float32 [1024, 1, 1024], P('fsdp')
- grad_gain: float32 [5632], replicated
- grad_bias: float32 [5632], replicated
- new_running_mean: float32 [5632], replicated
- new_running_var: float32 [5632], replicated
Inputs may be any that keep to these rules, and one draw needn't show every extreme that they name: `valid_mask`: 1 marks a pixel that enters the norms' statistics.
All inputs are finite; a program needn't handle non-finite values.
Results may differ from a plain program's by a relative error of at most 0.03.
Values may be sent and summed in bfloat16 or wider, within the bound.
No kernel may reach another device: no remote copies, remote signals or barrier semaphores. Data moves between devices by JAX's collectives and lax.ppermute only.
A program may use at most 384 MiB of HBM per device.

v0:
```python
import functools

import jax
import jax.numpy as jnp
from jax import lax
from jax.experimental import pallas as pl
from jax.experimental.pallas import tpu as pltpu
from jax.sharding import PartitionSpec as P

norm_eps = 1e-05
momentum_rate = 0.1
ALL = ("dp", "fsdp")
F32 = jnp.float32
BF16 = jnp.bfloat16
VMEM_LIMIT = 58 * 1024 * 1024


def params():
    return pltpu.CompilerParams(vmem_limit_bytes=VMEM_LIMIT)


def tile_masks(centres, grid_side):
    extent = 2 * grid_side
    coords = jnp.arange(extent, dtype=jnp.int32)
    lower_half = (coords[None, :] >= centres[:, 0:1]).astype(jnp.int32)
    right_half = (coords[None, :] >= centres[:, 1:2]).astype(jnp.int32)
    tiles = 2 * lower_half[:, :, None] + right_half[:, None, :]
    fine_pad = jnp.pad(tiles, ((0, 0), (1, 1), (1, 1)), constant_values=-1)
    own_tile = tiles[:, ::2, ::2]
    coarse_pad = jnp.pad(own_tile, ((0, 0), (1, 1), (1, 1)), constant_values=-1)
    down_list, back_list, mid_list = [], [], []
    for a in range(3):
        for b in range(3):
            down = (
                fine_pad[:, a : a + extent : 2, b : b + extent : 2] == own_tile
            ).astype(F32)
            down_list.append(down)
            rows, cols = int(a == 0), int(b == 0)
            back_list.append(jnp.pad(down, ((0, 0), (0, rows), (0, cols)))[:, rows:, cols:])
            mid_list.append(
                (coarse_pad[:, a : a + grid_side, b : b + grid_side] == own_tile).astype(F32)
            )

    def lanes(parts):
        flat = jnp.stack(parts).reshape(9, -1, 1)
        return jnp.broadcast_to(flat, (9, flat.shape[1], 128)).astype(BF16)

    return lanes(down_list), lanes(back_list), lanes(mid_list)


def mish_parts(y):
    u = jnp.exp(-jnp.abs(y))
    pos = y > 0.0
    num = jnp.where(pos, 1.0 + 2.0 * u, u * (u + 2.0))
    gap = jnp.where(pos, 2.0 * u * u, 2.0)
    return u, pos, num, gap, num + gap


def mish(y):
    _, _, num, _, den = mish_parts(y)
    return y * (num / den)


def mish_slope(y):
    u, pos, num, gap, den = mish_parts(y)
    once = 1.0 + u
    both = 1.0 / (den * once)
    inv = both * once
    sig = jnp.where(pos, 1.0, u) * (both * den)
    return num * inv + y * sig * (gap * inv) * ((den + num) * inv)


def mish_both(y):
    u, pos, num, gap, den = mish_parts(y)
    once = 1.0 + u
    both = 1.0 / (den * once)
    inv = both * once
    sig = jnp.where(pos, 1.0, u) * (both * den)
    tan = num * inv
    return y * tan, tan + y * sig * (gap * inv) * ((den + num) * inv)


def col_shift(x, step):
    if step == 0:
        return x
    rows = x.shape[0]
    return pltpu.roll(x.astype(F32), (-step) % rows, 0).astype(BF16)


def row_shift(x, step):
    if step == 0:
        return x
    if step > 0:
        return jnp.concatenate([x[step:], x[:step]], axis=0)
    return jnp.concatenate([x[step:], x[: x.shape[0] + step]], axis=0)


def masked(x, lane_mask):
    reps = x.shape[1] // 128
    return x * jnp.concatenate([lane_mask] * reps, axis=1)


def tap_weight(w_ref, tap):
    w = w_ref[:, tap]
    return w.reshape(w.shape[0] * w.shape[1], w.shape[2])


def dot_nn(a, b):
    return lax.dot_general(a, b, (((1,), (0,)), ((), ())), preferred_element_type=F32)


def dot_nt(a, b):
    return lax.dot_general(a, b, (((1,), (1,)), ((), ())), preferred_element_type=F32)


def dot_tn(a, b):
    return lax.dot_general(a, b, (((0,), (0,)), ((), ())), preferred_element_type=F32)


def mid_taps(x, side):
    cols = [col_shift(x, b - 1) for b in range(3)]
    for tap in range(9):
        a, b = divmod(tap, 3)
        yield tap, row_shift(cols[b], side * (a - 1))


def down_taps(phase, side):
    cols = {}
    for pr in range(2):
        for b in range(3):
            x = phase(2 * pr + int(b != 1))
            cols[pr, b] = col_shift(x, -1) if b == 0 else x
    for tap in range(9):
        a, b = divmod(tap, 3)
        yield tap, row_shift(cols[int(a != 1), b], -side if a == 0 else 0)


def device_total(s_ref):
    count, _, channels = s_ref.shape
    start = jnp.zeros((2, channels), F32)
    return lax.fori_loop(0, count, lambda i, t: t + s_ref[i], start, unroll=8)


def moments(s_ref, cnt_ref):
    count = s_ref.shape[0]
    total = device_total(s_ref)
    inv_n = cnt_ref[2 * count + 1]
    mean = total[0:1] * inv_n

    def spread(i, t):
        d = s_ref[i][0:1] - cnt_ref[i] * mean
        return t + d * d * cnt_ref[count + i]

    between = lax.fori_loop(0, count, spread, jnp.zeros_like(mean), unroll=8)
    var = (total[1:2] + between) * inv_n
    return mean, var, lax.rsqrt(var + norm_eps)


def write_moments(mv_ref, mean, var, inv):
    mv_ref[0:1] = mean
    mv_ref[1:2] = var
    mv_ref[2:3] = inv
    mv_ref[3:8] = jnp.zeros((5, mean.shape[1]), F32)


def collect_moments(out, valid, acc_ref, num_ref, st_ref):
    step = pl.program_id(0)
    n = jnp.sum(valid, axis=0, keepdims=True)
    total = jnp.sum(out * valid, axis=0, keepdims=True)
    mean = total / jnp.maximum(n, 1.0)
    centred = out - mean
    squares = jnp.sum(valid * centred * centred, axis=0, keepdims=True)

    @pl.when(step == 0)
    def _():
        acc_ref[0:1] = total
        acc_ref[1:2] = squares
        num_ref[0:1] = jnp.broadcast_to(n, (1, 128))

    @pl.when(step > 0)
    def _():
        n_old = num_ref[0:1, 0:1]
        n_new = n_old + n
        old_mean = acc_ref[0:1] / jnp.maximum(n_old, 1.0)
        gap = mean - old_mean
        acc_ref[0:1] = acc_ref[0:1] + total
        acc_ref[1:2] = acc_ref[1:2] + squares + gap * gap * (n * n_old / jnp.maximum(n_new, 1.0))
        num_ref[0:1] = jnp.broadcast_to(n_new, (1, 128))

    @pl.when(step == pl.num_programs(0) - 1)
    def _():
        st_ref[...] = jnp.broadcast_to(acc_ref[0:2][None], st_ref.shape)


def collect_sums(g, xhat, acc_ref, st_ref):
    step = pl.program_id(0)
    first = jnp.sum(g, axis=0, keepdims=True)
    second = jnp.sum(g * xhat, axis=0, keepdims=True)

    @pl.when(step == 0)
    def _():
        acc_ref[0:1] = first
        acc_ref[1:2] = second

    @pl.when(step > 0)
    def _():
        acc_ref[0:1] = acc_ref[0:1] + first
        acc_ref[1:2] = acc_ref[1:2] + second

    @pl.when(step == pl.num_programs(0) - 1)
    def _():
        st_ref[...] = jnp.broadcast_to(acc_ref[0:2][None], st_ref.shape)


def prep_kernel(x_ref, ph_ref):
    half = ph_ref.shape[1]
    p = lax.broadcasted_iota(jnp.int32, (half, 2 * half), 0)
    s = lax.broadcasted_iota(jnp.int32, (half, 2 * half), 1)
    for pr in range(2):
        x = x_ref[0, :, pr]
        x = x.reshape(2 * half, x.shape[-1])
        for pc in range(2):
            pick = jnp.where(s == 2 * p + pc, 1.0, 0.0).astype(BF16)
            ph_ref[2 * pr + pc] = dot_nn(pick, x).astype(BF16)


def first_kernel(side, ph_ref, m_ref, valid_ref, w_ref, z_ref, st_ref, acc_ref, num_ref):
    out = None
    for tap, x in down_taps(lambda k: ph_ref[k], side):
        part = dot_nn(masked(x, m_ref[tap]), tap_weight(w_ref, tap))
        out = part if out is None else out + part
    z_ref[...] = out
    collect_moments(out, valid_ref[...], acc_ref, num_ref, st_ref)


def forward_kernel(kind, side, z_ref, s_ref, cnt_ref, gain_ref, bias_ref, valid_ref, w_ref, *rest):
    rest = list(rest)
    m_ref = rest.pop(0) if kind == "three" else None
    other_ref = rest.pop(0) if kind in ("resid", "join") else None
    v_ref = rest.pop(0)
    keep_ref = rest.pop(0) if kind in ("split", "resid") else None
    mv_ref, out_ref, st_ref, acc_ref, num_ref = rest
    mean, var, inv = moments(s_ref, cnt_ref)

    @pl.when(pl.program_id(0) == 0)
    def _():
        write_moments(mv_ref, mean, var, inv)

    act = mish(((z_ref[...] - mean) * inv) * gain_ref[...] + bias_ref[...])
    if kind == "split":
        half = act.shape[1] // 2
        low = act.astype(BF16)
        v_ref[...] = low
        keep_ref[...] = act[:, half:]
        v = low[:, half:]
    elif kind == "resid":
        act = other_ref[...] + act
        keep_ref[...] = act
        v = act.astype(BF16)
        v_ref[...] = v
    elif kind == "join":
        v = jnp.concatenate([other_ref[...], act.astype(BF16)], axis=1)
        v_ref[...] = v
    else:
        v = act.astype(BF16)
        v_ref[...] = v
    if kind == "three":
        out = None
        for tap, x in mid_taps(v, side):
            part = dot_nn(masked(x, m_ref[tap]), tap_weight(w_ref, tap))
            out = part if out is None else out + part
    else:
        out = dot_nn(v, w_ref[...])
    out_ref[...] = out
    collect_moments(out, valid_ref[...], acc_ref, num_ref, st_ref)


def top_kernel(
    z_ref, s_ref, cnt_ref, gain_ref, bias_ref, cot_ref, o_ref, mv_ref, g_ref, st_ref, acc_ref
):
    mean, var, inv = moments(s_ref, cnt_ref)

    @pl.when(pl.program_id(0) == 0)
    def _():
        write_moments(mv_ref, mean, var, inv)

    xhat = (z_ref[...] - mean) * inv
    act, slope = mish_both(xhat * gain_ref[...] + bias_ref[...])
    o_ref[...] = act.astype(BF16)
    g = cot_ref[...].astype(F32) * slope
    g_ref[...] = g
    collect_sums(g, xhat, acc_ref, st_ref)


def norm_grad(g_ref, z_ref, mv_ref, s_ref, gain_ref, valid_ref, cnt_ref, tot_ref):
    total = device_total(s_ref)

    @pl.when(pl.program_id(0) == 0)
    def _():
        tot_ref[0:2] = total
        tot_ref[2:8] = jnp.zeros((6, total.shape[1]), F32)

    inv = mv_ref[2:3]
    inv_n = cnt_ref[2 * s_ref.shape[0] + 1]
    xhat = (z_ref[...] - mv_ref[0:1]) * inv
    mean_part = (valid_ref[...] * inv_n) * (total[0:1] + xhat * total[1:2])
    return (gain_ref[...] * inv * (g_ref[...] - mean_part)).astype(BF16)


def backward_kernel(
    kind,
    side,
    g_ref,
    z_ref,
    mv_ref,
    s_ref,
    gain_ref,
    valid_ref,
    cnt_ref,
    w_ref,
    zp_ref,
    mvp_ref,
    gainp_ref,
    biasp_ref,
    *rest,
):
    rest = list(rest)
    m_ref = rest.pop(0) if kind == "three" else None
    add_ref = rest.pop(0) if kind in ("add", "merge") else None
    route_ref = rest.pop(0) if kind == "merge" else None
    dz_ref, tot_ref = rest.pop(0), rest.pop(0)
    keep_ref = rest.pop(0) if kind in ("part", "keep", "add") else None
    gp_ref, st_ref, acc_ref = rest
    dz = norm_grad(g_ref, z_ref, mv_ref, s_ref, gain_ref, valid_ref, cnt_ref, tot_ref)
    dz_ref[...] = dz
    if kind == "three":
        ga = None
        for tap, x in mid_taps(dz, side):
            part = dot_nt(masked(x, m_ref[tap]), tap_weight(w_ref, 8 - tap))
            ga = part if ga is None else ga + part
    else:
        ga = dot_nt(dz, w_ref[...])
    if kind == "part":
        half = ga.shape[1] // 2
        keep_ref[...] = ga[:, :half]
        ga = ga[:, half:]
    elif kind == "keep":
        keep_ref[...] = ga
    elif kind == "add":
        ga = ga + add_ref[...]
        keep_ref[...] = ga
    elif kind == "merge":
        ga = jnp.concatenate([route_ref[...], ga + add_ref[...]], axis=1)
    xhat = (zp_ref[...] - mvp_ref[0:1]) * mvp_ref[2:3]
    gp = ga * mish_slope(xhat * gainp_ref[...] + biasp_ref[...])
    gp_ref[...] = gp
    collect_sums(gp, xhat, acc_ref, st_ref)


def last_norm_kernel(
    g_ref, z_ref, mv_ref, s_ref, gain_ref, valid_ref, cnt_ref, dz_ref, tot_ref
):
    dz_ref[...] = norm_grad(g_ref, z_ref, mv_ref, s_ref, gain_ref, valid_ref, cnt_ref, tot_ref)


def input_grad_kernel(side, dz_ref, m_ref, w_ref, o_ref):
    dz = dz_ref[...]
    rows = dz.shape[0]
    moved = {}
    for dj in range(2):
        base = col_shift(dz, dj)
        for di in range(2):
            moved[di, dj] = row_shift(base, side * di)
    s = lax.broadcasted_iota(jnp.int32, (2 * rows, 2 * rows), 0)
    k = lax.broadcasted_iota(jnp.int32, (2 * rows, 2 * rows), 1)
    source = jnp.where(k < rows, 2 * k, 2 * (k - rows) + 1)
    put = jnp.where(s == source, 1.0, 0.0).astype(BF16)
    choices = (((1, 0),), ((2, 0), (0, 1)))
    for pr in range(2):
        both = []
        for pc in range(2):
            total = None
            for a, di in choices[pr]:
                for b, dj in choices[pc]:
                    tap = 3 * a + b
                    part = dot_nt(masked(moved[di, dj], m_ref[tap]), tap_weight(w_ref, tap))
                    total = part if total is None else total + part
            both.append(total.astype(BF16))
        out = dot_nn(put, jnp.concatenate(both, axis=0)).astype(BF16)
        o_ref[0, :, pr] = out.reshape(side, 2 * side, out.shape[1])


def weight_grad_kernel(stride, side, x_ref, m_ref, dz_ref, o_ref):
    dz = dz_ref[...]
    taps = mid_taps(x_ref[...], side) if stride == 1 else down_taps(lambda k: x_ref[k], side)
    for tap, x in taps:
        grad = dot_tn(masked(x, m_ref[tap]), dz).astype(BF16)
        o_ref[:, tap] = grad.reshape(o_ref.shape[0], o_ref.shape[2], o_ref.shape[3])


def per_device(
    segment_input,
    cotangent,
    tile_centres,
    valid_mask,
    w_down,
    w_split,
    w_reduce,
    w_spread,
    w_trans,
    w_unite,
    bn_gain,
    bn_bias,
    running_mean,
    running_var,
):
    images, side, _, width = cotangent.shape
    half = w_trans.shape[2]
    c_prev = segment_input.shape[3]
    blocks = w_reduce.shape[0]
    per_image = side * side
    pixels = images * per_image
    fsdp = lax.axis_size("fsdp")
    devices = lax.axis_size("dp") * fsdp
    steps = images
    rows = pixels // steps

    def gather(shard):
        return lax.all_gather(shard, "fsdp", axis=0, tiled=False)

    full_down = gather(w_down.transpose(1, 0, 2))
    full_split = lax.all_gather(w_split[:, 0], "fsdp", axis=0, tiled=True)
    full_unite = lax.all_gather(w_unite[:, 0], "fsdp", axis=0, tiled=True)
    narrow = lax.all_gather(
        jnp.concatenate([w_reduce[b, :, 0] for b in range(blocks)] + [w_trans[:, 0]], axis=1),
        "fsdp",
        axis=0,
        tiled=True,
    )
    full_spread = [gather(w_spread[b].transpose(1, 0, 2)) for b in range(blocks)]

    mask_down, mask_back, mask_mid = tile_masks(tile_centres, side)
    valid = valid_mask.astype(F32).reshape(pixels, 1)
    own_count = jnp.broadcast_to(jnp.sum(valid), (devices, 1, 128))
    counts = lax.all_to_all(own_count, ALL, 0, 0, tiled=True)[:, 0, 0]
    whole_count = jnp.sum(counts)
    cnt = jnp.concatenate(
        [counts, 1.0 / jnp.maximum(counts, 1.0), jnp.stack([whole_count, 1.0 / whole_count])]
    )

    def exchange(st):
        return lax.all_to_all(st, ALL, 0, 0, tiled=True)

    smem = pl.BlockSpec(memory_space=pltpu.SMEM)

    def fixed(shape):
        return pl.BlockSpec(shape, lambda i: (0,) * len(shape))

    def single(shape, index=None):
        index = index or (0,) * len(shape)
        return pl.BlockSpec(shape, lambda i: index, pipeline_mode=pl.Buffered(1))

    def tall(channels, column=0):
        return pl.BlockSpec((rows, channels), lambda i: (i, column))

    mask_spec = pl.BlockSpec((9, rows, 128), lambda i: (0, i, 0))
    valid_spec = pl.BlockSpec((rows, 1), lambda i: (i, 0))

    def shaped(shape, dtype):
        return jax.ShapeDtypeStruct(shape, dtype)

    def stat_shape(channels):
        return shaped((devices, 2, channels), F32)

    widths = [width, width] + [half] * (2 * blocks) + [half, width]
    starts = [sum(widths[:i]) for i in range(len(widths))]
    gains = [bn_gain[s : s + c].reshape(1, c) for s, c in zip(starts, widths)]
    biases = [bn_bias[s : s + c].reshape(1, c) for s, c in zip(starts, widths)]
    layers = len(widths)

    weights = [None] * layers
    weights[0] = (full_down, single(full_down.shape))
    weights[1] = (full_split, single(full_split.shape))
    for b in range(blocks):
        weights[2 + 2 * b] = (narrow, single((half, half), (0, b)))
        weights[3 + 2 * b] = (full_spread[b], single(full_spread[b].shape))
    weights[layers - 2] = (narrow, single((half, half), (0, blocks)))
    weights[layers - 1] = (full_unite, single(full_unite.shape))

    x6 = segment_input.reshape(images, side, 2, 2 * side, c_prev)
    phases = pl.pallas_call(
        prep_kernel,
        grid=(images,),
        in_specs=[pl.BlockSpec((1, side, 2, 2 * side, c_prev), lambda i: (i, 0, 0, 0, 0))],
        out_specs=pl.BlockSpec((4, per_image, c_prev), lambda i: (0, i, 0)),
        out_shape=shaped((4, pixels, c_prev), BF16),
        compiler_params=params(),
        name="parity_images",
    )(x6)

    def scratch(channels):
        return [pltpu.VMEM((8, channels), F32), pltpu.VMEM((8, 128), F32)]

    z, st = [None] * layers, [None] * layers
    z[0], st[0] = pl.pallas_call(
        functools.partial(first_kernel, side),
        grid=(steps,),
        in_specs=[
            pl.BlockSpec((4, rows, c_prev), lambda i: (0, i, 0)),
            mask_spec,
            valid_spec,
            weights[0][1],
        ],
        out_specs=[tall(width), fixed((devices, 2, width))],
        out_shape=[shaped((pixels, width), F32), stat_shape(width)],
        scratch_shapes=scratch(width),
        compiler_params=params(),
        name="down_forward",
    )(phases, mask_down, valid, full_down)

    inputs = [None] * layers
    moment = [None] * layers

    def forward(layer, kind, extra=(), extra_specs=()):
        prev, channels = layer - 1, widths[layer - 1]
        w, w_spec = weights[layer]
        gathered = exchange(st[prev])
        args = [z[prev], gathered, cnt, gains[prev], biases[prev], valid, w, *extra]
        specs = [
            tall(channels),
            fixed((devices, 2, channels)),
            smem,
            fixed((1, channels)),
            fixed((1, channels)),
            valid_spec,
            w_spec,
            *extra_specs,
        ]
        v_width = 2 * half if kind == "join" else channels
        out_specs, out_shape = [tall(v_width)], [shaped((pixels, v_width), BF16)]
        if kind in ("split", "resid"):
            out_specs.append(tall(half))
            out_shape.append(shaped((pixels, half), F32))
        n = widths[layer]
        out_specs += [fixed((8, channels)), tall(n), fixed((devices, 2, n))]
        out_shape += [shaped((8, channels), F32), shaped((pixels, n), F32), stat_shape(n)]
        outs = list(
            pl.pallas_call(
                functools.partial(forward_kernel, kind, side),
                grid=(steps,),
                in_specs=specs,
                out_specs=out_specs,
                out_shape=out_shape,
                scratch_shapes=scratch(n),
                compiler_params=params(),
                name="forward_" + kind,
            )(*args)
        )
        inputs[layer] = outs.pop(0)
        keep = outs.pop(0) if kind in ("split", "resid") else None
        moment[prev], z[layer], st[layer] = outs
        return keep

    forward(1, "plain")
    stream = None
    for b in range(blocks):
        if b == 0:
            stream = forward(2, "split")
        else:
            stream = forward(2 + 2 * b, "resid", (stream,), (tall(half),))
        forward(3 + 2 * b, "three", (mask_mid,), (mask_spec,))
    forward(layers - 2, "resid", (stream,), (tall(half),))
    split_low = inputs[2]
    forward(layers - 1, "join", (split_low,), (tall(half),))

    last = layers - 1
    n = widths[last]
    output, moment[last], g, st_back = pl.pallas_call(
        top_kernel,
        grid=(steps,),
        in_specs=[
            tall(n),
            fixed((devices, 2, n)),
            smem,
            fixed((1, n)),
            fixed((1, n)),
            tall(n),
        ],
        out_specs=[tall(n), fixed((8, n)), tall(n), fixed((devices, 2, n))],
        out_shape=[
            shaped((pixels, n), BF16),
            shaped((8, n), F32),
            shaped((pixels, n), F32),
            stat_shape(n),
        ],
        scratch_shapes=[pltpu.VMEM((8, n), F32)],
        compiler_params=params(),
        name="top",
    )(z[last], exchange(st[last]), cnt, gains[last], biases[last], cotangent.reshape(pixels, n))

    totals = [None] * layers
    dz = [None] * layers

    def backward(layer, kind, g, gathered, extra=(), extra_specs=()):
        prev, channels = layer - 1, widths[layer]
        cp = widths[prev]
        w, w_spec = weights[layer]
        args = [g, z[layer], moment[layer], gathered, gains[layer], valid, cnt, w]
        args += [z[prev], moment[prev], gains[prev], biases[prev], *extra]
        specs = [
            tall(channels),
            tall(channels),
            fixed((8, channels)),
            fixed((devices, 2, channels)),
            fixed((1, channels)),
            valid_spec,
            smem,
            w_spec,
            tall(cp),
            fixed((8, cp)),
            fixed((1, cp)),
            fixed((1, cp)),
            *extra_specs,
        ]
        out_specs = [tall(channels), fixed((8, channels))]
        out_shape = [shaped((pixels, channels), BF16), shaped((8, channels), F32)]
        if kind in ("part", "keep", "add"):
            out_specs.append(tall(half))
            out_shape.append(shaped((pixels, half), F32))
        out_specs += [tall(cp), fixed((devices, 2, cp))]
        out_shape += [shaped((pixels, cp), F32), stat_shape(cp)]
        outs = list(
            pl.pallas_call(
                functools.partial(backward_kernel, kind, side),
                grid=(steps,),
                in_specs=specs,
                out_specs=out_specs,
                out_shape=out_shape,
                scratch_shapes=[pltpu.VMEM((8, cp), F32)],
                compiler_params=params(),
                name="backward_" + kind,
            )(*args)
        )
        dz[layer], totals[layer] = outs.pop(0), outs.pop(0)
        keep = outs.pop(0) if kind in ("part", "keep", "add") else None
        return outs[0], outs[1], keep

    def tap_grad(stride, x, lane_mask, dz_low, w_shape):
        return pl.pallas_call(
            functools.partial(weight_grad_kernel, stride, side),
            out_shape=shaped(w_shape, BF16),
            compiler_params=params(),
            name="weight_grad_" + str(stride),
        )(x, lane_mask, dz_low)

    def flat_grad(x, dz_low):
        return jnp.einsum("pk,pn->kn", x, dz_low, preferred_element_type=F32).astype(BF16)

    def scatter(grad):
        return lax.psum_scatter(grad, "fsdp", scatter_dimension=0, tiled=True)

    def sum_over_groups(own):
        groups = lax.axis_size("dp")
        parts = own.reshape(groups, own.shape[0] // groups, own.shape[1])
        parts = lax.all_to_all(parts, "dp", 0, 0, tiled=True)
        part = jnp.sum(parts.astype(F32), axis=0).astype(BF16)
        back = lax.all_to_all(
            jnp.broadcast_to(part[None], (groups, *part.shape)), "dp", 0, 0, tiled=True
        )
        return back.reshape(own.shape).astype(F32)

    def beside(st_back, grad, *due):
        return lax.optimization_barrier((exchange(st_back), grad, *due))[0]

    g, st_back, grad_route = backward(last, "part", g, exchange(st_back))
    grad_unite = flat_grad(inputs[last], dz[last])
    own_unite = scatter(grad_unite)
    g, st_back, grad_stream = backward(last - 1, "keep", g, beside(st_back, grad_unite))
    narrow_grads = [None] * (blocks + 1)
    narrow_grads[blocks] = flat_grad(inputs[last - 1], dz[last - 1])
    gathered = beside(st_back, narrow_grads[blocks])
    own_spread = [None] * blocks
    for b in reversed(range(blocks)):
        layer = 3 + 2 * b
        g, st_back, _ = backward(layer, "three", g, gathered, (mask_mid,), (mask_spec,))
        own = tap_grad(1, inputs[layer], mask_mid, dz[layer], full_spread[b].shape)
        due = (own_unite,) if b == blocks - 1 else ()
        gathered = beside(st_back, own, *due)
        own_spread[b] = scatter(own)
        layer = 2 + 2 * b
        if b > 0:
            g, st_back, grad_stream = backward(
                layer, "add", g, gathered, (grad_stream,), (tall(half),)
            )
            low = inputs[layer]
        else:
            g, st_back, _ = backward(
                layer, "merge", g, gathered, (grad_stream, grad_route), (tall(half), tall(half))
            )
            low = inputs[layer][:, half:]
        narrow_grads[b] = flat_grad(low, dz[layer])
        due = own_spread[1:2] if b == 0 else ()
        gathered = beside(st_back, narrow_grads[b], *due)
    own_narrow = scatter(jnp.concatenate(narrow_grads, axis=1))
    g, st_back, _ = backward(1, "plain", g, gathered)
    grad_split = flat_grad(inputs[1], dz[1])
    own_split = scatter(grad_split)
    dz[0], totals[0] = pl.pallas_call(
        last_norm_kernel,
        grid=(steps,),
        in_specs=[
            tall(width),
            tall(width),
            fixed((8, width)),
            fixed((devices, 2, width)),
            fixed((1, width)),
            valid_spec,
            smem,
        ],
        out_specs=[tall(width), fixed((8, width))],
        out_shape=[shaped((pixels, width), BF16), shaped((8, width), F32)],
        compiler_params=params(),
        name="down_norm",
    )(g, z[0], moment[0], beside(st_back, grad_split, own_spread[0]), gains[0], valid, cnt)
    grad_down = tap_grad(2, phases, mask_down, dz[0], full_down.shape)
    own_down = scatter(grad_down)
    dz_low, _ = lax.optimization_barrier((dz[0], grad_down))
    input_grad = pl.pallas_call(
        functools.partial(input_grad_kernel, side),
        grid=(images,),
        in_specs=[
            pl.BlockSpec((per_image, width), lambda i: (i, 0)),
            pl.BlockSpec((9, per_image, 128), lambda i: (0, i, 0)),
            weights[0][1],
        ],
        out_specs=pl.BlockSpec((1, side, 2, 2 * side, c_prev), lambda i: (i, 0, 0, 0, 0)),
        out_shape=shaped(x6.shape, BF16),
        compiler_params=params(),
        name="input_grad",
    )(dz_low, mask_back, full_down).reshape(segment_input.shape)

    packed = [own_unite, own_split, own_narrow, *own_spread]
    flat = [o.reshape(-1, half) for o in packed]
    sums = sum_over_groups(jnp.concatenate(flat, axis=0))
    ends = [0]
    for f in flat:
        ends.append(ends[-1] + f.shape[0])
    pieces = [sums[a:e].reshape(o.shape) for a, e, o in zip(ends, ends[1:], packed)]
    grad_unite, grad_split, narrow_grad = pieces[:3]
    spread_grads = [piece[0].transpose(1, 0, 2) for piece in pieces[3:]]
    grad_down = sum_over_groups(own_down.reshape(-1, width)).reshape(own_down.shape)
    grad_down = grad_down[0].transpose(1, 0, 2)

    means = jnp.concatenate([m[0] for m in moment])
    variances = jnp.concatenate([m[1] for m in moment])
    new_mean = (1.0 - momentum_rate) * running_mean + momentum_rate * means
    new_var = (1.0 - momentum_rate) * running_var + momentum_rate * variances * whole_count / (
        whole_count - 1.0
    )
    grad_reduce = jnp.stack([narrow_grad[:, None, half * b : half * (b + 1)] for b in range(blocks)])
    return (
        output.reshape(cotangent.shape),
        input_grad,
        grad_down,
        grad_split[:, None],
        grad_reduce,
        jnp.stack(spread_grads),
        narrow_grad[:, None, half * blocks :],
        grad_unite[:, None],
        jnp.concatenate([t[1] for t in totals]),
        jnp.concatenate([t[0] for t in totals]),
        new_mean,
        new_var,
    )


def solution(mesh):
    image = P(ALL, None, None, None)
    row3 = P("fsdp", None, None)
    row4 = P(None, "fsdp", None, None)
    return jax.shard_map(
        per_device,
        mesh=mesh,
        in_specs=(
            image,
            image,
            P(ALL, None),
            P(ALL, None, None),
            row3,
            row3,
            row4,
            row4,
            row3,
            row3,
            P(),
            P(),
            P(),
            P(),
        ),
        out_specs=(image, image, row3, row3, row4, row4, row3, row3, P(), P(), P(), P()),
        check_vma=False,
    )
```

profile of v0, /device:TPU:0, one launch (start us, length us, event | category | flops | bytes accessed | tf_op | source)
XLA Modules:
  0.0 790.2 jit_solution(10374228775026773891)
XLA Ops:
  14.8 7.3 all-to-all-start.1
  26.0 6.1 parity_images.1.ph_ref.x_ref
  34.1 69.4 %all-gather.14.cloned.1.call-done = bf16[72,64,1024]{2,1,0:T(8,128)(2,1)} async-done(((bf16[9,64,1024]{2,1,0:T(8,128)(2,1)}), bf16[72,64,1024]{2,1,0:T(8,128)(2,1)}) %all-gather.14.cloned.1.call-update) | async-done | bytes 9437200 | tf_op jit(solution)/shard_map/all_gather | solution.py:429
  106.2 16.8 %down_forward.1 = (f32[1024,1024]{1,0:T(8,128)}, f32[32,2,1024]{2,1,0:T(2,128)}) custom-call(bf16[4,1024,512]{2,1,0:T(8,128)(2,1)} %parity_images.1.ph_ref.x_ref, bf16[9,1024,128]{2,1,0:T(8,128)(2,1)} %broadcast_in_dim.14.m_ref, f32[1024,1]{1,0:T(8,128)} %reshape.302.valid_ref, bf16[8,9,64,1024]{3,2,1,0:T(8,128)(2,1)} %bitcast.115), custom_call_target="tpu_custom_call" | custom-call | tf_op jit(solution)/shard_map/down_forward/pallas_call | solution.py:505
  129.3 5.4 all-gather.16.cloned.1.call-done
  134.6 4.2 all-to-all-done.s_ref
  139.6 10.0 %forward_plain.1 = (bf16[1024,1024]{1,0:T(8,128)(2,1)}, f32[8,1024]{1,0:T(8,128)}, f32[1024,1024]{1,0:T(8,128)}, f32[32,2,1024]{2,1,0:T(2,128)}) custom-call(f32[1024,1024]{1,0:T(8,128)} %get-tuple-element.89.z_ref.zp_ref, f32[32,2,1024]{2,1,0:T(2,128)} %copy-done.3, f32[66]{0:T(128)} %pad_maximum_fusion.4.cnt_ref, f32[1,1024]{1,0:T(1,128)} %bitcast.139, ...), custom_call_target="tpu_custom_call" | custom-call | tf_op jit(solution)/shard_map/forward_plain/pallas_call | solution.py:548
  152.2 15.7 %all-gather.12.cloned.1.call-done.w_ref = bf16[512,1536]{1,0:T(8,128)(2,1)} async-done(((bf16[64,1536]{1,0:T(8,128)(2,1)}), bf16[512,1536]{1,0:T(8,128)(2,1)}) %all-gather.12.cloned.1.call-update) | async-done | bytes 1572880 | tf_op jit(solution)/shard_map/all_gather | solution.py:434
  169.1 9.0 %forward_split.1 = (bf16[1024,1024]{1,0:T(8,128)(2,1)}, f32[1024,512]{1,0:T(8,128)}, f32[8,1024]{1,0:T(8,128)}, f32[1024,512]{1,0:T(8,128)}, f32[32,2,512]{2,1,0:T(2,128)}) custom-call(f32[1024,1024]{1,0:T(8,128)} %get-tuple-element.91.z_ref.zp_ref, f32[32,2,1024]{2,1,0:T(2,128)} %copy-done.4, f32[66]{0:T(128)} %pad_maximum_fusion.4.cnt_ref, ...), custom_call_target="tpu_custom_call" | custom-call | tf_op jit(solution)/shard_map/forward_split/pallas_call | solution.py:548
  183.4 39.6 %all-gather.18.cloned.1.call-done = bf16[72,64,512]{2,1,0:T(8,128)(2,1)} async-done(((bf16[9,64,512]{2,1,0:T(8,128)(2,1)}), bf16[72,64,512]{2,1,0:T(8,128)(2,1)}) %all-gather.18.cloned.1.call-update) | async-done | bytes 4718608 | tf_op jit(solution)/shard_map/all_gather | solution.py:429
  225.7 11.8 %forward_three.2 = (bf16[1024,512]{1,0:T(8,128)(2,1)}, f32[8,512]{1,0:T(8,128)}, f32[1024,512]{1,0:T(8,128)}, f32[32,2,512]{2,1,0:T(2,128)}) custom-call(f32[1024,512]{1,0:T(8,128)} %get-tuple-element.93.z_ref.zp_ref, f32[32,2,512]{2,1,0:T(2,128)} %copy-done.9, f32[66]{0:T(128)} %pad_maximum_fusion.4.cnt_ref, f32[1,512]{1,0:T(1,128)} %bitcast.155, ...), custom_call_target="tpu_custom_call" | custom-call | tf_op jit(solution)/shard_map/forward_three/pallas_call | solution.py:548
  237.5 16.1 %all_to_all.105.s_ref = f32[32,2,512]{2,1,0:T(2,128)} all-to-all(f32[32,2,512]{2,1,0:T(2,128)} %get-tuple-element.96), channel_id=1, replica_groups=mesh['dp'=4,'fsdp'=8] {'dp','fsdp'}, dimensions={0} | all-to-all | bytes 262144 | tf_op jit(solution)/shard_map/all_to_all | solution.py:452
  253.5 7.1 forward_resid.2
  263.2 16.8 %all-gather.20.cloned.1.call-done = bf16[72,64,512]{2,1,0:T(8,128)(2,1)} async-done(((bf16[9,64,512]{2,1,0:T(8,128)(2,1)}), bf16[72,64,512]{2,1,0:T(8,128)(2,1)}) %all-gather.20.cloned.1.call-update) | async-done | bytes 4718608 | tf_op jit(solution)/shard_map/all_gather | solution.py:429
  280.6 11.7 %forward_three.3 = (bf16[1024,512]{1,0:T(8,128)(2,1)}, f32[8,512]{1,0:T(8,128)}, f32[1024,512]{1,0:T(8,128)}, f32[32,2,512]{2,1,0:T(2,128)}) custom-call(f32[1024,512]{1,0:T(8,128)} %get-tuple-element.98.z_ref.zp_ref, f32[32,2,512]{2,1,0:T(2,128)} %copy-done.10, f32[66]{0:T(128)} %pad_maximum_fusion.4.cnt_ref, f32[1,512]{1,0:T(1,128)} %bitcast.164, ...), custom_call_target="tpu_custom_call" | custom-call | tf_op jit(solution)/shard_map/forward_three/pallas_call | solution.py:548
  292.4 15.4 %all_to_all.106.s_ref = f32[32,2,512]{2,1,0:T(2,128)} all-to-all(f32[32,2,512]{2,1,0:T(2,128)} %get-tuple-element.101), channel_id=1, replica_groups=mesh['dp'=4,'fsdp'=8] {'dp','fsdp'}, dimensions={0} | all-to-all | bytes 262144 | tf_op jit(solution)/shard_map/all_to_all | solution.py:452
  307.8 7.1 forward_resid.3
  317.5 8.1 %all-to-all-done.7.s_ref = f32[32,2,512]{2,1,0:T(2,128)S(1)} async-done(((f32[32,2,512]{2,1,0:T(2,128)}), f32[32,2,512]{2,1,0:T(2,128)S(1)}, u32[]{:S(2)}, u32[]{:S(2)}) %all-to-all-start.7) | async-done | bytes 131104 | tf_op jit(solution)/shard_map/all_to_all | solution.py:452
  326.3 9.0 %forward_join.1 = (bf16[1024,1024]{1,0:T(8,128)(2,1)}, f32[8,512]{1,0:T(8,128)}, f32[1024,1024]{1,0:T(8,128)}, f32[32,2,1024]{2,1,0:T(2,128)}) custom-call(f32[1024,512]{1,0:T(8,128)} %get-tuple-element.103.z_ref.zp_ref, f32[32,2,512]{2,1,0:T(2,128)} %copy-done.11, f32[66]{0:T(128)} %pad_maximum_fusion.4.cnt_ref, f32[1,512]{1,0:T(1,128)} %bitcast.152, ...), custom_call_target="tpu_custom_call" | custom-call | tf_op jit(solution)/shard_map/forward_join/pallas_call | solution.py:548
  335.3 13.3 %all_to_all.107.s_ref = f32[32,2,1024]{2,1,0:T(2,128)} all-to-all(f32[32,2,1024]{2,1,0:T(2,128)} %get-tuple-element.107), channel_id=1, replica_groups=mesh['dp'=4,'fsdp'=8] {'dp','fsdp'}, dimensions={0} | all-to-all | bytes 524288 | tf_op jit(solution)/shard_map/all_to_all | solution.py:452
  348.6 9.4 %top.1 = (bf16[1024,1024]{1,0:T(8,128)(2,1)}, f32[8,1024]{1,0:T(8,128)}, f32[1024,1024]{1,0:T(8,128)}, f32[32,2,1024]{2,1,0:T(2,128)}) custom-call(f32[1024,1024]{1,0:T(8,128)} %get-tuple-element.106.z_ref, f32[32,2,1024]{2,1,0:T(2,128)} %all_to_all.107.s_ref, f32[66]{0:T(128)} %pad_maximum_fusion.4.cnt_ref, f32[1,1024]{1,0:T(1,128)} %bitcast.150, ...), custom_call_target="tpu_custom_call" | custom-call | tf_op jit(solution)/shard_map/top/pallas_call | solution.py:578
  358.0 13.7 %all_to_all.108.s_ref = f32[32,2,1024]{2,1,0:T(2,128)} all-to-all(f32[32,2,1024]{2,1,0:T(2,128)} %get-tuple-element.111), channel_id=1, replica_groups=mesh['dp'=4,'fsdp'=8] {'dp','fsdp'}, dimensions={0} | all-to-all | bytes 524288 | tf_op jit(solution)/shard_map/all_to_all | solution.py:452
  371.7 10.7 %backward_part.1 = (bf16[1024,1024]{1,0:T(8,128)(2,1)}, f32[8,1024]{1,0:T(8,128)}, f32[1024,512]{1,0:T(8,128)}, f32[1024,512]{1,0:T(8,128)}, f32[32,2,512]{2,1,0:T(2,128)}) custom-call(f32[1024,1024]{1,0:T(8,128)} %get-tuple-element.109.g_ref, f32[1024,1024]{1,0:T(8,128)} %get-tuple-element.106.z_ref, f32[8,1024]{1,0:T(8,128)} %get-tuple-element.110.mv_ref, ...), custom_call_target="tpu_custom_call" | custom-call | tf_op jit(solution)/shard_map/backward_part/pallas_call | solution.py:633
  382.4 5.3 convolution_convert_fusion.1
  388.7 11.8 %all_to_all.109.s_ref = f32[32,2,512]{2,1,0:T(2,128)} all-to-all(f32[32,2,512]{2,1,0:T(2,128)S(1)} %copy-done.17), channel_id=1, replica_groups=mesh['dp'=4,'fsdp'=8] {'dp','fsdp'}, dimensions={0} | all-to-all | bytes 262144 | tf_op jit(solution)/shard_map/all_to_all | solution.py:452
  400.5 7.9 backward_keep.1
  413.4 7.3 all-to-all-done.11.s_ref
  421.3 12.7 %backward_three.2 = (bf16[1024,512]{1,0:T(8,128)(2,1)}, f32[8,512]{1,0:T(8,128)}, f32[1024,512]{1,0:T(8,128)}, f32[32,2,512]{2,1,0:T(2,128)}) custom-call(f32[1024,512]{1,0:T(8,128)} %get-tuple-element.119.g_ref, f32[1024,512]{1,0:T(8,128)} %get-tuple-element.100.z_ref.zp_ref, f32[8,512]{1,0:T(8,128)} %get-tuple-element.118.mvp_ref.mv_ref, ...), custom_call_target="tpu_custom_call" | custom-call | tf_op jit(solution)/shard_map/backward_three/pallas_call | solution.py:633
  434.0 9.5 %weight_grad_1.2 = bf16[8,9,64,512]{3,2,1,0:T(8,128)(2,1)} custom-call(bf16[1024,512]{1,0:T(8,128)(2,1)} %get-tuple-element.127.x_ref, bf16[9,1024,128]{2,1,0:T(8,128)(2,1)} %broadcast_in_dim.16.rest_0_.m_ref, bf16[1024,512]{1,0:T(8,128)(2,1)} %get-tuple-element.128.dz_ref), custom_call_target="tpu_custom_call" | custom-call | tf_op jit(solution)/shard_map/weight_grad_1/pallas_call | solution.py:649
  444.4 12.0 %all_to_all.110.s_ref = f32[32,2,512]{2,1,0:T(2,128)} all-to-all(f32[32,2,512]{2,1,0:T(2,128)S(1)} %copy-done.18), channel_id=1, replica_groups=mesh['dp'=4,'fsdp'=8] {'dp','fsdp'}, dimensions={0} | all-to-all | bytes 262144 | tf_op jit(solution)/shard_map/all_to_all | solution.py:452
  456.4 8.6 %backward_add.1 = (bf16[1024,512]{1,0:T(8,128)(2,1)}, f32[8,512]{1,0:T(8,128)}, f32[1024,512]{1,0:T(8,128)}, f32[1024,512]{1,0:T(8,128)}, f32[32,2,512]{2,1,0:T(2,128)}) custom-call(f32[1024,512]{1,0:T(8,128)} %get-tuple-element.125.g_ref, f32[1024,512]{1,0:T(8,128)} %get-tuple-element.98.z_ref.zp_ref, f32[8,512]{1,0:T(8,128)} %get-tuple-element.124.mvp_ref.mv_ref, ...), custom_call_target="tpu_custom_call" | custom-call | tf_op jit(solution)/shard_map/backward_add/pallas_call | solution.py:633
  470.0 7.9 %all-to-all-done.13.s_ref = f32[32,2,512]{2,1,0:T(2,128)S(1)} async-done(((f32[32,2,512]{2,1,0:T(2,128)}), f32[32,2,512]{2,1,0:T(2,128)S(1)}, u32[]{:S(2)}, u32[]{:S(2)}) %all-to-all-start.13) | async-done | bytes 131104 | tf_op jit(solution)/shard_map/all_to_all | solution.py:452
  478.6 12.7 %backward_three.3 = (bf16[1024,512]{1,0:T(8,128)(2,1)}, f32[8,512]{1,0:T(8,128)}, f32[1024,512]{1,0:T(8,128)}, f32[32,2,512]{2,1,0:T(2,128)}) custom-call(f32[1024,512]{1,0:T(8,128)} %get-tuple-element.132.g_ref, f32[1024,512]{1,0:T(8,128)} %get-tuple-element.95.z_ref.zp_ref, f32[8,512]{1,0:T(8,128)} %get-tuple-element.130.mvp_ref.mv_ref, ...), custom_call_target="tpu_custom_call" | custom-call | tf_op jit(solution)/shard_map/backward_three/pallas_call | solution.py:633
  491.2 9.6 %weight_grad_1.3 = bf16[8,9,64,512]{3,2,1,0:T(8,128)(2,1)} custom-call(bf16[1024,512]{1,0:T(8,128)(2,1)} %get-tuple-element.140.x_ref, bf16[9,1024,128]{2,1,0:T(8,128)(2,1)} %broadcast_in_dim.16.rest_0_.m_ref, bf16[1024,512]{1,0:T(8,128)(2,1)} %get-tuple-element.141.dz_ref), custom_call_target="tpu_custom_call" | custom-call | tf_op jit(solution)/shard_map/weight_grad_1/pallas_call | solution.py:649
  501.7 10.5 %all_to_all.111.s_ref = f32[32,2,512]{2,1,0:T(2,128)} all-to-all(f32[32,2,512]{2,1,0:T(2,128)S(1)} %copy-done.16), channel_id=1, replica_groups=mesh['dp'=4,'fsdp'=8] {'dp','fsdp'}, dimensions={0} | all-to-all | bytes 262144 | tf_op jit(solution)/shard_map/all_to_all | solution.py:452
  512.3 13.3 %backward_merge.1 = (bf16[1024,512]{1,0:T(8,128)(2,1)}, f32[8,512]{1,0:T(8,128)}, f32[1024,1024]{1,0:T(8,128)}, f32[32,2,1024]{2,1,0:T(2,128)}) custom-call(f32[1024,512]{1,0:T(8,128)} %get-tuple-element.138.g_ref, f32[1024,512]{1,0:T(8,128)} %get-tuple-element.93.z_ref.zp_ref, f32[8,512]{1,0:T(8,128)} %get-tuple-element.137.mvp_ref.mv_ref, ...), custom_call_target="tpu_custom_call" | custom-call | tf_op jit(solution)/shard_map/backward_merge/pallas_call | solution.py:633
  529.4 17.9 %all_to_all.112.s_ref = f32[32,2,1024]{2,1,0:T(2,128)} all-to-all(f32[32,2,1024]{2,1,0:T(2,128)S(1)} %copy-done.13), channel_id=1, replica_groups=mesh['dp'=4,'fsdp'=8] {'dp','fsdp'}, dimensions={0} | all-to-all | bytes 524288 | tf_op jit(solution)/shard_map/all_to_all | solution.py:452
  547.3 12.8 %backward_plain.1 = (bf16[1024,1024]{1,0:T(8,128)(2,1)}, f32[8,1024]{1,0:T(8,128)}, f32[1024,1024]{1,0:T(8,128)}, f32[32,2,1024]{2,1,0:T(2,128)}) custom-call(f32[1024,1024]{1,0:T(8,128)} %get-tuple-element.146.g_ref, f32[1024,1024]{1,0:T(8,128)} %get-tuple-element.91.z_ref.zp_ref, f32[8,1024]{1,0:T(8,128)} %get-tuple-element.143.mvp_ref.mv_ref, ...), custom_call_target="tpu_custom_call" | custom-call | tf_op jit(solution)/shard_map/backward_plain/pallas_call | solution.py:633
  560.1 5.4 convolution_convert_fusion
  566.4 17.3 %all_to_all.113.s_ref = f32[32,2,1024]{2,1,0:T(2,128)} all-to-all(f32[32,2,1024]{2,1,0:T(2,128)S(1)} %copy-done.14), channel_id=1, replica_groups=mesh['dp'=4,'fsdp'=8] {'dp','fsdp'}, dimensions={0} | all-to-all | bytes 524288 | tf_op jit(solution)/shard_map/all_to_all | solution.py:452
  583.7 6.1 down_norm.1
  589.8 17.1 %weight_grad_2.1 = bf16[8,9,64,1024]{3,2,1,0:T(8,128)(2,1)} custom-call(bf16[4,1024,512]{2,1,0:T(8,128)(2,1)} %parity_images.1.ph_ref.x_ref, bf16[9,1024,128]{2,1,0:T(8,128)(2,1)} %broadcast_in_dim.14.m_ref, bf16[1024,1024]{1,0:T(8,128)(2,1)} %get-tuple-element.157.dz_ref), custom_call_target="tpu_custom_call" | custom-call | tf_op jit(solution)/shard_map/weight_grad_2/pallas_call | solution.py:649
  618.8 16.8 %reduce-scatter.17.cloned.1.call-done = bf16[128,1024]{1,0:T(8,128)(2,1)} async-done(((bf16[1024,1024]{1,0:T(8,128)(2,1)}), bf16[128,1024]{1,0:T(8,128)(2,1)}) %reduce-scatter.17.cloned.1.call-update) | async-done | bytes 262160 | tf_op jit(solution)/shard_map/reduce_scatter | solution.py:660
  647.3 14.6 %all-to-all-done.19 = bf16[4,464,512]{2,1,0:T(8,128)(2,1)S(1)} async-done(((bf16[4,464,512]{2,1,0:T(8,128)(2,1)}), bf16[4,464,512]{2,1,0:T(8,128)(2,1)S(1)}, u32[]{:S(2)}, u32[]{:S(2)}) %all-to-all-start.19) | async-done | bytes 1900576 | tf_op jit(solution)/shard_map/all_to_all | solution.py:665
  668.5 21.4 %all-to-all-done.20 = bf16[4,464,512]{2,1,0:T(8,128)(2,1)S(1)} async-done(((bf16[4,464,512]{2,1,0:T(8,128)(2,1)}), bf16[4,464,512]{2,1,0:T(8,128)(2,1)S(1)}, u32[]{:S(2)}, u32[]{:S(2)}) %all-to-all-start.20) | async-done | bytes 1900576 | tf_op jit(solution)/shard_map/all_to_all | solution.py:667
  689.8 46.1 %reduce-scatter.15.cloned.1.call-done = bf16[1,9,64,1024]{3,2,1,0:T(8,128)(2,1)} async-done(((bf16[8,9,64,1024]{3,2,1,0:T(8,128)(2,1)}), bf16[1,9,64,1024]{3,2,1,0:T(8,128)(2,1)}) %reduce-scatter.15.cloned.1.call-update) | async-done | bytes 1179664 | tf_op jit(solution)/shard_map/reduce_scatter | solution.py:660
  742.5 17.8 %input_grad.1 = bf16[4,16,2,32,512]{4,3,2,1,0:T(8,128)(2,1)} custom-call(bf16[1024,1024]{1,0:T(8,128)(2,1)} %get-tuple-element.157.dz_ref, bf16[9,1024,128]{2,1,0:T(8,128)(2,1)} %broadcast_in_dim.17.m_ref, bf16[8,9,64,1024]{3,2,1,0:T(8,128)(2,1)} %bitcast.116), custom_call_target="tpu_custom_call" | custom-call | tf_op jit(solution)/shard_map/input_grad/pallas_call | solution.py:728
  764.3 4.2 all-to-all-start.18
  (248 shorter events, 112.7 us)
Async XLA Ops:
  7.2 4.0 copy-start.2
  7.2 96.3 %all-gather.14.cloned.1.call-start = ((), (), s32[]{:S(2)}) async-start(), calls=%async_computation.33 | async-start | bytes 10616832 | tf_op jit(solution)/shard_map/all_gather | solution.py:429
  7.9 126.7 %all-gather.16.cloned.1.call-start = ((), (), s32[]{:S(2)}) async-start(), calls=%async_computation.34 | async-start | bytes 2359296 | tf_op jit(solution)/shard_map/all_gather | solution.py:432
  8.7 159.3 %all-gather.12.cloned.1.call-start = ((), (), s32[]{:S(2)}) async-start(), calls=%async_computation.27 | async-start | bytes 1769472 | tf_op jit(solution)/shard_map/all_gather | solution.py:434
  9.6 3.4 copy-start.19
  11.1 11.6 %copy-start.24 = (s32[4,2]{0,1:T(2,128)S(1)}, s32[4,2]{0,1:T(2,128)}, u32[]{:S(2)}) copy-start(s32[4,2]{0,1:T(2,128)} %param.16) | copy-start | bytes 100
  11.2 211.8 %all-gather.18.cloned.1.call-start = ((), (), s32[]{:S(2)}) async-start(), calls=%async_computation.35 | async-start | bytes 5308416 | tf_op jit(solution)/shard_map/all_gather | solution.py:429
  12.4 13.0 %copy-start.22 = (f32[5632]{0:T(1024)S(1)}, f32[5632]{0:T(1024)}, u32[]{:S(2)}) copy-start(f32[5632]{0:T(1024)} %param.24) | copy-start | bytes 67588
  12.4 267.6 %all-gather.20.cloned.1.call-start = ((), (), s32[]{:S(2)}) async-start(), calls=%async_computation.36 | async-start | bytes 5308416 | tf_op jit(solution)/shard_map/all_gather | solution.py:429
  14.8 108.1 %all-to-all-start.1 = ((f32[32,1,128]{2,1,0:T(1,128)}), f32[32,1,128]{2,1,0:T(1,128)S(1)}, u32[]{:S(2)}, u32[]{:S(2)}) async-start(f32[32,1,128]{2,1,0:T(1,128)} %broadcast_in_dim.15), calls=%async_computation.1 | async-start | bytes 32768 | tf_op jit(solution)/shard_map/all_to_all | solution.py:445
  22.2 295.4 %all-gather.22.cloned.1.call-start = ((), (), s32[]{:S(2)}) async-start(), calls=%async_computation.37 | async-start | bytes 2359296 | tf_op jit(solution)/shard_map/all_gather | solution.py:433
  106.2 19.7 %copy-start.23 = (f32[5632]{0:T(1024)S(1)}, f32[5632]{0:T(1024)}, u32[]{:S(2)}) copy-start(f32[5632]{0:T(1024)} %param.25) | copy-start | bytes 67588
  122.9 15.9 %all-to-all-start = ((f32[32,2,1024]{2,1,0:T(2,128)}), f32[32,2,1024]{2,1,0:T(2,128)S(1)}, u32[]{:S(2)}, u32[]{:S(2)}) async-start(f32[32,2,1024]{2,1,0:T(2,128)} %get-tuple-element.90), calls=%async_computation | async-start | bytes 524288 | tf_op jit(solution)/shard_map/all_to_all | solution.py:452
  149.6 18.8 %all-to-all-start.2 = ((f32[32,2,1024]{2,1,0:T(2,128)}), f32[32,2,1024]{2,1,0:T(2,128)S(1)}, u32[]{:S(2)}, u32[]{:S(2)}) async-start(f32[32,2,1024]{2,1,0:T(2,128)} %get-tuple-element.92), calls=%async_computation.2 | async-start | bytes 524288 | tf_op jit(solution)/shard_map/all_to_all | solution.py:452
  178.1 44.9 %all-to-all-start.3 = ((f32[32,2,512]{2,1,0:T(2,128)}), f32[32,2,512]{2,1,0:T(2,128)S(1)}, u32[]{:S(2)}, u32[]{:S(2)}) async-start(f32[32,2,512]{2,1,0:T(2,128)} %get-tuple-element.94), calls=%async_computation.3 | async-start | bytes 262144 | tf_op jit(solution)/shard_map/all_to_all | solution.py:452
  223.0 2.7 copy-start.9
  260.6 19.4 %all-to-all-start.5 = ((f32[32,2,512]{2,1,0:T(2,128)}), f32[32,2,512]{2,1,0:T(2,128)S(1)}, u32[]{:S(2)}, u32[]{:S(2)}) async-start(f32[32,2,512]{2,1,0:T(2,128)} %get-tuple-element.99), calls=%async_computation.5 | async-start | bytes 262144 | tf_op jit(solution)/shard_map/all_to_all | solution.py:452
  314.9 10.8 %all-to-all-start.7 = ((f32[32,2,512]{2,1,0:T(2,128)}), f32[32,2,512]{2,1,0:T(2,128)S(1)}, u32[]{:S(2)}, u32[]{:S(2)}) async-start(f32[32,2,512]{2,1,0:T(2,128)} %get-tuple-element.104), calls=%async_computation.7 | async-start | bytes 262144 | tf_op jit(solution)/shard_map/all_to_all | solution.py:452
  317.5 138.9 %reduce-scatter.9.cloned.1.call-start = ((), (), s32[]{:S(2)}) async-start(), calls=%async_computation.28 | async-start | bytes 2359296 | tf_op jit(solution)/shard_map/reduce_scatter | solution.py:660
  371.7 10.7 %copy-start.28 = (bf16[1024,1024]{1,0:T(8,128)(2,1)S(1)}, bf16[1024,1024]{1,0:T(8,128)(2,1)}, u32[]{:S(2)}) copy-start(bf16[1024,1024]{1,0:T(8,128)(2,1)} %get-tuple-element.115) | copy-start | bytes 6291460
  400.5 10.8 %copy-start.30 = (bf16[1024,512]{1,0:T(8,128)(2,1)S(1)}, bf16[1024,512]{1,0:T(8,128)(2,1)}, u32[]{:S(2)}) copy-start(bf16[1024,512]{1,0:T(8,128)(2,1)} %get-tuple-element.121) | copy-start | bytes 3145732
  408.4 12.3 %all-to-all-start.11 = ((f32[32,2,512]{2,1,0:T(2,128)}), f32[32,2,512]{2,1,0:T(2,128)S(1)}, u32[]{:S(2)}, u32[]{:S(2)}) async-start(f32[32,2,512]{2,1,0:T(2,128)} %get-tuple-element.120), calls=%async_computation.11 | async-start | bytes 262144 | tf_op jit(solution)/shard_map/all_to_all | solution.py:452
  411.3 135.9 %reduce-scatter.11.cloned.1.call-start = ((), (), s32[]{:S(2)}) async-start(), calls=%async_computation.29 | async-start | bytes 5308416 | tf_op jit(solution)/shard_map/reduce_scatter | solution.py:660
  456.4 11.6 %copy-start.29 = (bf16[1024,512]{1,0:T(8,128)(2,1)S(1)}, bf16[1024,512]{1,0:T(8,128)(2,1)}, u32[]{:S(2)}) copy-start(bf16[1024,512]{1,0:T(8,128)(2,1)} %get-tuple-element.134) | copy-start | bytes 3145732
  465.0 12.9 %all-to-all-start.13 = ((f32[32,2,512]{2,1,0:T(2,128)}), f32[32,2,512]{2,1,0:T(2,128)S(1)}, u32[]{:S(2)}, u32[]{:S(2)}) async-start(f32[32,2,512]{2,1,0:T(2,128)} %get-tuple-element.133), calls=%async_computation.14 | async-start | bytes 262144 | tf_op jit(solution)/shard_map/all_to_all | solution.py:452
  467.7 116.0 %reduce-scatter.13.cloned.1.call-start = ((), (), s32[]{:S(2)}) async-start(), calls=%async_computation.30 | async-start | bytes 5308416 | tf_op jit(solution)/shard_map/reduce_scatter | solution.py:660
  500.8 0.9 copy-start.16
  500.8 116.9 %reduce-scatter.19.cloned.1.call-start = ((), (), s32[]{:S(2)}) async-start(), calls=%async_computation.38 | async-start | bytes 1769472 | tf_op jit(solution)/shard_map/reduce_scatter | solution.py:660
  512.3 13.3 %copy-start.1 = (bf16[1024,1024]{1,0:T(8,128)(2,1)S(1)}, bf16[1024,1024]{1,0:T(8,128)(2,1)}, u32[]{:S(2)}) copy-start(bf16[1024,1024]{1,0:T(8,128)(2,1)} %get-tuple-element.105.rest_0_) | copy-start | bytes 6291460
  527.7 1.7 copy-start.13
  529.3 106.2 %reduce-scatter.17.cloned.1.call-start = ((), (), s32[]{:S(2)}) async-start(), calls=%async_computation.32 | async-start | bytes 2359296 | tf_op jit(solution)/shard_map/reduce_scatter | solution.py:660
  547.3 12.8 %copy-start.27 = (bf16[1024,1024]{1,0:T(8,128)(2,1)S(1)}, bf16[1024,1024]{1,0:T(8,128)(2,1)}, u32[]{:S(2)}) copy-start(bf16[1024,1024]{1,0:T(8,128)(2,1)} %get-tuple-element.153) | copy-start | bytes 6291460
  565.5 0.9 copy-start.14
  565.5 170.4 %reduce-scatter.15.cloned.1.call-start = ((), (), s32[]{:S(2)}) async-start(), calls=%async_computation.31 | async-start | bytes 10616832 | tf_op jit(solution)/shard_map/reduce_scatter | solution.py:660
  606.9 10.0 %copy-start.20 = (f32[5632]{0:T(1024)S(1)}, f32[5632]{0:T(1024)}, u32[]{:S(2)}) copy-start(f32[5632]{0:T(1024)} %param.27) | copy-start | bytes 67588
  606.9 10.1 %copy-start.21 = (f32[5632]{0:T(1024)S(1)}, f32[5632]{0:T(1024)}, u32[]{:S(2)}) copy-start(f32[5632]{0:T(1024)} %param.26) | copy-start | bytes 67588
  606.9 10.7 %copy-start.12 = (bf16[128,1024]{1,0:T(8,128)(2,1)S(1)}, bf16[128,1024]{1,0:T(8,128)(2,1)}, u32[]{:S(2)}) copy-start(bf16[128,1024]{1,0:T(8,128)(2,1)} %reduce-scatter.9.cloned.1.call-done) | copy-start | bytes 786436
  607.0 29.7 %copy-start.6 = (bf16[1,9,64,512]{3,2,1,0:T(8,128)(2,1)S(1)}, bf16[1,9,64,512]{3,2,1,0:T(8,128)(2,1)}, u32[]{:S(2)}) copy-start(bf16[1,9,64,512]{3,2,1,0:T(8,128)(2,1)} %reduce-scatter.13.cloned.1.call-done) | copy-start | bytes 1769476
  617.0 19.7 %copy-start.5 = (bf16[1,9,64,512]{3,2,1,0:T(8,128)(2,1)S(1)}, bf16[1,9,64,512]{3,2,1,0:T(8,128)(2,1)}, u32[]{:S(2)}) copy-start(bf16[1,9,64,512]{3,2,1,0:T(8,128)(2,1)} %reduce-scatter.11.cloned.1.call-done) | copy-start | bytes 1769476
  636.8 1.3 copy-start
  638.0 23.8 %all-to-all-start.19 = ((bf16[4,464,512]{2,1,0:T(8,128)(2,1)}), bf16[4,464,512]{2,1,0:T(8,128)(2,1)S(1)}, u32[]{:S(2)}, u32[]{:S(2)}) async-start(bf16[4,464,512]{2,1,0:T(8,128)(2,1)} %bitcast.130), calls=%async_computation.24 | async-start | bytes 3801088 | tf_op jit(solution)/shard_map/all_to_all | solution.py:665
  663.8 26.0 %all-to-all-start.20 = ((bf16[4,464,512]{2,1,0:T(8,128)(2,1)}), bf16[4,464,512]{2,1,0:T(8,128)(2,1)S(1)}, u32[]{:S(2)}, u32[]{:S(2)}) async-start(bf16[4,464,512]{2,1,0:T(8,128)(2,1)} %broadcast_in_dim.19), calls=%async_computation.25 | async-start | bytes 3801088 | tf_op jit(solution)/shard_map/all_to_all | solution.py:667
  667.5 72.3 %copy-start.15 = (bf16[9,1024,1]{1,0,2:T(8,128)(2,1)S(1)}, bf16[9,1024,1]{1,0,2:T(8,128)(2,1)}, u32[]{:S(2)}) copy-start(bf16[9,1024,1]{1,0,2:T(8,128)(2,1)} %stack.160) | copy-start | bytes 55300
  735.9 27.0 %all-to-all-start.17 = ((bf16[4,144,1024]{2,1,0:T(8,128)(2,1)}), bf16[4,144,1024]{2,1,0:T(8,128)(2,1)S(1)}, u32[]{:S(2)}, u32[]{:S(2)}) async-start(bf16[4,144,1024]{2,1,0:T(8,128)(2,1)} %bitcast.133), calls=%async_computation.21 | async-start | bytes 2359296 | tf_op jit(solution)/shard_map/all_to_all | solution.py:665
  760.3 2.6 copy-start.25
  760.3 2.6 copy-start.26
  764.3 17.0 %all-to-all-start.18 = ((bf16[4,144,1024]{2,1,0:T(8,128)(2,1)}), bf16[4,144,1024]{2,1,0:T(8,128)(2,1)S(1)}, u32[]{:S(2)}, u32[]{:S(2)}) async-start(bf16[4,144,1024]{2,1,0:T(8,128)(2,1)} %broadcast_in_dim.18), calls=%async_computation.22 | async-start | bytes 2359296 | tf_op jit(solution)/shard_map/all_to_all | solution.py:667
  768.5 2.7 slice-start
  (8 other events, 5.8 us)
Sparse Core Ops, SparseCore 0:
  9.6 93.7 all-gather.13
  105.0 29.5 all-gather.15
  136.9 31.0 all-gather.11
  170.0 52.9 all-gather.17
  224.5 55.4 all-gather.19
  281.4 31.0 all-gather.21
  387.9 36.9 reduce-scatter.8
  443.6 57.6 reduce-scatter.10
  503.6 57.7 reduce-scatter.12
  563.6 35.1 reduce-scatter.18
  601.1 34.3 reduce-scatter.16
  637.7 98.0 reduce-scatter.14
where the time goes:
time: 801 us; the launch traced here: 790 us
  waiting for transfers between devices  280 us (35%)
  Pallas kernels  237 us (30%)
  blocking collectives  128 us (16%)
  local copies, waits for them, and re-layouts  57.1 us (7%)
  starting transfers between devices  42.8 us (5%)
  between operations  17.6 us (2%)
  matrix products  16.7 us (2%)
  other arithmetic  12 us (1%)
    all_to_all x9, blocking collectives, exchange(): return lax.all_to_all(st, ALL, 0, 0, tiled=True)  128 us
    all_gather x3, waiting for transfers between devices, gather(): return lax.all_gather(shard, 'fsdp', axis=0, tiled=False)  126 us
    pallas_call x7, Pallas kernels, backward(): pl.pallas_call(functools.partial(backward_kernel, kind, side), grid=(step...  78.7 us
    pallas_call x7, Pallas kernels, forward(): pl.pallas_call(functools.partial(forward_kernel, kind, side), grid=(steps...  65.7 us
    reduce_scatter x6, waiting for transfers between devices, scatter(): return lax.psum_scatter(grad, 'fsdp', scatter_dimension=0, tiled=True)  62.8 us
    pallas_call x3, Pallas kernels, tap_grad(): pl.pallas_call(functools.partial(weight_grad_kernel, stride, side), out_s...  36.1 us
    all_to_all x7, waiting for transfers between devices, exchange(): return lax.all_to_all(st, ALL, 0, 0, tiled=True)  28.1 us
    all_to_all x2, waiting for transfers between devices, sum_over_groups(): lax.all_to_all(jnp.broadcast_to(part[None], (groups, *part.shape)), 'dp',...  24.6 us
  transfers between devices with their start and end apart: 24, of which 15 were waited for; matrix products, arithmetic and copies ran while one was open for 9% of the time, Pallas kernels for 26%

commit v1 on v0

--- a/solution.py
+++ b/solution.py
@@ -19,33 +19,8 @@
     return pltpu.CompilerParams(vmem_limit_bytes=VMEM_LIMIT)
 
 
-def tile_masks(centres, grid_side):
-    extent = 2 * grid_side
-    coords = jnp.arange(extent, dtype=jnp.int32)
-    lower_half = (coords[None, :] >= centres[:, 0:1]).astype(jnp.int32)
-    right_half = (coords[None, :] >= centres[:, 1:2]).astype(jnp.int32)
-    tiles = 2 * lower_half[:, :, None] + right_half[:, None, :]
-    fine_pad = jnp.pad(tiles, ((0, 0), (1, 1), (1, 1)), constant_values=-1)
-    own_tile = tiles[:, ::2, ::2]
-    coarse_pad = jnp.pad(own_tile, ((0, 0), (1, 1), (1, 1)), constant_values=-1)
-    down_list, back_list, mid_list = [], [], []
-    for a in range(3):
-        for b in range(3):
-            down = (
-                fine_pad[:, a : a + extent : 2, b : b + extent : 2] == own_tile
-            ).astype(F32)
-            down_list.append(down)
-            rows, cols = int(a == 0), int(b == 0)
-            back_list.append(jnp.pad(down, ((0, 0), (0, rows), (0, cols)))[:, rows:, cols:])
-            mid_list.append(
-                (coarse_pad[:, a : a + grid_side, b : b + grid_side] == own_tile).astype(F32)
-            )
-
-    def lanes(parts):
-        flat = jnp.stack(parts).reshape(9, -1, 1)
-        return jnp.broadcast_to(flat, (9, flat.shape[1], 128)).astype(BF16)
-
-    return lanes(down_list), lanes(back_list), lanes(mid_list)
+def cost(products, elements):
+    return pl.CostEstimate(flops=2 * products, transcendentals=0, bytes_accessed=4 * elements)
 
 
 def mish_parts(y):
@@ -103,6 +78,23 @@
 def tap_weight(w_ref, tap):
     w = w_ref[:, tap]
     return w.reshape(w.shape[0] * w.shape[1], w.shape[2])
+
+
+def down_weight(direct_ref, spread_ref, tap):
+    taps = direct_ref.shape[1]
+    if tap < taps:
+        return tap_weight(direct_ref, tap)
+    w = spread_ref[tap - taps]
+    shards, held, half = w.shape
+    own = held // 2
+    sides = [w[:, k : k + own].reshape(shards * own, half) for k in (0, own)]
+    return jnp.concatenate(sides, axis=1)
+
+
+def column_blocks(w_ref, depth):
+    if len(w_ref.shape) == 2:
+        return [w_ref[...]]
+    return [w_ref[k].reshape(depth, w_ref.shape[3]) for k in range(w_ref.shape[0])]
 
 
 def dot_nn(a, b):
@@ -212,7 +204,7 @@
         st_ref[...] = jnp.broadcast_to(acc_ref[0:2][None], st_ref.shape)
 
 
-def prep_kernel(x_ref, ph_ref):
+def prep_kernel(side, centre_ref, x_ref, ph_ref, down_ref, back_ref, mid_ref):
     half = ph_ref.shape[1]
     p = lax.broadcasted_iota(jnp.int32, (half, 2 * half), 0)
     s = lax.broadcasted_iota(jnp.int32, (half, 2 * half), 1)
@@ -223,11 +215,38 @@
             pick = jnp.where(s == 2 * p + pc, 1.0, 0.0).astype(BF16)
             ph_ref[2 * pr + pc] = dot_nn(pick, x).astype(BF16)
 
-
-def first_kernel(side, ph_ref, m_ref, valid_ref, w_ref, z_ref, st_ref, acc_ref, num_ref):
+    image = pl.program_id(0)
+    pixel = lax.broadcasted_iota(jnp.int32, (half, 128), 0)
+    spots = (pixel // side, pixel % side)
+    centre = (centre_ref[image, 0], centre_ref[image, 1])
+
+    def inside(own, other, middle, extent):
+        same = (other >= middle) == (own >= middle)
+        return jnp.where(same & (other >= 0) & (other < extent), 1.0, 0.0)
+
+    down, back, mid = [], [], []
+    for axis in range(2):
+        at, middle = spots[axis], centre[axis]
+        down.append([inside(2 * at, 2 * at + a - 1, middle, 2 * side) for a in range(3)])
+        mid.append([inside(2 * at, 2 * (at + a - 1), middle, 2 * side) for a in range(3)])
+        moved = []
+        for a in range(3):
+            to = at + int(a == 0)
+            hit = inside(2 * to, 2 * to + a - 1, middle, 2 * side)
+            moved.append(jnp.where(to < side, hit, 0.0))
+        back.append(moved)
+    for ref, parts in ((down_ref, down), (back_ref, back), (mid_ref, mid)):
+        for tap in range(9):
+            a, b = divmod(tap, 3)
+            ref[tap] = (parts[0][a] * parts[1][b]).astype(BF16)
+
+
+def first_kernel(
+    side, ph_ref, m_ref, valid_ref, wa_ref, wb_ref, z_ref, st_ref, acc_ref, num_ref
+):
     out = None
     for tap, x in down_taps(lambda k: ph_ref[k], side):
-        part = dot_nn(masked(x, m_ref[tap]), tap_weight(w_ref, tap))
+        part = dot_nn(masked(x, m_ref[tap]), down_weight(wa_ref, wb_ref, tap))
         out = part if out is None else out + part
     z_ref[...] = out
     collect_moments(out, valid_ref[...], acc_ref, num_ref, st_ref)
@@ -270,7 +289,8 @@
             part = dot_nn(masked(x, m_ref[tap]), tap_weight(w_ref, tap))
             out = part if out is None else out + part
     else:
-        out = dot_nn(v, w_ref[...])
+        outs = [dot_nn(v, w) for w in column_blocks(w_ref, v.shape[1])]
+        out = outs[0] if len(outs) == 1 else jnp.concatenate(outs, axis=1)
     out_ref[...] = out
     collect_moments(out, valid_ref[...], acc_ref, num_ref, st_ref)
 
@@ -310,6 +330,7 @@
 def backward_kernel(
     kind,
     side,
+    depth,
     g_ref,
     z_ref,
     mv_ref,
@@ -339,7 +360,11 @@
             part = dot_nt(masked(x, m_ref[tap]), tap_weight(w_ref, 8 - tap))
             ga = part if ga is None else ga + part
     else:
-        ga = dot_nt(dz, w_ref[...])
+        ga, at = None, 0
+        for w in column_blocks(w_ref, depth):
+            part = dot_nt(dz[:, at : at + w.shape[1]], w)
+            ga = part if ga is None else ga + part
+            at += w.shape[1]
     if kind == "part":
         half = ga.shape[1] // 2
         keep_ref[...] = ga[:, :half]
@@ -363,7 +388,7 @@
     dz_ref[...] = norm_grad(g_ref, z_ref, mv_ref, s_ref, gain_ref, valid_ref, cnt_ref, tot_ref)
 
 
-def input_grad_kernel(side, dz_ref, m_ref, w_ref, o_ref):
+def input_grad_kernel(side, dz_ref, m_ref, wa_ref, wb_ref, o_ref):
     dz = dz_ref[...]
     rows = dz.shape[0]
     moved = {}
@@ -383,19 +408,28 @@
             for a, di in choices[pr]:
                 for b, dj in choices[pc]:
                     tap = 3 * a + b
-                    part = dot_nt(masked(moved[di, dj], m_ref[tap]), tap_weight(w_ref, tap))
+                    w = down_weight(wa_ref, wb_ref, tap)
+                    part = dot_nt(masked(moved[di, dj], m_ref[tap]), w)
                     total = part if total is None else total + part
             both.append(total.astype(BF16))
         out = dot_nn(put, jnp.concatenate(both, axis=0)).astype(BF16)
         o_ref[0, :, pr] = out.reshape(side, 2 * side, out.shape[1])
 
 
-def weight_grad_kernel(stride, side, x_ref, m_ref, dz_ref, o_ref):
+def weight_grad_kernel(stride, side, first, x_ref, m_ref, dz_ref, o_ref):
     dz = dz_ref[...]
+    by_shard = len(o_ref.shape) == 4
+    count = o_ref.shape[1] if by_shard else o_ref.shape[0]
     taps = mid_taps(x_ref[...], side) if stride == 1 else down_taps(lambda k: x_ref[k], side)
     for tap, x in taps:
+        if not first <= tap < first + count:
+            continue
         grad = dot_tn(masked(x, m_ref[tap]), dz).astype(BF16)
-        o_ref[:, tap] = grad.reshape(o_ref.shape[0], o_ref.shape[2], o_ref.shape[3])
+        if by_shard:
+            grad = grad.reshape(o_ref.shape[0], o_ref.shape[2], o_ref.shape[3])
+            o_ref[:, tap - first] = grad
+        else:
+            o_ref[tap - first] = grad
 
 
 def per_device(
@@ -428,18 +462,49 @@
     def gather(shard):
         return lax.all_gather(shard, "fsdp", axis=0, tiled=False)
 
-    full_down = gather(w_down.transpose(1, 0, 2))
-    full_split = lax.all_gather(w_split[:, 0], "fsdp", axis=0, tiled=True)
+    groups = lax.axis_size("dp")
+    taps = 9 - groups
+    down = w_down.transpose(1, 0, 2)
+    halves = [down[taps:, :, k : k + half] for k in range(0, width, half)]
+    units = [w_split[:, 0, k : k + half] for k in range(0, width, half)]
+    units += [w_reduce[b, :, 0] for b in range(blocks)] + [w_trans[:, 0]]
+    units.append(jnp.zeros_like(w_trans[:, 0]))
+    early = jnp.concatenate(units, axis=0).reshape(groups, -1, half)
+    quarters = jnp.concatenate([*halves, early], axis=1)
+    own_quarter = lax.dynamic_index_in_dim(quarters, lax.axis_index("dp"), 0, keepdims=False)
+    quarter = gather(own_quarter)
+    full_down = gather(lax.optimization_barrier((down[:taps], own_quarter))[0])
+    tap_rows = 2 * down.shape[1]
+    narrow_rows = w_trans.shape[0]
+    split_rows = 2 * w_split.shape[0]
+
+    group = lax.axis_index("dp")
+
+    def to_group(x, k):
+        return lax.ppermute(x, "dp", [(i, i ^ k) for i in range(groups)])
+
+    def send_to_groups(piece):
+        return [to_group(piece, k) for k in range(1, groups)]
+
+    def in_order(piece, received):
+        held = jnp.zeros((groups, *piece.shape), piece.dtype)
+        for k, got in enumerate([piece, *received]):
+            held = lax.dynamic_update_index_in_dim(held, got, group ^ k, 0)
+        return held
+
+    def deal(parts):
+        held = [lax.dynamic_index_in_dim(parts, group ^ k, 0, False) for k in range(groups)]
+        return held, [to_group(held[k], k) for k in range(1, groups)]
+
+    def add_parts(own, received):
+        total = own.astype(F32)
+        for got in received:
+            total = total + got.astype(F32)
+        return total.astype(BF16)
+
+    full_spread = [gather(w_spread[b].transpose(1, 0, 2)) for b in range(blocks)]
     full_unite = lax.all_gather(w_unite[:, 0], "fsdp", axis=0, tiled=True)
-    narrow = lax.all_gather(
-        jnp.concatenate([w_reduce[b, :, 0] for b in range(blocks)] + [w_trans[:, 0]], axis=1),
-        "fsdp",
-        axis=0,
-        tiled=True,
-    )
-    full_spread = [gather(w_spread[b].transpose(1, 0, 2)) for b in range(blocks)]
-
-    mask_down, mask_back, mask_mid = tile_masks(tile_centres, side)
+
     valid = valid_mask.astype(F32).reshape(pixels, 1)
     own_count = jnp.broadcast_to(jnp.sum(valid), (devices, 1, 128))
     counts = lax.all_to_all(own_count, ALL, 0, 0, tiled=True)[:, 0, 0]
@@ -478,25 +543,43 @@
     biases = [bn_bias[s : s + c].reshape(1, c) for s, c in zip(starts, widths)]
     layers = len(widths)
 
+    def narrow_spec(k):
+        return single((1, fsdp, narrow_rows, half), (2 + k // 2, 0, k % 2, 0))
+
     weights = [None] * layers
     weights[0] = (full_down, single(full_down.shape))
-    weights[1] = (full_split, single(full_split.shape))
     for b in range(blocks):
-        weights[2 + 2 * b] = (narrow, single((half, half), (0, b)))
         weights[3 + 2 * b] = (full_spread[b], single(full_spread[b].shape))
-    weights[layers - 2] = (narrow, single((half, half), (0, blocks)))
     weights[layers - 1] = (full_unite, single(full_unite.shape))
 
     x6 = segment_input.reshape(images, side, 2, 2 * side, c_prev)
-    phases = pl.pallas_call(
-        prep_kernel,
+    mask_shape = shaped((9, pixels, 128), BF16)
+    mask_block = pl.BlockSpec((9, per_image, 128), lambda i: (0, i, 0))
+    phases, mask_down, mask_back, mask_mid = pl.pallas_call(
+        functools.partial(prep_kernel, side),
         grid=(images,),
-        in_specs=[pl.BlockSpec((1, side, 2, 2 * side, c_prev), lambda i: (i, 0, 0, 0, 0))],
-        out_specs=pl.BlockSpec((4, per_image, c_prev), lambda i: (0, i, 0)),
-        out_shape=shaped((4, pixels, c_prev), BF16),
+        in_specs=[
+            pl.BlockSpec(memory_space=pltpu.SMEM),
+            pl.BlockSpec((1, side, 2, 2 * side, c_prev), lambda i: (i, 0, 0, 0, 0)),
+        ],
+        out_specs=[
+            pl.BlockSpec((4, per_image, c_prev), lambda i: (0, i, 0)),
+            mask_block,
+            mask_block,
+            mask_block,
+        ],
+        out_shape=[shaped((4, pixels, c_prev), BF16), mask_shape, mask_shape, mask_shape],
         compiler_params=params(),
+        cost_estimate=cost(0, 5 * pixels * c_prev),
         name="parity_images",
-    )(x6)
+    )(tile_centres, x6)
+    quarter, phases, mask_down, mask_back, mask_mid, cnt = lax.optimization_barrier(
+        (quarter, phases, mask_down, mask_back, mask_mid, cnt)
+    )
+    piece = quarter[:, :tap_rows]
+    down_rest = in_order(piece, send_to_groups(piece))
+    early_piece = lax.optimization_barrier((quarter[:, tap_rows:], down_rest))[0]
+    early_got = send_to_groups(early_piece)
 
     def scratch(channels):
         return [pltpu.VMEM((8, channels), F32), pltpu.VMEM((8, 128), F32)]
@@ -510,21 +593,30 @@
             mask_spec,
             valid_spec,
             weights[0][1],
+            single(down_rest.shape),
         ],
         out_specs=[tall(width), fixed((devices, 2, width))],
         out_shape=[shaped((pixels, width), F32), stat_shape(width)],
         scratch_shapes=scratch(width),
         compiler_params=params(),
+        cost_estimate=cost(9 * pixels * c_prev * width, 6 * pixels * width),
         name="down_forward",
-    )(phases, mask_down, valid, full_down)
+    )(phases, mask_down, valid, full_down, down_rest)
+
+    *early_got, first_gathered = lax.optimization_barrier((*early_got, exchange(st[0])))
+    early = in_order(early_piece, early_got)
+    weights[1] = (early, single((2, *early.shape[1:]), (0, 0, 0, 0)))
+    for k, layer in enumerate([2 + 2 * b for b in range(blocks)] + [layers - 2]):
+        weights[layer] = (early, narrow_spec(k))
 
     inputs = [None] * layers
     moment = [None] * layers
 
-    def forward(layer, kind, extra=(), extra_specs=()):
+    def forward(layer, kind, extra=(), extra_specs=(), gathered=None):
         prev, channels = layer - 1, widths[layer - 1]
         w, w_spec = weights[layer]
-        gathered = exchange(st[prev])
+        if gathered is None:
+            gathered = exchange(st[prev])
         args = [z[prev], gathered, cnt, gains[prev], biases[prev], valid, w, *extra]
         specs = [
             tall(channels),
@@ -553,6 +645,7 @@
                 out_shape=out_shape,
                 scratch_shapes=scratch(n),
                 compiler_params=params(),
+                cost_estimate=cost(9 * pixels * half * half * int(kind == "three"), 8 * pixels * half + 4 * pixels * channels),
                 name="forward_" + kind,
             )(*args)
         )
@@ -561,7 +654,7 @@
         moment[prev], z[layer], st[layer] = outs
         return keep
 
-    forward(1, "plain")
+    forward(1, "plain", gathered=first_gathered)
     stream = None
     for b in range(blocks):
         if b == 0:
@@ -595,6 +688,7 @@
         ],
         scratch_shapes=[pltpu.VMEM((8, n), F32)],
         compiler_params=params(),
+        cost_estimate=cost(0, 8 * pixels * n),
         name="top",
     )(z[last], exchange(st[last]), cnt, gains[last], biases[last], cotangent.reshape(pixels, n))
 
@@ -605,6 +699,7 @@
         prev, channels = layer - 1, widths[layer]
         cp = widths[prev]
         w, w_spec = weights[layer]
+        depth = 2 * half if kind == "part" else (half if kind == "merge" else cp)
         args = [g, z[layer], moment[layer], gathered, gains[layer], valid, cnt, w]
         args += [z[prev], moment[prev], gains[prev], biases[prev], *extra]
         specs = [
@@ -631,13 +726,14 @@
         out_shape += [shaped((pixels, cp), F32), stat_shape(cp)]
         outs = list(
             pl.pallas_call(
-                functools.partial(backward_kernel, kind, side),
+                functools.partial(backward_kernel, kind, side, depth),
                 grid=(steps,),
                 in_specs=specs,
                 out_specs=out_specs,
                 out_shape=out_shape,
                 scratch_shapes=[pltpu.VMEM((8, cp), F32)],
                 compiler_params=params(),
+                cost_estimate=cost(9 * pixels * half * half * int(kind == "three"), 8 * pixels * half + 4 * pixels * cp),
                 name="backward_" + kind,
             )(*args)
         )
@@ -645,11 +741,12 @@
         keep = outs.pop(0) if kind in ("part", "keep", "add") else None
         return outs[0], outs[1], keep
 
-    def tap_grad(stride, x, lane_mask, dz_low, w_shape):
+    def tap_grad(stride, x, lane_mask, dz_low, w_shape, first=0):
         return pl.pallas_call(
-            functools.partial(weight_grad_kernel, stride, side),
+            functools.partial(weight_grad_kernel, stride, side, first),
             out_shape=shaped(w_shape, BF16),
             compiler_params=params(),
+            cost_estimate=cost(9 * pixels * half * dz_low.shape[1], 2 * pixels * dz_low.shape[1]),
             name="weight_grad_" + str(stride),
         )(x, lane_mask, dz_low)
 
@@ -659,33 +756,33 @@
     def scatter(grad):
         return lax.psum_scatter(grad, "fsdp", scatter_dimension=0, tiled=True)
 
-    def sum_over_groups(own):
-        groups = lax.axis_size("dp")
+    def sum_own_part(own):
         parts = own.reshape(groups, own.shape[0] // groups, own.shape[1])
         parts = lax.all_to_all(parts, "dp", 0, 0, tiled=True)
-        part = jnp.sum(parts.astype(F32), axis=0).astype(BF16)
-        back = lax.all_to_all(
-            jnp.broadcast_to(part[None], (groups, *part.shape)), "dp", 0, 0, tiled=True
-        )
-        return back.reshape(own.shape).astype(F32)
+        return jnp.sum(parts.astype(F32), axis=0).astype(BF16)
+
+    def give_back(part):
+        sent = jnp.broadcast_to(part[None], (groups, *part.shape))
+        return lax.all_to_all(sent, "dp", 0, 0, tiled=True).astype(F32)
 
     def beside(st_back, grad, *due):
-        return lax.optimization_barrier((exchange(st_back), grad, *due))[0]
+        return lax.optimization_barrier((exchange(st_back), grad, *due))[:2]
 
     g, st_back, grad_route = backward(last, "part", g, exchange(st_back))
     grad_unite = flat_grad(inputs[last], dz[last])
+    gathered, grad_unite = beside(st_back, grad_unite)
     own_unite = scatter(grad_unite)
-    g, st_back, grad_stream = backward(last - 1, "keep", g, beside(st_back, grad_unite))
+    g, st_back, grad_stream = backward(last - 1, "keep", g, gathered)
     narrow_grads = [None] * (blocks + 1)
     narrow_grads[blocks] = flat_grad(inputs[last - 1], dz[last - 1])
-    gathered = beside(st_back, narrow_grads[blocks])
+    gathered, narrow_grads[blocks] = beside(st_back, narrow_grads[blocks])
     own_spread = [None] * blocks
     for b in reversed(range(blocks)):
         layer = 3 + 2 * b
         g, st_back, _ = backward(layer, "three", g, gathered, (mask_mid,), (mask_spec,))
         own = tap_grad(1, inputs[layer], mask_mid, dz[layer], full_spread[b].shape)
         due = (own_unite,) if b == blocks - 1 else ()
-        gathered = beside(st_back, own, *due)
+        gathered, own = beside(st_back, own, *due)
         own_spread[b] = scatter(own)
         layer = 2 + 2 * b
         if b > 0:
@@ -700,11 +797,12 @@
             low = inputs[layer][:, half:]
         narrow_grads[b] = flat_grad(low, dz[layer])
         due = own_spread[1:2] if b == 0 else ()
-        gathered = beside(st_back, narrow_grads[b], *due)
-    own_narrow = scatter(jnp.concatenate(narrow_grads, axis=1))
+        gathered, narrow_grads[b] = beside(st_back, narrow_grads[b], *due)
     g, st_back, _ = backward(1, "plain", g, gathered)
-    grad_split = flat_grad(inputs[1], dz[1])
-    own_split = scatter(grad_split)
+    split_grads = [flat_grad(inputs[1], dz[1][:, k : k + half]) for k in range(0, width, half)]
+    late = [w.reshape(fsdp, -1, half) for w in (*split_grads, *narrow_grads)]
+    gathered, grad_late = beside(st_back, jnp.concatenate(late, axis=1))
+    own_late = scatter(grad_late)[0]
     dz[0], totals[0] = pl.pallas_call(
         last_norm_kernel,
         grid=(steps,),
@@ -720,11 +818,19 @@
         out_specs=[tall(width), fixed((8, width))],
         out_shape=[shaped((pixels, width), BF16), shaped((8, width), F32)],
         compiler_params=params(),
+        cost_estimate=cost(0, 5 * pixels * width),
         name="down_norm",
-    )(g, z[0], moment[0], beside(st_back, grad_split, own_spread[0]), gains[0], valid, cnt)
-    grad_down = tap_grad(2, phases, mask_down, dz[0], full_down.shape)
-    own_down = scatter(grad_down)
-    dz_low, _ = lax.optimization_barrier((dz[0], grad_down))
+    )(g, z[0], moment[0], gathered, gains[0], valid, cnt)
+    direct = tap_grad(2, phases, mask_down, dz[0], full_down.shape)
+    own_direct = scatter(direct)
+    dz_low = lax.optimization_barrier((dz[0], direct, own_spread[0]))[0]
+    rest = tap_grad(2, phases, mask_down, dz_low, (groups, c_prev, width), taps)
+    first_packed = lax.optimization_barrier((*own_spread, own_unite, direct))[:-1]
+    first_packed = [o.reshape(-1, half) for o in first_packed]
+    first_part = sum_own_part(jnp.concatenate(first_packed, axis=0))
+    first_part, rest = lax.optimization_barrier((first_part, rest))
+    rest_held, rest_got = deal(rest)
+    *rest_held, dz_low = lax.optimization_barrier((*rest_held, dz_low))
     input_grad = pl.pallas_call(
         functools.partial(input_grad_kernel, side),
         grid=(images,),
@@ -732,24 +838,43 @@
             pl.BlockSpec((per_image, width), lambda i: (i, 0)),
             pl.BlockSpec((9, per_image, 128), lambda i: (0, i, 0)),
             weights[0][1],
+            single(down_rest.shape),
         ],
         out_specs=pl.BlockSpec((1, side, 2, 2 * side, c_prev), lambda i: (i, 0, 0, 0, 0)),
         out_shape=shaped(x6.shape, BF16),
         compiler_params=params(),
+        cost_estimate=cost(9 * pixels * c_prev * width, 8 * pixels * width),
         name="input_grad",
-    )(dz_low, mask_back, full_down).reshape(segment_input.shape)
-
-    packed = [own_unite, own_split, own_narrow, *own_spread]
-    flat = [o.reshape(-1, half) for o in packed]
-    sums = sum_over_groups(jnp.concatenate(flat, axis=0))
-    ends = [0]
-    for f in flat:
-        ends.append(ends[-1] + f.shape[0])
-    pieces = [sums[a:e].reshape(o.shape) for a, e, o in zip(ends, ends[1:], packed)]
-    grad_unite, grad_split, narrow_grad = pieces[:3]
-    spread_grads = [piece[0].transpose(1, 0, 2) for piece in pieces[3:]]
-    grad_down = sum_over_groups(own_down.reshape(-1, width)).reshape(own_down.shape)
-    grad_down = grad_down[0].transpose(1, 0, 2)
+    )(dz_low, mask_back, full_down, down_rest).reshape(segment_input.shape)
+
+    *received, input_grad = lax.optimization_barrier((*rest_got, input_grad))
+    rest_sum = add_parts(rest_held[0], received)
+    own_rest = scatter(rest_sum)
+    *totals, rest_sum = lax.optimization_barrier((*totals, rest_sum))
+    *moment, rest_sum = lax.optimization_barrier((*moment, rest_sum))
+    first_part = lax.optimization_barrier((first_part, rest_sum))[0]
+    first_sums = give_back(first_part).reshape(-1, half)
+    own_late, own_direct, first_sums = lax.optimization_barrier((own_late, own_direct, first_sums))
+    second = [own_late, own_direct.reshape(-1, width)]
+    cut = [o.reshape(groups, -1, o.shape[-1]) for o in second]
+    cut[1] = cut[1].reshape(groups, -1, half)
+    second_part = sum_own_part(jnp.concatenate(cut, axis=1).reshape(-1, half))
+    late_rows = own_late.shape[0]
+    late_own = late_rows // groups
+    sums = give_back(second_part)
+    grad_direct = sums[:, late_own:].reshape(own_direct.shape[1:])
+    late_sums = sums[:, :late_own].reshape(-1, half)
+    spread_rows = first_packed[0].shape[0]
+    split_parts = late_sums[:split_rows].reshape(-1, split_rows // 2, half)
+    grad_split = jnp.concatenate([split_parts[0], split_parts[1]], axis=1)
+    narrow = late_sums[split_rows:].reshape(blocks + 1, narrow_rows, 1, half)
+    grad_spread = first_sums[: blocks * spread_rows]
+    grad_spread = grad_spread.reshape(blocks, 9, narrow_rows, half).transpose(0, 2, 1, 3)
+    grad_unite = first_sums[blocks * spread_rows :].reshape(own_unite.shape)[:, None]
+    grad_split, narrow, grad_spread, grad_unite, grad_direct, own_rest = lax.optimization_barrier(
+        (grad_split, narrow, grad_spread, grad_unite, grad_direct, own_rest)
+    )
+    grad_down = jnp.concatenate([grad_direct, give_back(own_rest)], axis=0).transpose(1, 0, 2)
 
     means = jnp.concatenate([m[0] for m in moment])
     variances = jnp.concatenate([m[1] for m in moment])
@@ -757,16 +882,15 @@
     new_var = (1.0 - momentum_rate) * running_var + momentum_rate * variances * whole_count / (
         whole_count - 1.0
     )
-    grad_reduce = jnp.stack([narrow_grad[:, None, half * b : half * (b + 1)] for b in range(blocks)])
     return (
         output.reshape(cotangent.shape),
         input_grad,
         grad_down,
         grad_split[:, None],
-        grad_reduce,
-        jnp.stack(spread_grads),
-        narrow_grad[:, None, half * blocks :],
-        grad_unite[:, None],
+        narrow[:blocks],
+        grad_spread,
+        narrow[blocks],
+        grad_unite,
         jnp.concatenate([t[1] for t in totals]),
         jnp.concatenate([t[0] for t in totals]),
         new_mean,

time: 801 us -> 724 us (0.904)
  waiting for transfers between devices: 280 us -> 183 us
  blocking collectives: 128 us -> 72.3 us
  starting transfers between devices: 42.8 us -> 76.4 us
  local copies, waits for them, and re-layouts: 57.1 us -> 84.2 us
    all_gather x3 -> x4, waiting for transfers between devices: 126 us -> 7.84 us  [gather(): return lax.all_gather(shard, 'fsdp', axis=0, tiled=False)]
    ppermute x0 -> x9, waiting for transfers between devices: none -> 91.4 us  [to_group(): return lax.ppermute(x, 'dp', [(i, i ^ k) for i in range(groups)])]
    reduce_scatter x6, waiting for transfers between devices: 62.8 us -> 0.08 us  [scatter(): return lax.psum_scatter(grad, 'fsdp', scatter_dimension=0, tiled=True)]
    all_to_all x9 -> x5, blocking collectives: 128 us -> 72.3 us  [exchange(): return lax.all_to_all(st, ALL, 0, 0, tiled=True)]
    all_to_all x7 -> x11, waiting for transfers between devices: 28.1 us -> 65 us  [exchange(): return lax.all_to_all(st, ALL, 0, 0, tiled=True)]
    all_to_all x4 -> x5, waiting for transfers between devices: 39.2 us -> 17.7 us  [the longest x2 11 us: sum_own_part(): parts = lax.all_to_all(parts, 'dp', 0, 0, tiled=True)]
    all_gather x2 -> x0, waiting for transfers between devices: 21.1 us -> none  [the longest x1 15.7 us: per_device(): lax.all_gather(jnp.concatenate([w_reduce[b, :, 0] for b in range(blocks)]...]
    all_to_all x7 -> x11, starting transfers between devices: 19.6 us -> 37.1 us  [exchange(): return lax.all_to_all(st, ALL, 0, 0, tiled=True)]
  transfers between devices with their start and end apart: 24 -> 37, of which waited for: 15 -> 20; matrix products, arithmetic and copies ran while one was open for 9% -> 14% of each run, Pallas kernels for 26% -> 30%
where the time goes in v1:
time: 724 us; the launch traced here: 710 us
  Pallas kernels  243 us (34%)
  waiting for transfers between devices  183 us (25%)
  local copies, waits for them, and re-layouts  84.2 us (12%)
  starting transfers between devices  76.4 us (11%)
  blocking collectives  72.3 us (10%)
  other arithmetic  18.1 us (3%)
  between operations  17.3 us (2%)
  matrix products  15.8 us (2%)
    ppermute x9, waiting for transfers between devices, to_group(): return lax.ppermute(x, 'dp', [(i, i ^ k) for i in range(groups)])  91.4 us
    pallas_call x7, Pallas kernels, backward(): pl.pallas_call(functools.partial(backward_kernel, kind, side, depth), gri...  77.7 us
    all_to_all x5, blocking collectives, exchange(): return lax.all_to_all(st, ALL, 0, 0, tiled=True)  72.3 us
    pallas_call x7, Pallas kernels, forward(): pl.pallas_call(functools.partial(forward_kernel, kind, side), grid=(steps...  65.5 us
    all_to_all x11, waiting for transfers between devices, exchange(): return lax.all_to_all(st, ALL, 0, 0, tiled=True)  65 us
    pallas_call x4, Pallas kernels, tap_grad(): pl.pallas_call(functools.partial(weight_grad_kernel, stride, side, first)...  40.5 us
    all_to_all x11, starting transfers between devices, exchange(): return lax.all_to_all(st, ALL, 0, 0, tiled=True)  37.1 us
    unnamed x108, local copies, waits for them, and re-layouts  25.2 us
  transfers between devices with their start and end apart: 37, of which 20 were waited for; matrix products, arithmetic and copies ran while one was open for 14% of the time, Pallas kernels for 30%

profile of v1, /device:TPU:0, one launch (start us, length us, event | category | flops | bytes accessed | tf_op | source)
XLA Modules:
  0.0 710.0 jit_solution(4804596317626413664)
XLA Ops:
  18.4 7.3 %all-to-all-start = ((f32[32,1,128]{2,1,0:T(1,128)}), f32[32,1,128]{2,1,0:T(1,128)S(1)}, u32[]{:S(2)}, u32[]{:S(2)}) async-start(f32[32,1,128]{2,1,0:T(1,128)} %broadcast_in_dim.53), calls=%async_computation | async-start | bytes 32768 | tf_op jit(solution)/shard_map/all_to_all | solution.py:510
  26.4 9.2 %parity_images.1 = (bf16[4,1024,512]{2,1,0:T(8,128)(2,1)}, bf16[9,1024,128]{2,1,0:T(8,128)(2,1)}, bf16[9,1024,128]{2,1,0:T(8,128)(2,1)}, bf16[9,1024,128]{2,1,0:T(8,128)(2,1)}) custom-call(s32[4,2]{1,0:T(4,128)} %copy.61.centre_ref, bf16[4,16,2,32,512]{4,3,2,1,0:T(8,128)(2,1)} %bitcast.136), custom_call_target="tpu_custom_call" | custom-call | bytes 10485760 | tf_op jit(solution)/shard_map/parity_images/pallas_call | solution.py:558
  38.3 7.8 %all-gather.10.cloned.1.call-done = bf16[8,256,512]{2,1,0:T(8,128)(2,1)} async-done(((bf16[1,256,512]{2,1,0:T(8,128)(2,1)}), bf16[8,256,512]{2,1,0:T(8,128)(2,1)}) %all-gather.10.cloned.1.call-update) | async-done | bytes 2097168 | tf_op jit(solution)/shard_map/all_gather | solution.py:463
  57.2 18.0 %collective-permute-done = bf16[8,128,512]{2,1,0:T(8,128)(2,1)} collective-permute-done((bf16[8,128,512]{2,1,0:T(8,128)(2,1)}, bf16[8,128,512]{2,1,0:T(8,128)(2,1)}, u32[]{:S(2)}, u32[]{:S(2)}) %collective-permute-start) | collective-permute-done | bytes 1048608 | tf_op jit(solution)/shard_map/ppermute | solution.py:484
  77.5 20.5 %collective-permute-done.1 = bf16[8,128,512]{2,1,0:T(8,128)(2,1)S(1)} collective-permute-done((bf16[8,128,512]{2,1,0:T(8,128)(2,1)}, bf16[8,128,512]{2,1,0:T(8,128)(2,1)S(1)}, u32[]{:S(2)}, u32[]{:S(2)}) %collective-permute-start.1) | collective-permute-done | bytes 1048608 | tf_op jit(solution)/shard_map/ppermute | solution.py:484
  103.7 16.8 %down_forward.1 = (f32[1024,1024]{1,0:T(8,128)}, f32[32,2,1024]{2,1,0:T(2,128)}) custom-call(bf16[4,1024,512]{2,1,0:T(8,128)(2,1)} %get-tuple-element.151.ph_ref.x_ref, bf16[9,1024,128]{2,1,0:T(8,128)(2,1)} %get-tuple-element.152.m_ref, f32[1024,1]{1,0:T(8,128)} %reshape.190.valid_ref, bf16[8,5,64,1024]{3,2,1,0:T(8,128)(2,1)} %bitcast.222, ...), custom_call_target="tpu_custom_call" | custom-call | flops 9663676416 | bytes 25165824 | tf_op jit(solution)/shard_map/down_forward/pallas_call | solution.py:588
  128.2 20.4 %collective-permute-done.4 = bf16[8,128,512]{2,1,0:T(8,128)(2,1)S(1)} collective-permute-done((bf16[8,128,512]{2,1,0:T(8,128)(2,1)S(1)}, bf16[8,128,512]{2,1,0:T(8,128)(2,1)S(1)}, u32[]{:S(2)}, u32[]{:S(2)}) %collective-permute-start.4) | collective-permute-done | bytes 1048608 | tf_op jit(solution)/shard_map/ppermute | solution.py:484
  155.4 9.8 %forward_plain.1 = (bf16[1024,1024]{1,0:T(8,128)(2,1)}, f32[8,1024]{1,0:T(8,128)}, f32[1024,1024]{1,0:T(8,128)}, f32[32,2,1024]{2,1,0:T(2,128)}) custom-call(f32[1024,1024]{1,0:T(8,128)} %get-tuple-element.154.z_ref.zp_ref, f32[32,2,1024]{2,1,0:T(2,128)} %copy-done.7, f32[66]{0:T(128)} %pad_maximum_fusion.3.cnt_ref, f32[1,1024]{1,0:T(1,128)} %bitcast.152, ...), custom_call_target="tpu_custom_call" | custom-call | bytes 33554432 | tf_op jit(solution)/shard_map/forward_plain/pallas_call | solution.py:640
  165.2 21.6 %all_to_all.110.s_ref = f32[32,2,1024]{2,1,0:T(2,128)} all-to-all(f32[32,2,1024]{2,1,0:T(2,128)} %get-tuple-element.163), channel_id=1, replica_groups=mesh['dp'=4,'fsdp'=8] {'dp','fsdp'}, dimensions={0} | all-to-all | bytes 524288 | tf_op jit(solution)/shard_map/all_to_all | solution.py:517
  186.9 9.0 %forward_split.1 = (bf16[1024,1024]{1,0:T(8,128)(2,1)}, f32[1024,512]{1,0:T(8,128)}, f32[8,1024]{1,0:T(8,128)}, f32[1024,512]{1,0:T(8,128)}, f32[32,2,512]{2,1,0:T(2,128)}) custom-call(f32[1024,1024]{1,0:T(8,128)} %get-tuple-element.162.z_ref.zp_ref, f32[32,2,1024]{2,1,0:T(2,128)} %all_to_all.110.s_ref, f32[66]{0:T(128)} %pad_maximum_fusion.3.cnt_ref, ...), custom_call_target="tpu_custom_call" | custom-call | bytes 33554432 | tf_op jit(solution)/shard_map/forward_split/pallas_call | solution.py:640
  199.7 11.7 %all-to-all-done.3.s_ref = f32[32,2,512]{2,1,0:T(2,128)S(1)} async-done(((f32[32,2,512]{2,1,0:T(2,128)}), f32[32,2,512]{2,1,0:T(2,128)S(1)}, u32[]{:S(2)}, u32[]{:S(2)}) %all-to-all-start.3) | async-done | bytes 131104 | tf_op jit(solution)/shard_map/all_to_all | solution.py:517
  212.0 11.7 %forward_three.2 = (bf16[1024,512]{1,0:T(8,128)(2,1)}, f32[8,512]{1,0:T(8,128)}, f32[1024,512]{1,0:T(8,128)}, f32[32,2,512]{2,1,0:T(2,128)}) custom-call(f32[1024,512]{1,0:T(8,128)} %get-tuple-element.164.z_ref.zp_ref, f32[32,2,512]{2,1,0:T(2,128)} %copy-done.15, f32[66]{0:T(128)} %pad_maximum_fusion.3.cnt_ref, f32[1,512]{1,0:T(1,128)} %bitcast.192, ...), custom_call_target="tpu_custom_call" | custom-call | flops 4831838208 | bytes 25165824 | tf_op jit(solution)/shard_map/forward_three/pallas_call | solution.py:640
  223.8 12.7 %all_to_all.111.s_ref = f32[32,2,512]{2,1,0:T(2,128)} all-to-all(f32[32,2,512]{2,1,0:T(2,128)} %get-tuple-element.168), channel_id=1, replica_groups=mesh['dp'=4,'fsdp'=8] {'dp','fsdp'}, dimensions={0} | all-to-all | bytes 262144 | tf_op jit(solution)/shard_map/all_to_all | solution.py:517
  236.5 7.1 %forward_resid.2 = (bf16[1024,512]{1,0:T(8,128)(2,1)}, f32[1024,512]{1,0:T(8,128)}, f32[8,512]{1,0:T(8,128)}, f32[1024,512]{1,0:T(8,128)}, f32[32,2,512]{2,1,0:T(2,128)}) custom-call(f32[1024,512]{1,0:T(8,128)} %get-tuple-element.167.z_ref.zp_ref, f32[32,2,512]{2,1,0:T(2,128)} %all_to_all.111.s_ref, f32[66]{0:T(128)} %pad_maximum_fusion.3.cnt_ref, ...), custom_call_target="tpu_custom_call" | custom-call | bytes 25165824 | tf_op jit(solution)/shard_map/forward_resid/pallas_call | solution.py:640
  247.3 8.1 %all-to-all-done.5.s_ref = f32[32,2,512]{2,1,0:T(2,128)S(1)} async-done(((f32[32,2,512]{2,1,0:T(2,128)}), f32[32,2,512]{2,1,0:T(2,128)S(1)}, u32[]{:S(2)}, u32[]{:S(2)}) %all-to-all-start.5) | async-done | bytes 131104 | tf_op jit(solution)/shard_map/all_to_all | solution.py:517
  256.1 11.7 %forward_three.3 = (bf16[1024,512]{1,0:T(8,128)(2,1)}, f32[8,512]{1,0:T(8,128)}, f32[1024,512]{1,0:T(8,128)}, f32[32,2,512]{2,1,0:T(2,128)}) custom-call(f32[1024,512]{1,0:T(8,128)} %get-tuple-element.170.z_ref.zp_ref, f32[32,2,512]{2,1,0:T(2,128)} %copy-done.18, f32[66]{0:T(128)} %pad_maximum_fusion.3.cnt_ref, f32[1,512]{1,0:T(1,128)} %bitcast.215, ...), custom_call_target="tpu_custom_call" | custom-call | flops 4831838208 | bytes 25165824 | tf_op jit(solution)/shard_map/forward_three/pallas_call | solution.py:640
  267.9 11.4 %all_to_all.112.s_ref = f32[32,2,512]{2,1,0:T(2,128)} all-to-all(f32[32,2,512]{2,1,0:T(2,128)} %get-tuple-element.173), channel_id=1, replica_groups=mesh['dp'=4,'fsdp'=8] {'dp','fsdp'}, dimensions={0} | all-to-all | bytes 262144 | tf_op jit(solution)/shard_map/all_to_all | solution.py:517
  279.3 7.0 forward_resid.3
  289.0 8.1 %all-to-all-done.7.s_ref = f32[32,2,512]{2,1,0:T(2,128)S(1)} async-done(((f32[32,2,512]{2,1,0:T(2,128)}), f32[32,2,512]{2,1,0:T(2,128)S(1)}, u32[]{:S(2)}, u32[]{:S(2)}) %all-to-all-start.7) | async-done | bytes 131104 | tf_op jit(solution)/shard_map/all_to_all | solution.py:517
  297.8 9.1 %forward_join.1 = (bf16[1024,1024]{1,0:T(8,128)(2,1)}, f32[8,512]{1,0:T(8,128)}, f32[1024,1024]{1,0:T(8,128)}, f32[32,2,1024]{2,1,0:T(2,128)}) custom-call(f32[1024,512]{1,0:T(8,128)} %get-tuple-element.175.z_ref.zp_ref, f32[32,2,512]{2,1,0:T(2,128)} %copy-done.12, f32[66]{0:T(128)} %pad_maximum_fusion.3.cnt_ref, f32[1,512]{1,0:T(1,128)} %bitcast.164, ...), custom_call_target="tpu_custom_call" | custom-call | bytes 25165824 | tf_op jit(solution)/shard_map/forward_join/pallas_call | solution.py:640
  306.8 13.3 %all_to_all.113.s_ref = f32[32,2,1024]{2,1,0:T(2,128)} all-to-all(f32[32,2,1024]{2,1,0:T(2,128)} %get-tuple-element.179), channel_id=1, replica_groups=mesh['dp'=4,'fsdp'=8] {'dp','fsdp'}, dimensions={0} | all-to-all | bytes 524288 | tf_op jit(solution)/shard_map/all_to_all | solution.py:517
  320.1 9.4 %top.1 = (bf16[1024,1024]{1,0:T(8,128)(2,1)}, f32[8,1024]{1,0:T(8,128)}, f32[1024,1024]{1,0:T(8,128)}, f32[32,2,1024]{2,1,0:T(2,128)}) custom-call(f32[1024,1024]{1,0:T(8,128)} %get-tuple-element.178.z_ref, f32[32,2,1024]{2,1,0:T(2,128)} %all_to_all.113.s_ref, f32[66]{0:T(128)} %pad_maximum_fusion.3.cnt_ref, f32[1,1024]{1,0:T(1,128)} %bitcast.158, ...), custom_call_target="tpu_custom_call" | custom-call | bytes 33554432 | tf_op jit(solution)/shard_map/top/pallas_call | solution.py:671
  329.5 13.3 %all_to_all.114.s_ref = f32[32,2,1024]{2,1,0:T(2,128)} all-to-all(f32[32,2,1024]{2,1,0:T(2,128)} %get-tuple-element.183), channel_id=1, replica_groups=mesh['dp'=4,'fsdp'=8] {'dp','fsdp'}, dimensions={0} | all-to-all | bytes 524288 | tf_op jit(solution)/shard_map/all_to_all | solution.py:517
  342.8 10.7 %backward_part.1 = (bf16[1024,1024]{1,0:T(8,128)(2,1)}, f32[8,1024]{1,0:T(8,128)}, f32[1024,512]{1,0:T(8,128)}, f32[1024,512]{1,0:T(8,128)}, f32[32,2,512]{2,1,0:T(2,128)}) custom-call(f32[1024,1024]{1,0:T(8,128)} %get-tuple-element.181.g_ref, f32[1024,1024]{1,0:T(8,128)} %get-tuple-element.178.z_ref, f32[8,1024]{1,0:T(8,128)} %get-tuple-element.281.mv_ref, ...), custom_call_target="tpu_custom_call" | custom-call | bytes 25165824 | tf_op jit(solution)/shard_map/backward_part/pallas_call | solution.py:728
  356.4 5.3 convolution_convert_fusion
  365.1 7.8 %backward_keep.1 = (bf16[1024,512]{1,0:T(8,128)(2,1)}, f32[8,512]{1,0:T(8,128)}, f32[1024,512]{1,0:T(8,128)}, f32[1024,512]{1,0:T(8,128)}, f32[32,2,512]{2,1,0:T(2,128)}) custom-call(f32[1024,512]{1,0:T(8,128)} %get-tuple-element.185.g_ref, f32[1024,512]{1,0:T(8,128)} %get-tuple-element.175.z_ref.zp_ref, f32[8,512]{1,0:T(8,128)} %get-tuple-element.280.mvp_ref.mv_ref, ...), custom_call_target="tpu_custom_call" | custom-call | bytes 25165824 | tf_op jit(solution)/shard_map/backward_keep/pallas_call | solution.py:728
  378.4 7.5 %all-to-all-done.11.s_ref = f32[32,2,512]{2,1,0:T(2,128)S(1)} async-done(((f32[32,2,512]{2,1,0:T(2,128)}), f32[32,2,512]{2,1,0:T(2,128)S(1)}, u32[]{:S(2)}, u32[]{:S(2)}) %all-to-all-start.11) | async-done | bytes 131104 | tf_op jit(solution)/shard_map/all_to_all | solution.py:517
  386.6 12.7 %backward_three.2 = (bf16[1024,512]{1,0:T(8,128)(2,1)}, f32[8,512]{1,0:T(8,128)}, f32[1024,512]{1,0:T(8,128)}, f32[32,2,512]{2,1,0:T(2,128)}) custom-call(f32[1024,512]{1,0:T(8,128)} %get-tuple-element.191.g_ref, f32[1024,512]{1,0:T(8,128)} %get-tuple-element.172.z_ref.zp_ref, f32[8,512]{1,0:T(8,128)} %get-tuple-element.279.mvp_ref.mv_ref, ...), custom_call_target="tpu_custom_call" | custom-call | flops 4831838208 | bytes 25165824 | tf_op jit(solution)/shard_map/backward_three/pallas_call | solution.py:728
  402.0 9.5 %weight_grad_1.2 = bf16[8,9,64,512]{3,2,1,0:T(8,128)(2,1)} custom-call(bf16[1024,512]{1,0:T(8,128)(2,1)} %get-tuple-element.199.x_ref, bf16[9,1024,128]{2,1,0:T(8,128)(2,1)} %get-tuple-element.166.rest_0_.m_ref, bf16[1024,512]{1,0:T(8,128)(2,1)} %get-tuple-element.200.dz_ref), custom_call_target="tpu_custom_call" | custom-call | flops 4831838208 | bytes 4194304 | tf_op jit(solution)/shard_map/weight_grad_1/pallas_call | solution.py:745
  412.1 8.3 %backward_add.1 = (bf16[1024,512]{1,0:T(8,128)(2,1)}, f32[8,512]{1,0:T(8,128)}, f32[1024,512]{1,0:T(8,128)}, f32[1024,512]{1,0:T(8,128)}, f32[32,2,512]{2,1,0:T(2,128)}) custom-call(f32[1024,512]{1,0:T(8,128)} %get-tuple-element.197.g_ref, f32[1024,512]{1,0:T(8,128)} %get-tuple-element.170.z_ref.zp_ref, f32[8,512]{1,0:T(8,128)} %get-tuple-element.278.mvp_ref.mv_ref, ...), custom_call_target="tpu_custom_call" | custom-call | bytes 25165824 | tf_op jit(solution)/shard_map/backward_add/pallas_call | solution.py:728
  420.4 5.8 all-to-all-start.13
  428.3 8.2 %all-to-all-done.13.s_ref = f32[32,2,512]{2,1,0:T(2,128)S(1)} async-done(((f32[32,2,512]{2,1,0:T(2,128)}), f32[32,2,512]{2,1,0:T(2,128)S(1)}, u32[]{:S(2)}, u32[]{:S(2)}) %all-to-all-start.13) | async-done | bytes 131104 | tf_op jit(solution)/shard_map/all_to_all | solution.py:517
  437.1 12.7 %backward_three.3 = (bf16[1024,512]{1,0:T(8,128)(2,1)}, f32[8,512]{1,0:T(8,128)}, f32[1024,512]{1,0:T(8,128)}, f32[32,2,512]{2,1,0:T(2,128)}) custom-call(f32[1024,512]{1,0:T(8,128)} %get-tuple-element.205.g_ref, f32[1024,512]{1,0:T(8,128)} %get-tuple-element.167.z_ref.zp_ref, f32[8,512]{1,0:T(8,128)} %get-tuple-element.277.mvp_ref.mv_ref, ...), custom_call_target="tpu_custom_call" | custom-call | flops 4831838208 | bytes 25165824 | tf_op jit(solution)/shard_map/backward_three/pallas_call | solution.py:728
  452.6 9.5 %weight_grad_1.3 = bf16[8,9,64,512]{3,2,1,0:T(8,128)(2,1)} custom-call(bf16[1024,512]{1,0:T(8,128)(2,1)} %get-tuple-element.212.x_ref, bf16[9,1024,128]{2,1,0:T(8,128)(2,1)} %get-tuple-element.166.rest_0_.m_ref, bf16[1024,512]{1,0:T(8,128)(2,1)} %get-tuple-element.213.dz_ref), custom_call_target="tpu_custom_call" | custom-call | flops 4831838208 | bytes 4194304 | tf_op jit(solution)/shard_map/weight_grad_1/pallas_call | solution.py:745
  463.2 13.0 %backward_merge.1 = (bf16[1024,512]{1,0:T(8,128)(2,1)}, f32[8,512]{1,0:T(8,128)}, f32[1024,1024]{1,0:T(8,128)}, f32[32,2,1024]{2,1,0:T(2,128)}) custom-call(f32[1024,512]{1,0:T(8,128)} %get-tuple-element.216.g_ref, f32[1024,512]{1,0:T(8,128)} %get-tuple-element.164.z_ref.zp_ref, f32[8,512]{1,0:T(8,128)} %get-tuple-element.276.mvp_ref.mv_ref, ...), custom_call_target="tpu_custom_call" | custom-call | bytes 33554432 | tf_op jit(solution)/shard_map/backward_merge/pallas_call | solution.py:728
  476.1 5.4 all-to-all-start.15
  484.3 12.5 %all-to-all-done.15.s_ref = f32[32,2,1024]{2,1,0:T(2,128)S(1)} async-done(((f32[32,2,1024]{2,1,0:T(2,128)}), f32[32,2,1024]{2,1,0:T(2,128)S(1)}, u32[]{:S(2)}, u32[]{:S(2)}) %all-to-all-start.15) | async-done | bytes 262176 | tf_op jit(solution)/shard_map/all_to_all | solution.py:517
  497.5 12.5 %backward_plain.1 = (bf16[1024,1024]{1,0:T(8,128)(2,1)}, f32[8,1024]{1,0:T(8,128)}, f32[1024,1024]{1,0:T(8,128)}, f32[32,2,1024]{2,1,0:T(2,128)}) custom-call(f32[1024,1024]{1,0:T(8,128)} %get-tuple-element.221.g_ref, f32[1024,1024]{1,0:T(8,128)} %get-tuple-element.162.z_ref.zp_ref, f32[8,1024]{1,0:T(8,128)} %get-tuple-element.275.mvp_ref.mv_ref, ...), custom_call_target="tpu_custom_call" | custom-call | bytes 33554432 | tf_op jit(solution)/shard_map/backward_plain/pallas_call | solution.py:728
  522.6 5.3 all-to-all-done.16.s_ref
  528.6 6.1 down_norm.1
  534.7 11.5 %weight_grad_2.2 = bf16[8,5,64,1024]{3,2,1,0:T(8,128)(2,1)} custom-call(bf16[4,1024,512]{2,1,0:T(8,128)(2,1)} %get-tuple-element.151.ph_ref.x_ref, bf16[9,1024,128]{2,1,0:T(8,128)(2,1)} %get-tuple-element.152.m_ref, bf16[1024,1024]{1,0:T(8,128)(2,1)} %get-tuple-element.240.dz_ref), custom_call_target="tpu_custom_call" | custom-call | flops 9663676416 | bytes 8388608 | tf_op jit(solution)/shard_map/weight_grad_2/pallas_call | solution.py:745
  558.9 10.1 %weight_grad_2.3 = bf16[4,512,1024]{2,1,0:T(8,128)(2,1)} custom-call(bf16[4,1024,512]{2,1,0:T(8,128)(2,1)} %get-tuple-element.151.ph_ref.x_ref, bf16[9,1024,128]{2,1,0:T(8,128)(2,1)} %get-tuple-element.152.m_ref, bf16[1024,1024]{1,0:T(8,128)(2,1)} %get-tuple-element.240.dz_ref), custom_call_target="tpu_custom_call" | custom-call | flops 9663676416 | bytes 8388608 | tf_op jit(solution)/shard_map/weight_grad_2/pallas_call | solution.py:745
  569.0 7.5 %all-to-all-done.17 = bf16[4,352,512]{2,1,0:T(8,128)(2,1)S(1)} async-done(((bf16[4,352,512]{2,1,0:T(8,128)(2,1)}), bf16[4,352,512]{2,1,0:T(8,128)(2,1)S(1)}, u32[]{:S(2)}, u32[]{:S(2)}) %all-to-all-start.17) | async-done | bytes 1441824 | tf_op jit(solution)/shard_map/all_to_all | solution.py:761
  590.7 17.9 %input_grad.1 = bf16[4,16,2,32,512]{4,3,2,1,0:T(8,128)(2,1)} custom-call(bf16[1024,1024]{1,0:T(8,128)(2,1)} %get-tuple-element.240.dz_ref, bf16[9,1024,128]{2,1,0:T(8,128)(2,1)} %get-tuple-element.241.m_ref, bf16[8,5,64,1024]{3,2,1,0:T(8,128)(2,1)} %bitcast.223, bf16[4,8,128,512]{3,2,1,0:T(8,128)(2,1)} %bitcast_dynamic-update-slice_fusion.4.wb_ref), custom_call_target="tpu_custom_call" | custom-call | flops 9663676416 | bytes 33554432 | tf_op jit(solution)/shard_map/input_grad/pallas_call | solution.py:834
  608.6 30.3 %collective-permute-done.7 = bf16[512,1024]{1,0:T(8,128)(2,1)} collective-permute-done((bf16[512,1024]{1,0:T(8,128)(2,1)}, bf16[512,1024]{1,0:T(8,128)(2,1)}, u32[]{:S(2)}, u32[]{:S(2)}) %collective-permute-start.7) | collective-permute-done | bytes 1048608 | tf_op jit(solution)/shard_map/ppermute | solution.py:484
  651.7 4.4 all-to-all-start.19
  669.6 4.5 all-to-all-start.20
  679.9 5.3 all-to-all-done.20
  (250 shorter events, 173.2 us)
Async XLA Ops:
  7.2 39.0 %all-gather.10.cloned.1.call-start = ((), (), s32[]{:S(2)}) async-start(), calls=%async_computation.28 | async-start | bytes 2359296 | tf_op jit(solution)/shard_map/all_gather | solution.py:463
  13.6 90.0 %all-gather.12.cloned.1.call-start = ((), (), s32[]{:S(2)}) async-start(), calls=%async_computation.35 | async-start | bytes 5898240 | tf_op jit(solution)/shard_map/all_gather | solution.py:463
  14.6 11.1 %copy-start.27 = (s32[4,2]{0,1:T(2,128)S(1)}, s32[4,2]{0,1:T(2,128)}, u32[]{:S(2)}) copy-start(s32[4,2]{0,1:T(2,128)} %param.16) | copy-start | bytes 100
  14.7 185.0 %all-gather.14.cloned.1.call-start = ((), (), s32[]{:S(2)}) async-start(), calls=%async_computation.36 | async-start | bytes 5308416 | tf_op jit(solution)/shard_map/all_gather | solution.py:463
  15.9 231.4 %all-gather.16.cloned.1.call-start = ((), (), s32[]{:S(2)}) async-start(), calls=%async_computation.37 | async-start | bytes 5308416 | tf_op jit(solution)/shard_map/all_gather | solution.py:463
  18.4 17.2 %all-to-all-start = ((f32[32,1,128]{2,1,0:T(1,128)}), f32[32,1,128]{2,1,0:T(1,128)S(1)}, u32[]{:S(2)}, u32[]{:S(2)}) async-start(f32[32,1,128]{2,1,0:T(1,128)} %broadcast_in_dim.53), calls=%async_computation | async-start | bytes 32768 | tf_op jit(solution)/shard_map/all_to_all | solution.py:510
  25.7 263.3 %all-gather.18.cloned.1.call-start = ((), (), s32[]{:S(2)}) async-start(), calls=%async_computation.38 | async-start | bytes 2359296 | tf_op jit(solution)/shard_map/all_gather | solution.py:506
  48.8 26.3 %collective-permute-start = (bf16[8,128,512]{2,1,0:T(8,128)(2,1)}, bf16[8,128,512]{2,1,0:T(8,128)(2,1)}, u32[]{:S(2)}, u32[]{:S(2)}) collective-permute-start(bf16[8,128,512]{2,1,0:T(8,128)(2,1)} %get-tuple-element.289), channel_id=1, source_target_pairs={{0,8},{8,0},{16,24},{24,16},{1,9},{9,1},{17,25},{25,17},{2,10},{10... | collective-permute-start | bytes 3145736 | tf_op jit(solution)/shard_map/ppermute | solution.py:484
  50.3 47.7 %collective-permute-start.1 = (bf16[8,128,512]{2,1,0:T(8,128)(2,1)}, bf16[8,128,512]{2,1,0:T(8,128)(2,1)S(1)}, u32[]{:S(2)}, u32[]{:S(2)}) collective-permute-start(bf16[8,128,512]{2,1,0:T(8,128)(2,1)} %get-tuple-element.289), channel_id=1, source_target_pairs={{0,16},{8,24},{16,0},{24,8},{1,17},{9,25},{17,1},{25,9},{2,18},{10... | collective-permute-start | bytes 3145736 | tf_op jit(solution)/shard_map/ppermute | solution.py:484
  51.8 47.3 %collective-permute-start.2 = (bf16[8,128,512]{2,1,0:T(8,128)(2,1)}, bf16[8,128,512]{2,1,0:T(8,128)(2,1)S(1)}, u32[]{:S(2)}, u32[]{:S(2)}) collective-permute-start(bf16[8,128,512]{2,1,0:T(8,128)(2,1)} %get-tuple-element.289), channel_id=1, source_target_pairs={{0,24},{8,16},{16,8},{24,0},{1,25},{9,17},{17,9},{25,1},{2,26},{10... | collective-permute-start | bytes 3145736 | tf_op jit(solution)/shard_map/ppermute | solution.py:484
  100.2 28.0 %collective-permute-start.3 = (bf16[8,128,512]{2,1,0:T(8,128)(2,1)S(1)}, bf16[8,128,512]{2,1,0:T(8,128)(2,1)S(1)}, u32[]{:S(2)}, u32[]{:S(2)}) collective-permute-start(bf16[8,128,512]{2,1,0:T(8,128)(2,1)S(1)} %get-tuple-element.155), channel_id=1, source_target_pairs={{0,8},{8,0},{16,24},{24,16},{1,9},{9,1},{17,25},{25,17},{2,10},{10... | collective-permute-start | bytes 3145736 | tf_op jit(solution)/shard_map/ppermute | solution.py:484
  100.3 48.3 %collective-permute-start.4 = (bf16[8,128,512]{2,1,0:T(8,128)(2,1)S(1)}, bf16[8,128,512]{2,1,0:T(8,128)(2,1)S(1)}, u32[]{:S(2)}, u32[]{:S(2)}) collective-permute-start(bf16[8,128,512]{2,1,0:T(8,128)(2,1)S(1)} %get-tuple-element.155), channel_id=1, source_target_pairs={{0,16},{8,24},{16,0},{24,8},{1,17},{9,25},{17,1},{25,9},{2,18},{10... | collective-permute-start | bytes 3145736 | tf_op jit(solution)/shard_map/ppermute | solution.py:484
  102.2 48.4 %collective-permute-start.5 = (bf16[8,128,512]{2,1,0:T(8,128)(2,1)S(1)}, bf16[8,128,512]{2,1,0:T(8,128)(2,1)}, u32[]{:S(2)}, u32[]{:S(2)}) collective-permute-start(bf16[8,128,512]{2,1,0:T(8,128)(2,1)S(1)} %get-tuple-element.155), channel_id=1, source_target_pairs={{0,24},{8,16},{16,8},{24,0},{1,25},{9,17},{17,9},{25,1},{2,26},{10... | collective-permute-start | bytes 3145736 | tf_op jit(solution)/shard_map/ppermute | solution.py:484
  103.7 19.7 %copy-start.22 = (f32[5632]{0:T(1024)S(1)}, f32[5632]{0:T(1024)}, u32[]{:S(2)}) copy-start(f32[5632]{0:T(1024)} %param.24) | copy-start | bytes 67588
  103.7 20.3 %copy-start.23 = (f32[5632]{0:T(1024)S(1)}, f32[5632]{0:T(1024)}, u32[]{:S(2)}) copy-start(f32[5632]{0:T(1024)} %param.25) | copy-start | bytes 67588
  120.5 30.4 %all-to-all-start.1 = ((f32[32,2,1024]{2,1,0:T(2,128)}), f32[32,2,1024]{2,1,0:T(2,128)S(1)}, u32[]{:S(2)}, u32[]{:S(2)}) async-start(f32[32,2,1024]{2,1,0:T(2,128)} %get-tuple-element.156), calls=%async_computation.1 | async-start | bytes 524288 | tf_op jit(solution)/shard_map/all_to_all | solution.py:517
  195.8 15.5 %all-to-all-start.3 = ((f32[32,2,512]{2,1,0:T(2,128)}), f32[32,2,512]{2,1,0:T(2,128)S(1)}, u32[]{:S(2)}, u32[]{:S(2)}) async-start(f32[32,2,512]{2,1,0:T(2,128)} %get-tuple-element.165), calls=%async_computation.3 | async-start | bytes 262144 | tf_op jit(solution)/shard_map/all_to_all | solution.py:517
  243.6 11.9 %all-to-all-start.5 = ((f32[32,2,512]{2,1,0:T(2,128)}), f32[32,2,512]{2,1,0:T(2,128)S(1)}, u32[]{:S(2)}, u32[]{:S(2)}) async-start(f32[32,2,512]{2,1,0:T(2,128)} %get-tuple-element.171), calls=%async_computation.5 | async-start | bytes 262144 | tf_op jit(solution)/shard_map/all_to_all | solution.py:517
  286.3 10.8 %all-to-all-start.7 = ((f32[32,2,512]{2,1,0:T(2,128)}), f32[32,2,512]{2,1,0:T(2,128)S(1)}, u32[]{:S(2)}, u32[]{:S(2)}) async-start(f32[32,2,512]{2,1,0:T(2,128)} %get-tuple-element.176), calls=%async_computation.7 | async-start | bytes 262144 | tf_op jit(solution)/shard_map/all_to_all | solution.py:517
  342.8 13.6 %copy-start.31 = (bf16[1024,1024]{1,0:T(8,128)(2,1)S(1)}, bf16[1024,1024]{1,0:T(8,128)(2,1)}, u32[]{:S(2)}) copy-start(bf16[1024,1024]{1,0:T(8,128)(2,1)} %get-tuple-element.187) | copy-start | bytes 6291460
  353.5 11.0 %all-to-all-start.10 = ((f32[32,2,512]{2,1,0:T(2,128)}), f32[32,2,512]{2,1,0:T(2,128)S(1)}, u32[]{:S(2)}, u32[]{:S(2)}) async-start(f32[32,2,512]{2,1,0:T(2,128)} %get-tuple-element.186), calls=%async_computation.10 | async-start | bytes 262144 | tf_op jit(solution)/shard_map/all_to_all | solution.py:517
  356.3 55.1 %reduce-scatter.7.cloned.1.call-start = ((), (), s32[]{:S(2)}) async-start(), calls=%async_computation.29 | async-start | bytes 2359296 | tf_op jit(solution)/shard_map/reduce_scatter | solution.py:757
  365.1 11.3 %copy-start.34 = (bf16[1024,512]{1,0:T(8,128)(2,1)S(1)}, bf16[1024,512]{1,0:T(8,128)(2,1)}, u32[]{:S(2)}) copy-start(bf16[1024,512]{1,0:T(8,128)(2,1)} %get-tuple-element.193) | copy-start | bytes 3145732
  373.0 12.9 %all-to-all-start.11 = ((f32[32,2,512]{2,1,0:T(2,128)}), f32[32,2,512]{2,1,0:T(2,128)S(1)}, u32[]{:S(2)}, u32[]{:S(2)}) async-start(f32[32,2,512]{2,1,0:T(2,128)} %get-tuple-element.192), calls=%async_computation.11 | async-start | bytes 262144 | tf_op jit(solution)/shard_map/all_to_all | solution.py:517
  399.3 12.2 %all-to-all-start.12 = ((f32[32,2,512]{2,1,0:T(2,128)}), f32[32,2,512]{2,1,0:T(2,128)S(1)}, u32[]{:S(2)}, u32[]{:S(2)}) async-start(f32[32,2,512]{2,1,0:T(2,128)} %get-tuple-element.198), calls=%async_computation.12 | async-start | bytes 262144 | tf_op jit(solution)/shard_map/all_to_all | solution.py:517
  402.0 94.9 %reduce-scatter.11.cloned.1.call-start = ((), (), s32[]{:S(2)}) async-start(), calls=%async_computation.31 | async-start | bytes 5308416 | tf_op jit(solution)/shard_map/reduce_scatter | solution.py:757
  412.1 14.2 %copy-start.33 = (bf16[1024,512]{1,0:T(8,128)(2,1)S(1)}, bf16[1024,512]{1,0:T(8,128)(2,1)}, u32[]{:S(2)}) copy-start(bf16[1024,512]{1,0:T(8,128)(2,1)} %get-tuple-element.207) | copy-start | bytes 3145732
  420.4 16.0 %all-to-all-start.13 = ((f32[32,2,512]{2,1,0:T(2,128)}), f32[32,2,512]{2,1,0:T(2,128)S(1)}, u32[]{:S(2)}, u32[]{:S(2)}) async-start(f32[32,2,512]{2,1,0:T(2,128)} %get-tuple-element.206), calls=%async_computation.14 | async-start | bytes 262144 | tf_op jit(solution)/shard_map/all_to_all | solution.py:517
  449.7 12.8 %all-to-all-start.14 = ((f32[32,2,512]{2,1,0:T(2,128)}), f32[32,2,512]{2,1,0:T(2,128)S(1)}, u32[]{:S(2)}, u32[]{:S(2)}) async-start(f32[32,2,512]{2,1,0:T(2,128)} %get-tuple-element.211), calls=%async_computation.15 | async-start | bytes 262144 | tf_op jit(solution)/shard_map/all_to_all | solution.py:517
  452.3 99.6 %reduce-scatter.9.cloned.1.call-start = ((), (), s32[]{:S(2)}) async-start(), calls=%async_computation.30 | async-start | bytes 5308416 | tf_op jit(solution)/shard_map/reduce_scatter | solution.py:757
  463.2 18.4 %copy-start.1 = (bf16[1024,1024]{1,0:T(8,128)(2,1)S(1)}, bf16[1024,1024]{1,0:T(8,128)(2,1)}, u32[]{:S(2)}) copy-start(bf16[1024,1024]{1,0:T(8,128)(2,1)} %get-tuple-element.177.rest_0_) | copy-start | bytes 6291460
  476.1 20.7 %all-to-all-start.15 = ((f32[32,2,1024]{2,1,0:T(2,128)}), f32[32,2,1024]{2,1,0:T(2,128)S(1)}, u32[]{:S(2)}, u32[]{:S(2)}) async-start(f32[32,2,1024]{2,1,0:T(2,128)} %get-tuple-element.222), calls=%async_computation.18 | async-start | bytes 524288 | tf_op jit(solution)/shard_map/all_to_all | solution.py:517
  497.5 15.4 %copy-start.30 = (bf16[1024,1024]{1,0:T(8,128)(2,1)S(1)}, bf16[1024,1024]{1,0:T(8,128)(2,1)}, u32[]{:S(2)}) copy-start(bf16[1024,1024]{1,0:T(8,128)(2,1)} %get-tuple-element.228) | copy-start | bytes 6291460
  510.1 17.9 %all-to-all-start.16 = ((f32[32,2,1024]{2,1,0:T(2,128)}), f32[32,2,1024]{2,1,0:T(2,128)S(1)}, u32[]{:S(2)}, u32[]{:S(2)}) async-start(f32[32,2,1024]{2,1,0:T(2,128)} %get-tuple-element.227), calls=%async_computation.19 | async-start | bytes 524288 | tf_op jit(solution)/shard_map/all_to_all | solution.py:517
  512.7 135.6 %reduce-scatter.13.cloned.1.call-start = ((), (), s32[]{:S(2)}) async-start(), calls=%async_computation.32 | async-start | bytes 4128768 | tf_op jit(solution)/shard_map/reduce_scatter | solution.py:757
  528.0 120.3 %reduce-scatter.15.cloned.1.call-start = ((), (), s32[]{:S(2)}) async-start(), calls=%async_computation.33 | async-start | bytes 5898240 | tf_op jit(solution)/shard_map/reduce_scatter | solution.py:757
  554.4 22.1 %all-to-all-start.17 = ((bf16[4,352,512]{2,1,0:T(8,128)(2,1)}), bf16[4,352,512]{2,1,0:T(8,128)(2,1)S(1)}, u32[]{:S(2)}, u32[]{:S(2)}) async-start(bf16[4,352,512]{2,1,0:T(8,128)(2,1)} %bitcast.51), calls=%async_computation.20 | async-start | bytes 2883584 | tf_op jit(solution)/shard_map/all_to_all | solution.py:761
  576.9 7.6 %copy-start.21 = (f32[5632]{0:T(1024)S(1)}, f32[5632]{0:T(1024)}, u32[]{:S(2)}) copy-start(f32[5632]{0:T(1024)} %param.27) | copy-start | bytes 67588
  581.0 27.6 %collective-permute-start.6 = (bf16[512,1024]{1,0:T(8,128)(2,1)}, bf16[512,1024]{1,0:T(8,128)(2,1)}, u32[]{:S(2)}, u32[]{:S(2)}) collective-permute-start(bf16[512,1024]{1,0:T(8,128)(2,1)} %get-tuple-element.287), channel_id=1, source_target_pairs={{0,8},{8,0},{16,24},{24,16},{1,9},{9,1},{17,25},{25,17},{2,10},{10... | collective-permute-start | bytes 3145736 | tf_op jit(solution)/shard_map/ppermute | solution.py:484
  582.4 56.5 %collective-permute-start.7 = (bf16[512,1024]{1,0:T(8,128)(2,1)}, bf16[512,1024]{1,0:T(8,128)(2,1)}, u32[]{:S(2)}, u32[]{:S(2)}) collective-permute-start(bf16[512,1024]{1,0:T(8,128)(2,1)} %get-tuple-element.286), channel_id=1, source_target_pairs={{0,16},{8,24},{16,0},{24,8},{1,17},{9,25},{17,1},{25,9},{2,18},{10... | collective-permute-start | bytes 3145736 | tf_op jit(solution)/shard_map/ppermute | solution.py:484
  583.0 56.0 %collective-permute-start.8 = (bf16[512,1024]{1,0:T(8,128)(2,1)S(1)}, bf16[512,1024]{1,0:T(8,128)(2,1)}, u32[]{:S(2)}, u32[]{:S(2)}) collective-permute-start(bf16[512,1024]{1,0:T(8,128)(2,1)S(1)} %get-tuple-element.285), channel_id=1, source_target_pairs={{0,24},{8,16},{16,8},{24,0},{1,25},{9,17},{17,9},{25,1},{2,26},{10... | collective-permute-start | bytes 3145736 | tf_op jit(solution)/shard_map/ppermute | solution.py:484
  586.3 60.2 %all-to-all-start.18 = ((bf16[4,352,512]{2,1,0:T(8,128)(2,1)}), bf16[4,352,512]{2,1,0:T(8,128)(2,1)}, u32[]{:S(2)}, u32[]{:S(2)}) async-start(bf16[4,352,512]{2,1,0:T(8,128)(2,1)} %broadcast_in_dim.62), calls=%async_computation.23 | async-start | bytes 2883584 | tf_op jit(solution)/shard_map/all_to_all | solution.py:766
  590.6 98.8 %reduce-scatter.17.cloned.1.call-start = ((), (), s32[]{:S(2)}) async-start(), calls=%async_computation.34 | async-start | bytes 1179648 | tf_op jit(solution)/shard_map/reduce_scatter | solution.py:757
  651.7 15.3 %all-to-all-start.19 = ((bf16[4,272,512]{2,1,0:T(8,128)(2,1)}), bf16[4,272,512]{2,1,0:T(8,128)(2,1)}, u32[]{:S(2)}, u32[]{:S(2)}) async-start(bf16[4,272,512]{2,1,0:T(8,128)(2,1)} %pad_maximum_fusion.1), calls=%async_computation.24 | async-start | bytes 2228224 | tf_op jit(solution)/shard_map/all_to_all | solution.py:761
  668.5 7.0 copy-start.24
  669.6 15.6 %all-to-all-start.20 = ((bf16[4,272,512]{2,1,0:T(8,128)(2,1)}), bf16[4,272,512]{2,1,0:T(8,128)(2,1)}, u32[]{:S(2)}, u32[]{:S(2)}) async-start(bf16[4,272,512]{2,1,0:T(8,128)(2,1)} %broadcast_in_dim.63), calls=%async_computation.25 | async-start | bytes 2228224 | tf_op jit(solution)/shard_map/all_to_all | solution.py:766
  689.3 9.1 %copy-start.2 = (f32[3,64,1,512]{3,2,1,0:T(1,128)S(1)}, f32[3,64,1,512]{3,2,1,0:T(1,128)}, u32[]{:S(2)}) copy-start(f32[3,64,1,512]{3,2,1,0:T(1,128)} %reshape.181) | copy-start | bytes 1179652
  691.2 10.1 %all-to-all-start.21 = ((bf16[4,64,1024]{2,1,0:T(8,128)(2,1)}), bf16[4,64,1024]{2,1,0:T(8,128)(2,1)S(1)}, u32[]{:S(2)}, u32[]{:S(2)}) async-start(bf16[4,64,1024]{2,1,0:T(8,128)(2,1)} %broadcast_in_dim.64), calls=%async_computation.27 | async-start | bytes 1048576 | tf_op jit(solution)/shard_map/all_to_all | solution.py:766
  (24 other events, 55.7 us)
Sparse Core Ops, SparseCore 0:
  13.8 32.3 all-gather.9
  47.8 55.1 all-gather.11
  104.6 55.5 all-gather.13
  161.8 58.5 all-gather.15
  221.8 30.3 all-gather.17
  364.6 36.2 reduce-scatter.6
  411.6 60.3 reduce-scatter.10
  474.3 62.2 reduce-scatter.8
  538.9 45.3 reduce-scatter.12
  586.4 58.2 reduce-scatter.14
  646.9 31.0 reduce-scatter.16

commit v2 on v1

--- a/solution.py
+++ b/solution.py
@@ -24,35 +24,24 @@
 
 
 def mish_parts(y):
-    u = jnp.exp(-jnp.abs(y))
-    pos = y > 0.0
-    num = jnp.where(pos, 1.0 + 2.0 * u, u * (u + 2.0))
-    gap = jnp.where(pos, 2.0 * u * u, 2.0)
-    return u, pos, num, gap, num + gap
+    e = jnp.exp(jnp.minimum(y, 20.0))
+    n = e * (e + 2.0)
+    return e, n, 1.0 / (n + 2.0)
 
 
 def mish(y):
-    _, _, num, _, den = mish_parts(y)
-    return y * (num / den)
+    _, n, r = mish_parts(y)
+    return y * (n * r)
 
 
 def mish_slope(y):
-    u, pos, num, gap, den = mish_parts(y)
-    once = 1.0 + u
-    both = 1.0 / (den * once)
-    inv = both * once
-    sig = jnp.where(pos, 1.0, u) * (both * den)
-    return num * inv + y * sig * (gap * inv) * ((den + num) * inv)
+    e, n, r = mish_parts(y)
+    return r * (n + (4.0 * y) * ((n - e) * r))
 
 
 def mish_both(y):
-    u, pos, num, gap, den = mish_parts(y)
-    once = 1.0 + u
-    both = 1.0 / (den * once)
-    inv = both * once
-    sig = jnp.where(pos, 1.0, u) * (both * den)
-    tan = num * inv
-    return y * tan, tan + y * sig * (gap * inv) * ((den + num) * inv)
+    e, n, r = mish_parts(y)
+    return y * (n * r), r * (n + (4.0 * y) * ((n - e) * r))
 
 
 def col_shift(x, step):
@@ -148,11 +137,16 @@
     return mean, var, lax.rsqrt(var + norm_eps)
 
 
-def write_moments(mv_ref, mean, var, inv):
-    mv_ref[0:1] = mean
-    mv_ref[1:2] = var
-    mv_ref[2:3] = inv
-    mv_ref[3:8] = jnp.zeros((5, mean.shape[1]), F32)
+def kept_moments(s_ref, cnt_ref, mv_ref):
+    @pl.when(pl.program_id(0) == 0)
+    def _():
+        mean, var, inv = moments(s_ref, cnt_ref)
+        mv_ref[0:1] = mean
+        mv_ref[1:2] = var
+        mv_ref[2:3] = inv
+        mv_ref[3:8] = jnp.zeros((5, mean.shape[1]), F32)
+
+    return mv_ref[0:1], mv_ref[2:3]
 
 
 def collect_moments(out, valid, acc_ref, num_ref, st_ref):
@@ -259,12 +253,7 @@
     v_ref = rest.pop(0)
     keep_ref = rest.pop(0) if kind in ("split", "resid") else None
     mv_ref, out_ref, st_ref, acc_ref, num_ref = rest
-    mean, var, inv = moments(s_ref, cnt_ref)
-
-    @pl.when(pl.program_id(0) == 0)
-    def _():
-        write_moments(mv_ref, mean, var, inv)
-
+    mean, inv = kept_moments(s_ref, cnt_ref, mv_ref)
     act = mish(((z_ref[...] - mean) * inv) * gain_ref[...] + bias_ref[...])
     if kind == "split":
         half = act.shape[1] // 2
@@ -298,33 +287,28 @@
 def top_kernel(
     z_ref, s_ref, cnt_ref, gain_ref, bias_ref, cot_ref, o_ref, mv_ref, g_ref, st_ref, acc_ref
 ):
-    mean, var, inv = moments(s_ref, cnt_ref)
-
-    @pl.when(pl.program_id(0) == 0)
-    def _():
-        write_moments(mv_ref, mean, var, inv)
-
+    mean, inv = kept_moments(s_ref, cnt_ref, mv_ref)
     xhat = (z_ref[...] - mean) * inv
     act, slope = mish_both(xhat * gain_ref[...] + bias_ref[...])
     o_ref[...] = act.astype(BF16)
     g = cot_ref[...].astype(F32) * slope
-    g_ref[...] = g
+    g_ref[...] = g.astype(BF16)
     collect_sums(g, xhat, acc_ref, st_ref)
 
 
 def norm_grad(g_ref, z_ref, mv_ref, s_ref, gain_ref, valid_ref, cnt_ref, tot_ref):
-    total = device_total(s_ref)
-
     @pl.when(pl.program_id(0) == 0)
     def _():
+        total = device_total(s_ref)
         tot_ref[0:2] = total
         tot_ref[2:8] = jnp.zeros((6, total.shape[1]), F32)
 
+    total = tot_ref[0:2]
     inv = mv_ref[2:3]
     inv_n = cnt_ref[2 * s_ref.shape[0] + 1]
     xhat = (z_ref[...] - mv_ref[0:1]) * inv
     mean_part = (valid_ref[...] * inv_n) * (total[0:1] + xhat * total[1:2])
-    return (gain_ref[...] * inv * (g_ref[...] - mean_part)).astype(BF16)
+    return (gain_ref[...] * inv * (g_ref[...].astype(F32) - mean_part)).astype(BF16)
 
 
 def backward_kernel(
@@ -378,7 +362,7 @@
         ga = jnp.concatenate([route_ref[...], ga + add_ref[...]], axis=1)
     xhat = (zp_ref[...] - mvp_ref[0:1]) * mvp_ref[2:3]
     gp = ga * mish_slope(xhat * gainp_ref[...] + biasp_ref[...])
-    gp_ref[...] = gp
+    gp_ref[...] = gp.astype(BF16)
     collect_sums(gp, xhat, acc_ref, st_ref)
 
 
@@ -683,7 +667,7 @@
         out_shape=[
             shaped((pixels, n), BF16),
             shaped((8, n), F32),
-            shaped((pixels, n), F32),
+            shaped((pixels, n), BF16),
             stat_shape(n),
         ],
         scratch_shapes=[pltpu.VMEM((8, n), F32)],
@@ -723,7 +707,7 @@
             out_specs.append(tall(half))
             out_shape.append(shaped((pixels, half), F32))
         out_specs += [tall(cp), fixed((devices, 2, cp))]
-        out_shape += [shaped((pixels, cp), F32), stat_shape(cp)]
+        out_shape += [shaped((pixels, cp), BF16), stat_shape(cp)]
         outs = list(
             pl.pallas_call(
                 functools.partial(backward_kernel, kind, side, depth),

time: 724 us -> 712 us (0.983)
  Pallas kernels: 243 us -> 225 us
  waiting for transfers between devices: 183 us -> 191 us
    pallas_call x7, Pallas kernels: 77.7 us -> 66.7 us  [backward(): pl.pallas_call(functools.partial(backward_kernel, kind, side, depth), gri...]
  transfers between devices with their start and end apart: 37 -> 37, of which waited for: 20 -> 21; matrix products, arithmetic and copies ran while one was open for 14% -> 14% of each run, Pallas kernels for 30% -> 29%
where the time goes in v2:
time: 712 us; the launch traced here: 699 us
  Pallas kernels  225 us (32%)
  waiting for transfers between devices  191 us (27%)
  local copies, waits for them, and re-layouts  83.8 us (12%)
  starting transfers between devices  81.9 us (12%)
  blocking collectives  65.7 us (9%)
  other arithmetic  18.2 us (3%)
  between operations  17.2 us (2%)
  matrix products  15.8 us (2%)
    ppermute x9, waiting for transfers between devices, to_group(): return lax.ppermute(x, 'dp', [(i, i ^ k) for i in range(groups)])  91.1 us
    pallas_call x7, Pallas kernels, backward(): pl.pallas_call(functools.partial(backward_kernel, kind, side, depth), gri...  66.7 us
    all_to_all x5, blocking collectives, exchange(): return lax.all_to_all(st, ALL, 0, 0, tiled=True)  65.7 us
    all_to_all x11, waiting for transfers between devices, exchange(): return lax.all_to_all(st, ALL, 0, 0, tiled=True)  63.7 us
    pallas_call x7, Pallas kernels, forward(): pl.pallas_call(functools.partial(forward_kernel, kind, side), grid=(steps...  60.8 us
    all_to_all x11, starting transfers between devices, exchange(): return lax.all_to_all(st, ALL, 0, 0, tiled=True)  42.9 us
    pallas_call x4, Pallas kernels, tap_grad(): pl.pallas_call(functools.partial(weight_grad_kernel, stride, side, first)...  40.6 us
    unnamed x108, local copies, waits for them, and re-layouts  25 us
  transfers between devices with their start and end apart: 37, of which 21 were waited for; matrix products, arithmetic and copies ran while one was open for 14% of the time, Pallas kernels for 29%

profile of v2, /device:TPU:0, one launch (start us, length us, event | category | flops | bytes accessed | tf_op | source)
XLA Modules:
  0.0 698.7 jit_solution(272375124112487595)
XLA Ops:
  18.3 7.3 %all-to-all-start = ((f32[32,1,128]{2,1,0:T(1,128)}), f32[32,1,128]{2,1,0:T(1,128)S(1)}, u32[]{:S(2)}, u32[]{:S(2)}) async-start(f32[32,1,128]{2,1,0:T(1,128)} %broadcast_in_dim.53), calls=%async_computation | async-start | bytes 32768 | tf_op jit(solution)/shard_map/all_to_all | solution.py:494
  26.4 9.2 %parity_images.1 = (bf16[4,1024,512]{2,1,0:T(8,128)(2,1)}, bf16[9,1024,128]{2,1,0:T(8,128)(2,1)}, bf16[9,1024,128]{2,1,0:T(8,128)(2,1)}, bf16[9,1024,128]{2,1,0:T(8,128)(2,1)}) custom-call(s32[4,2]{1,0:T(4,128)} %copy.61.centre_ref, bf16[4,16,2,32,512]{4,3,2,1,0:T(8,128)(2,1)} %bitcast.136), custom_call_target="tpu_custom_call" | custom-call | bytes 10485760 | tf_op jit(solution)/shard_map/parity_images/pallas_call | solution.py:542
  38.2 7.9 %all-gather.10.cloned.1.call-done = bf16[8,256,512]{2,1,0:T(8,128)(2,1)} async-done(((bf16[1,256,512]{2,1,0:T(8,128)(2,1)}), bf16[8,256,512]{2,1,0:T(8,128)(2,1)}) %all-gather.10.cloned.1.call-update) | async-done | bytes 2097168 | tf_op jit(solution)/shard_map/all_gather | solution.py:447
  57.2 18.0 %collective-permute-done = bf16[8,128,512]{2,1,0:T(8,128)(2,1)} collective-permute-done((bf16[8,128,512]{2,1,0:T(8,128)(2,1)}, bf16[8,128,512]{2,1,0:T(8,128)(2,1)}, u32[]{:S(2)}, u32[]{:S(2)}) %collective-permute-start) | collective-permute-done | bytes 1048608 | tf_op jit(solution)/shard_map/ppermute | solution.py:468
  77.5 20.5 %collective-permute-done.1 = bf16[8,128,512]{2,1,0:T(8,128)(2,1)S(1)} collective-permute-done((bf16[8,128,512]{2,1,0:T(8,128)(2,1)}, bf16[8,128,512]{2,1,0:T(8,128)(2,1)S(1)}, u32[]{:S(2)}, u32[]{:S(2)}) %collective-permute-start.1) | collective-permute-done | bytes 1048608 | tf_op jit(solution)/shard_map/ppermute | solution.py:468
  103.7 16.7 %down_forward.1 = (f32[1024,1024]{1,0:T(8,128)}, f32[32,2,1024]{2,1,0:T(2,128)}) custom-call(bf16[4,1024,512]{2,1,0:T(8,128)(2,1)} %get-tuple-element.151.ph_ref.x_ref, bf16[9,1024,128]{2,1,0:T(8,128)(2,1)} %get-tuple-element.152.m_ref, f32[1024,1]{1,0:T(8,128)} %reshape.190.valid_ref, bf16[8,5,64,1024]{3,2,1,0:T(8,128)(2,1)} %bitcast.222, ...), custom_call_target="tpu_custom_call" | custom-call | flops 9663676416 | bytes 25165824 | tf_op jit(solution)/shard_map/down_forward/pallas_call | solution.py:572
  128.2 20.4 %collective-permute-done.4 = bf16[8,128,512]{2,1,0:T(8,128)(2,1)S(1)} collective-permute-done((bf16[8,128,512]{2,1,0:T(8,128)(2,1)S(1)}, bf16[8,128,512]{2,1,0:T(8,128)(2,1)S(1)}, u32[]{:S(2)}, u32[]{:S(2)}) %collective-permute-start.4) | collective-permute-done | bytes 1048608 | tf_op jit(solution)/shard_map/ppermute | solution.py:468
  155.3 9.0 %forward_plain.1 = (bf16[1024,1024]{1,0:T(8,128)(2,1)}, f32[8,1024]{1,0:T(8,128)}, f32[1024,1024]{1,0:T(8,128)}, f32[32,2,1024]{2,1,0:T(2,128)}) custom-call(f32[1024,1024]{1,0:T(8,128)} %get-tuple-element.154.z_ref.zp_ref, f32[32,2,1024]{2,1,0:T(2,128)} %copy-done.7, f32[66]{0:T(128)} %pad_maximum_fusion.3.cnt_ref, f32[1,1024]{1,0:T(1,128)} %bitcast.152, ...), custom_call_target="tpu_custom_call" | custom-call | bytes 33554432 | tf_op jit(solution)/shard_map/forward_plain/pallas_call | solution.py:624
  164.3 16.2 %all_to_all.110.s_ref = f32[32,2,1024]{2,1,0:T(2,128)} all-to-all(f32[32,2,1024]{2,1,0:T(2,128)} %get-tuple-element.163), channel_id=1, replica_groups=mesh['dp'=4,'fsdp'=8] {'dp','fsdp'}, dimensions={0} | all-to-all | bytes 524288 | tf_op jit(solution)/shard_map/all_to_all | solution.py:501
  180.5 7.6 %forward_split.1 = (bf16[1024,1024]{1,0:T(8,128)(2,1)}, f32[1024,512]{1,0:T(8,128)}, f32[8,1024]{1,0:T(8,128)}, f32[1024,512]{1,0:T(8,128)}, f32[32,2,512]{2,1,0:T(2,128)}) custom-call(f32[1024,1024]{1,0:T(8,128)} %get-tuple-element.162.z_ref.zp_ref, f32[32,2,1024]{2,1,0:T(2,128)} %all_to_all.110.s_ref, f32[66]{0:T(128)} %pad_maximum_fusion.3.cnt_ref, ...), custom_call_target="tpu_custom_call" | custom-call | bytes 33554432 | tf_op jit(solution)/shard_map/forward_split/pallas_call | solution.py:624
  188.2 7.2 %all-to-all-start.3 = ((f32[32,2,512]{2,1,0:T(2,128)}), f32[32,2,512]{2,1,0:T(2,128)S(1)}, u32[]{:S(2)}, u32[]{:S(2)}) async-start(f32[32,2,512]{2,1,0:T(2,128)} %get-tuple-element.165), calls=%async_computation.3 | async-start | bytes 262144 | tf_op jit(solution)/shard_map/all_to_all | solution.py:501
  196.6 11.6 %all-to-all-done.3.s_ref = f32[32,2,512]{2,1,0:T(2,128)S(1)} async-done(((f32[32,2,512]{2,1,0:T(2,128)}), f32[32,2,512]{2,1,0:T(2,128)S(1)}, u32[]{:S(2)}, u32[]{:S(2)}) %all-to-all-start.3) | async-done | bytes 131104 | tf_op jit(solution)/shard_map/all_to_all | solution.py:501
  208.8 11.0 %forward_three.2 = (bf16[1024,512]{1,0:T(8,128)(2,1)}, f32[8,512]{1,0:T(8,128)}, f32[1024,512]{1,0:T(8,128)}, f32[32,2,512]{2,1,0:T(2,128)}) custom-call(f32[1024,512]{1,0:T(8,128)} %get-tuple-element.164.z_ref.zp_ref, f32[32,2,512]{2,1,0:T(2,128)} %copy-done.15, f32[66]{0:T(128)} %pad_maximum_fusion.3.cnt_ref, f32[1,512]{1,0:T(1,128)} %bitcast.192, ...), custom_call_target="tpu_custom_call" | custom-call | flops 4831838208 | bytes 25165824 | tf_op jit(solution)/shard_map/forward_three/pallas_call | solution.py:624
  219.9 11.4 %all_to_all.111.s_ref = f32[32,2,512]{2,1,0:T(2,128)} all-to-all(f32[32,2,512]{2,1,0:T(2,128)} %get-tuple-element.168), channel_id=1, replica_groups=mesh['dp'=4,'fsdp'=8] {'dp','fsdp'}, dimensions={0} | all-to-all | bytes 262144 | tf_op jit(solution)/shard_map/all_to_all | solution.py:501
  231.3 6.9 forward_resid.2
  241.1 11.3 %all-to-all-done.5.s_ref = f32[32,2,512]{2,1,0:T(2,128)S(1)} async-done(((f32[32,2,512]{2,1,0:T(2,128)}), f32[32,2,512]{2,1,0:T(2,128)S(1)}, u32[]{:S(2)}, u32[]{:S(2)}) %all-to-all-start.5) | async-done | bytes 131104 | tf_op jit(solution)/shard_map/all_to_all | solution.py:501
  253.0 11.0 %forward_three.3 = (bf16[1024,512]{1,0:T(8,128)(2,1)}, f32[8,512]{1,0:T(8,128)}, f32[1024,512]{1,0:T(8,128)}, f32[32,2,512]{2,1,0:T(2,128)}) custom-call(f32[1024,512]{1,0:T(8,128)} %get-tuple-element.170.z_ref.zp_ref, f32[32,2,512]{2,1,0:T(2,128)} %copy-done.18, f32[66]{0:T(128)} %pad_maximum_fusion.3.cnt_ref, f32[1,512]{1,0:T(1,128)} %bitcast.195, ...), custom_call_target="tpu_custom_call" | custom-call | flops 4831838208 | bytes 25165824 | tf_op jit(solution)/shard_map/forward_three/pallas_call | solution.py:624
  264.0 11.4 %all_to_all.112.s_ref = f32[32,2,512]{2,1,0:T(2,128)} all-to-all(f32[32,2,512]{2,1,0:T(2,128)} %get-tuple-element.173), channel_id=1, replica_groups=mesh['dp'=4,'fsdp'=8] {'dp','fsdp'}, dimensions={0} | all-to-all | bytes 262144 | tf_op jit(solution)/shard_map/all_to_all | solution.py:501
  275.4 6.9 forward_resid.3
  284.9 8.1 %all-to-all-done.7.s_ref = f32[32,2,512]{2,1,0:T(2,128)S(1)} async-done(((f32[32,2,512]{2,1,0:T(2,128)}), f32[32,2,512]{2,1,0:T(2,128)S(1)}, u32[]{:S(2)}, u32[]{:S(2)}) %all-to-all-start.7) | async-done | bytes 131104 | tf_op jit(solution)/shard_map/all_to_all | solution.py:501
  293.7 8.4 %forward_join.1 = (bf16[1024,1024]{1,0:T(8,128)(2,1)}, f32[8,512]{1,0:T(8,128)}, f32[1024,1024]{1,0:T(8,128)}, f32[32,2,1024]{2,1,0:T(2,128)}) custom-call(f32[1024,512]{1,0:T(8,128)} %get-tuple-element.175.z_ref.zp_ref, f32[32,2,512]{2,1,0:T(2,128)} %copy-done.12, f32[66]{0:T(128)} %pad_maximum_fusion.3.cnt_ref, f32[1,512]{1,0:T(1,128)} %bitcast.164, ...), custom_call_target="tpu_custom_call" | custom-call | bytes 25165824 | tf_op jit(solution)/shard_map/forward_join/pallas_call | solution.py:624
  302.2 13.3 %all_to_all.113.s_ref = f32[32,2,1024]{2,1,0:T(2,128)} all-to-all(f32[32,2,1024]{2,1,0:T(2,128)} %get-tuple-element.179), channel_id=1, replica_groups=mesh['dp'=4,'fsdp'=8] {'dp','fsdp'}, dimensions={0} | all-to-all | bytes 524288 | tf_op jit(solution)/shard_map/all_to_all | solution.py:501
  315.5 7.4 %top.1 = (bf16[1024,1024]{1,0:T(8,128)(2,1)}, f32[8,1024]{1,0:T(8,128)}, bf16[1024,1024]{1,0:T(8,128)(2,1)}, f32[32,2,1024]{2,1,0:T(2,128)}) custom-call(f32[1024,1024]{1,0:T(8,128)} %get-tuple-element.178.z_ref, f32[32,2,1024]{2,1,0:T(2,128)} %all_to_all.113.s_ref, f32[66]{0:T(128)} %pad_maximum_fusion.3.cnt_ref, f32[1,1024]{1,0:T(1,128)} %bitcast.158, ...), custom_call_target="tpu_custom_call" | custom-call | bytes 33554432 | tf_op jit(solution)/shard_map/top/pallas_call | solution.py:655
  322.8 13.3 %all_to_all.114.s_ref = f32[32,2,1024]{2,1,0:T(2,128)} all-to-all(f32[32,2,1024]{2,1,0:T(2,128)} %get-tuple-element.183), channel_id=1, replica_groups=mesh['dp'=4,'fsdp'=8] {'dp','fsdp'}, dimensions={0} | all-to-all | bytes 524288 | tf_op jit(solution)/shard_map/all_to_all | solution.py:501
  336.1 9.5 %backward_part.1 = (bf16[1024,1024]{1,0:T(8,128)(2,1)}, f32[8,1024]{1,0:T(8,128)}, f32[1024,512]{1,0:T(8,128)}, bf16[1024,512]{1,0:T(8,128)(2,1)}, f32[32,2,512]{2,1,0:T(2,128)}) custom-call(bf16[1024,1024]{1,0:T(8,128)(2,1)} %get-tuple-element.181.g_ref, f32[1024,1024]{1,0:T(8,128)} %get-tuple-element.178.z_ref, f32[8,1024]{1,0:T(8,128)} %get-tuple-element.281.mv_ref, ...), custom_call_target="tpu_custom_call" | custom-call | bytes 25165824 | tf_op jit(solution)/shard_map/backward_part/pallas_call | solution.py:712
  348.4 5.3 convolution_convert_fusion
  357.2 7.0 %backward_keep.1 = (bf16[1024,512]{1,0:T(8,128)(2,1)}, f32[8,512]{1,0:T(8,128)}, f32[1024,512]{1,0:T(8,128)}, bf16[1024,512]{1,0:T(8,128)(2,1)}, f32[32,2,512]{2,1,0:T(2,128)}) custom-call(bf16[1024,512]{1,0:T(8,128)(2,1)} %get-tuple-element.185.g_ref, f32[1024,512]{1,0:T(8,128)} %get-tuple-element.175.z_ref.zp_ref, ...), custom_call_target="tpu_custom_call" | custom-call | bytes 25165824 | tf_op jit(solution)/shard_map/backward_keep/pallas_call | solution.py:712
  369.0 7.2 %all-to-all-done.11.s_ref = f32[32,2,512]{2,1,0:T(2,128)S(1)} async-done(((f32[32,2,512]{2,1,0:T(2,128)}), f32[32,2,512]{2,1,0:T(2,128)S(1)}, u32[]{:S(2)}, u32[]{:S(2)}) %all-to-all-start.11) | async-done | bytes 131104 | tf_op jit(solution)/shard_map/all_to_all | solution.py:501
  376.8 11.4 %backward_three.2 = (bf16[1024,512]{1,0:T(8,128)(2,1)}, f32[8,512]{1,0:T(8,128)}, bf16[1024,512]{1,0:T(8,128)(2,1)}, f32[32,2,512]{2,1,0:T(2,128)}) custom-call(bf16[1024,512]{1,0:T(8,128)(2,1)} %get-tuple-element.191.g_ref, f32[1024,512]{1,0:T(8,128)} %get-tuple-element.172.z_ref.zp_ref, f32[8,512]{1,0:T(8,128)} %get-tuple-element.279.mvp_ref.mv_ref, ...), custom_call_target="tpu_custom_call" | custom-call | flops 4831838208 | bytes 25165824 | tf_op jit(solution)/shard_map/backward_three/pallas_call | solution.py:712
  391.3 9.5 %weight_grad_1.2 = bf16[8,9,64,512]{3,2,1,0:T(8,128)(2,1)} custom-call(bf16[1024,512]{1,0:T(8,128)(2,1)} %get-tuple-element.199.x_ref, bf16[9,1024,128]{2,1,0:T(8,128)(2,1)} %get-tuple-element.166.rest_0_.m_ref, bf16[1024,512]{1,0:T(8,128)(2,1)} %get-tuple-element.200.dz_ref), custom_call_target="tpu_custom_call" | custom-call | flops 4831838208 | bytes 4194304 | tf_op jit(solution)/shard_map/weight_grad_1/pallas_call | solution.py:729
  401.4 7.3 %backward_add.1 = (bf16[1024,512]{1,0:T(8,128)(2,1)}, f32[8,512]{1,0:T(8,128)}, f32[1024,512]{1,0:T(8,128)}, bf16[1024,512]{1,0:T(8,128)(2,1)}, f32[32,2,512]{2,1,0:T(2,128)}) custom-call(bf16[1024,512]{1,0:T(8,128)(2,1)} %get-tuple-element.197.g_ref, f32[1024,512]{1,0:T(8,128)} %get-tuple-element.170.z_ref.zp_ref, ...), custom_call_target="tpu_custom_call" | custom-call | bytes 25165824 | tf_op jit(solution)/shard_map/backward_add/pallas_call | solution.py:712
  408.8 5.8 all-to-all-start.13
  416.6 8.2 %all-to-all-done.13.s_ref = f32[32,2,512]{2,1,0:T(2,128)S(1)} async-done(((f32[32,2,512]{2,1,0:T(2,128)}), f32[32,2,512]{2,1,0:T(2,128)S(1)}, u32[]{:S(2)}, u32[]{:S(2)}) %all-to-all-start.13) | async-done | bytes 131104 | tf_op jit(solution)/shard_map/all_to_all | solution.py:501
  425.4 11.5 %backward_three.3 = (bf16[1024,512]{1,0:T(8,128)(2,1)}, f32[8,512]{1,0:T(8,128)}, bf16[1024,512]{1,0:T(8,128)(2,1)}, f32[32,2,512]{2,1,0:T(2,128)}) custom-call(bf16[1024,512]{1,0:T(8,128)(2,1)} %get-tuple-element.205.g_ref, f32[1024,512]{1,0:T(8,128)} %get-tuple-element.167.z_ref.zp_ref, f32[8,512]{1,0:T(8,128)} %get-tuple-element.277.mvp_ref.mv_ref, ...), custom_call_target="tpu_custom_call" | custom-call | flops 4831838208 | bytes 25165824 | tf_op jit(solution)/shard_map/backward_three/pallas_call | solution.py:712
  439.7 9.5 %weight_grad_1.3 = bf16[8,9,64,512]{3,2,1,0:T(8,128)(2,1)} custom-call(bf16[1024,512]{1,0:T(8,128)(2,1)} %get-tuple-element.212.x_ref, bf16[9,1024,128]{2,1,0:T(8,128)(2,1)} %get-tuple-element.166.rest_0_.m_ref, bf16[1024,512]{1,0:T(8,128)(2,1)} %get-tuple-element.213.dz_ref), custom_call_target="tpu_custom_call" | custom-call | flops 4831838208 | bytes 4194304 | tf_op jit(solution)/shard_map/weight_grad_1/pallas_call | solution.py:729
  450.3 9.8 %backward_merge.1 = (bf16[1024,512]{1,0:T(8,128)(2,1)}, f32[8,512]{1,0:T(8,128)}, bf16[1024,1024]{1,0:T(8,128)(2,1)}, f32[32,2,1024]{2,1,0:T(2,128)}) custom-call(bf16[1024,512]{1,0:T(8,128)(2,1)} %get-tuple-element.216.g_ref, f32[1024,512]{1,0:T(8,128)} %get-tuple-element.164.z_ref.zp_ref, f32[8,512]{1,0:T(8,128)} %get-tuple-element.276.mvp_ref.mv_ref, ...), custom_call_target="tpu_custom_call" | custom-call | bytes 33554432 | tf_op jit(solution)/shard_map/backward_merge/pallas_call | solution.py:712
  460.1 5.4 all-to-all-start.15
  468.2 8.3 %all-to-all-done.15.s_ref = f32[32,2,1024]{2,1,0:T(2,128)S(1)} async-done(((f32[32,2,1024]{2,1,0:T(2,128)}), f32[32,2,1024]{2,1,0:T(2,128)S(1)}, u32[]{:S(2)}, u32[]{:S(2)}) %all-to-all-start.15) | async-done | bytes 262176 | tf_op jit(solution)/shard_map/all_to_all | solution.py:501
  477.3 10.3 %backward_plain.1 = (bf16[1024,1024]{1,0:T(8,128)(2,1)}, f32[8,1024]{1,0:T(8,128)}, bf16[1024,1024]{1,0:T(8,128)(2,1)}, f32[32,2,1024]{2,1,0:T(2,128)}) custom-call(bf16[1024,1024]{1,0:T(8,128)(2,1)} %get-tuple-element.221.g_ref, f32[1024,1024]{1,0:T(8,128)} %get-tuple-element.162.z_ref.zp_ref, f32[8,1024]{1,0:T(8,128)} %get-tuple-element.275.mvp_ref.mv_ref, ...), custom_call_target="tpu_custom_call" | custom-call | bytes 33554432 | tf_op jit(solution)/shard_map/backward_plain/pallas_call | solution.py:712
  502.4 5.5 all-to-all-done.16.s_ref
  508.6 5.7 down_norm.1
  514.2 11.5 %weight_grad_2.2 = bf16[8,5,64,1024]{3,2,1,0:T(8,128)(2,1)} custom-call(bf16[4,1024,512]{2,1,0:T(8,128)(2,1)} %get-tuple-element.151.ph_ref.x_ref, bf16[9,1024,128]{2,1,0:T(8,128)(2,1)} %get-tuple-element.152.m_ref, bf16[1024,1024]{1,0:T(8,128)(2,1)} %get-tuple-element.240.dz_ref), custom_call_target="tpu_custom_call" | custom-call | flops 9663676416 | bytes 8388608 | tf_op jit(solution)/shard_map/weight_grad_2/pallas_call | solution.py:729
  538.3 10.1 %weight_grad_2.3 = bf16[4,512,1024]{2,1,0:T(8,128)(2,1)} custom-call(bf16[4,1024,512]{2,1,0:T(8,128)(2,1)} %get-tuple-element.151.ph_ref.x_ref, bf16[9,1024,128]{2,1,0:T(8,128)(2,1)} %get-tuple-element.152.m_ref, bf16[1024,1024]{1,0:T(8,128)(2,1)} %get-tuple-element.240.dz_ref), custom_call_target="tpu_custom_call" | custom-call | flops 9663676416 | bytes 8388608 | tf_op jit(solution)/shard_map/weight_grad_2/pallas_call | solution.py:729
  548.3 7.5 %all-to-all-done.17 = bf16[4,352,512]{2,1,0:T(8,128)(2,1)S(1)} async-done(((bf16[4,352,512]{2,1,0:T(8,128)(2,1)}), bf16[4,352,512]{2,1,0:T(8,128)(2,1)S(1)}, u32[]{:S(2)}, u32[]{:S(2)}) %all-to-all-start.17) | async-done | bytes 1441824 | tf_op jit(solution)/shard_map/all_to_all | solution.py:745
  570.2 17.9 %input_grad.1 = bf16[4,16,2,32,512]{4,3,2,1,0:T(8,128)(2,1)} custom-call(bf16[1024,1024]{1,0:T(8,128)(2,1)} %get-tuple-element.240.dz_ref, bf16[9,1024,128]{2,1,0:T(8,128)(2,1)} %get-tuple-element.241.m_ref, bf16[8,5,64,1024]{3,2,1,0:T(8,128)(2,1)} %bitcast.223, bf16[4,8,128,512]{3,2,1,0:T(8,128)(2,1)} %bitcast_dynamic-update-slice_fusion.4.wb_ref), custom_call_target="tpu_custom_call" | custom-call | flops 9663676416 | bytes 33554432 | tf_op jit(solution)/shard_map/input_grad/pallas_call | solution.py:818
  588.1 30.1 %collective-permute-done.7 = bf16[512,1024]{1,0:T(8,128)(2,1)} collective-permute-done((bf16[512,1024]{1,0:T(8,128)(2,1)}, bf16[512,1024]{1,0:T(8,128)(2,1)}, u32[]{:S(2)}, u32[]{:S(2)}) %collective-permute-start.7) | collective-permute-done | bytes 1048608 | tf_op jit(solution)/shard_map/ppermute | solution.py:468
  646.9 5.4 all-to-all-done.19
  664.9 8.2 %all-to-all-done.20 = bf16[4,272,512]{2,1,0:T(8,128)(2,1)} async-done(((bf16[4,272,512]{2,1,0:T(8,128)(2,1)}), bf16[4,272,512]{2,1,0:T(8,128)(2,1)}, u32[]{:S(2)}, u32[]{:S(2)}) %all-to-all-start.20) | async-done | bytes 1114144 | tf_op jit(solution)/shard_map/all_to_all | solution.py:750
  (250 shorter events, 181.7 us)
Async XLA Ops:
  7.2 39.0 %all-gather.10.cloned.1.call-start = ((), (), s32[]{:S(2)}) async-start(), calls=%async_computation.28 | async-start | bytes 2359296 | tf_op jit(solution)/shard_map/all_gather | solution.py:447
  13.6 90.1 %all-gather.12.cloned.1.call-start = ((), (), s32[]{:S(2)}) async-start(), calls=%async_computation.35 | async-start | bytes 5898240 | tf_op jit(solution)/shard_map/all_gather | solution.py:447
  14.6 11.1 %copy-start.27 = (s32[4,2]{0,1:T(2,128)S(1)}, s32[4,2]{0,1:T(2,128)}, u32[]{:S(2)}) copy-start(s32[4,2]{0,1:T(2,128)} %param.16) | copy-start | bytes 100
  14.6 182.0 %all-gather.14.cloned.1.call-start = ((), (), s32[]{:S(2)}) async-start(), calls=%async_computation.36 | async-start | bytes 5308416 | tf_op jit(solution)/shard_map/all_gather | solution.py:447
  15.8 225.2 %all-gather.16.cloned.1.call-start = ((), (), s32[]{:S(2)}) async-start(), calls=%async_computation.37 | async-start | bytes 5308416 | tf_op jit(solution)/shard_map/all_gather | solution.py:447
  18.3 17.2 %all-to-all-start = ((f32[32,1,128]{2,1,0:T(1,128)}), f32[32,1,128]{2,1,0:T(1,128)S(1)}, u32[]{:S(2)}, u32[]{:S(2)}) async-start(f32[32,1,128]{2,1,0:T(1,128)} %broadcast_in_dim.53), calls=%async_computation | async-start | bytes 32768 | tf_op jit(solution)/shard_map/all_to_all | solution.py:494
  25.6 259.3 %all-gather.18.cloned.1.call-start = ((), (), s32[]{:S(2)}) async-start(), calls=%async_computation.38 | async-start | bytes 2359296 | tf_op jit(solution)/shard_map/all_gather | solution.py:490
  48.8 26.3 %collective-permute-start = (bf16[8,128,512]{2,1,0:T(8,128)(2,1)}, bf16[8,128,512]{2,1,0:T(8,128)(2,1)}, u32[]{:S(2)}, u32[]{:S(2)}) collective-permute-start(bf16[8,128,512]{2,1,0:T(8,128)(2,1)} %get-tuple-element.289), channel_id=1, source_target_pairs={{0,8},{8,0},{16,24},{24,16},{1,9},{9,1},{17,25},{25,17},{2,10},{10... | collective-permute-start | bytes 3145736 | tf_op jit(solution)/shard_map/ppermute | solution.py:468
  50.3 47.7 %collective-permute-start.1 = (bf16[8,128,512]{2,1,0:T(8,128)(2,1)}, bf16[8,128,512]{2,1,0:T(8,128)(2,1)S(1)}, u32[]{:S(2)}, u32[]{:S(2)}) collective-permute-start(bf16[8,128,512]{2,1,0:T(8,128)(2,1)} %get-tuple-element.289), channel_id=1, source_target_pairs={{0,16},{8,24},{16,0},{24,8},{1,17},{9,25},{17,1},{25,9},{2,18},{10... | collective-permute-start | bytes 3145736 | tf_op jit(solution)/shard_map/ppermute | solution.py:468
  51.8 47.3 %collective-permute-start.2 = (bf16[8,128,512]{2,1,0:T(8,128)(2,1)}, bf16[8,128,512]{2,1,0:T(8,128)(2,1)S(1)}, u32[]{:S(2)}, u32[]{:S(2)}) collective-permute-start(bf16[8,128,512]{2,1,0:T(8,128)(2,1)} %get-tuple-element.289), channel_id=1, source_target_pairs={{0,24},{8,16},{16,8},{24,0},{1,25},{9,17},{17,9},{25,1},{2,26},{10... | collective-permute-start | bytes 3145736 | tf_op jit(solution)/shard_map/ppermute | solution.py:468
  100.2 28.0 %collective-permute-start.3 = (bf16[8,128,512]{2,1,0:T(8,128)(2,1)S(1)}, bf16[8,128,512]{2,1,0:T(8,128)(2,1)S(1)}, u32[]{:S(2)}, u32[]{:S(2)}) collective-permute-start(bf16[8,128,512]{2,1,0:T(8,128)(2,1)S(1)} %get-tuple-element.155), channel_id=1, source_target_pairs={{0,8},{8,0},{16,24},{24,16},{1,9},{9,1},{17,25},{25,17},{2,10},{10... | collective-permute-start | bytes 3145736 | tf_op jit(solution)/shard_map/ppermute | solution.py:468
  100.3 48.3 %collective-permute-start.4 = (bf16[8,128,512]{2,1,0:T(8,128)(2,1)S(1)}, bf16[8,128,512]{2,1,0:T(8,128)(2,1)S(1)}, u32[]{:S(2)}, u32[]{:S(2)}) collective-permute-start(bf16[8,128,512]{2,1,0:T(8,128)(2,1)S(1)} %get-tuple-element.155), channel_id=1, source_target_pairs={{0,16},{8,24},{16,0},{24,8},{1,17},{9,25},{17,1},{25,9},{2,18},{10... | collective-permute-start | bytes 3145736 | tf_op jit(solution)/shard_map/ppermute | solution.py:468
  102.2 48.4 %collective-permute-start.5 = (bf16[8,128,512]{2,1,0:T(8,128)(2,1)S(1)}, bf16[8,128,512]{2,1,0:T(8,128)(2,1)}, u32[]{:S(2)}, u32[]{:S(2)}) collective-permute-start(bf16[8,128,512]{2,1,0:T(8,128)(2,1)S(1)} %get-tuple-element.155), channel_id=1, source_target_pairs={{0,24},{8,16},{16,8},{24,0},{1,25},{9,17},{17,9},{25,1},{2,26},{10... | collective-permute-start | bytes 3145736 | tf_op jit(solution)/shard_map/ppermute | solution.py:468
  103.7 19.6 %copy-start.22 = (f32[5632]{0:T(1024)S(1)}, f32[5632]{0:T(1024)}, u32[]{:S(2)}) copy-start(f32[5632]{0:T(1024)} %param.24) | copy-start | bytes 67588
  103.7 20.2 %copy-start.23 = (f32[5632]{0:T(1024)S(1)}, f32[5632]{0:T(1024)}, u32[]{:S(2)}) copy-start(f32[5632]{0:T(1024)} %param.25) | copy-start | bytes 67588
  120.4 30.4 %all-to-all-start.1 = ((f32[32,2,1024]{2,1,0:T(2,128)}), f32[32,2,1024]{2,1,0:T(2,128)S(1)}, u32[]{:S(2)}, u32[]{:S(2)}) async-start(f32[32,2,1024]{2,1,0:T(2,128)} %get-tuple-element.156), calls=%async_computation.1 | async-start | bytes 524288 | tf_op jit(solution)/shard_map/all_to_all | solution.py:501
  188.2 20.0 %all-to-all-start.3 = ((f32[32,2,512]{2,1,0:T(2,128)}), f32[32,2,512]{2,1,0:T(2,128)S(1)}, u32[]{:S(2)}, u32[]{:S(2)}) async-start(f32[32,2,512]{2,1,0:T(2,128)} %get-tuple-element.165), calls=%async_computation.3 | async-start | bytes 262144 | tf_op jit(solution)/shard_map/all_to_all | solution.py:501
  238.2 14.2 %all-to-all-start.5 = ((f32[32,2,512]{2,1,0:T(2,128)}), f32[32,2,512]{2,1,0:T(2,128)S(1)}, u32[]{:S(2)}, u32[]{:S(2)}) async-start(f32[32,2,512]{2,1,0:T(2,128)} %get-tuple-element.171), calls=%async_computation.5 | async-start | bytes 262144 | tf_op jit(solution)/shard_map/all_to_all | solution.py:501
  282.3 10.8 %all-to-all-start.7 = ((f32[32,2,512]{2,1,0:T(2,128)}), f32[32,2,512]{2,1,0:T(2,128)S(1)}, u32[]{:S(2)}, u32[]{:S(2)}) async-start(f32[32,2,512]{2,1,0:T(2,128)} %get-tuple-element.176), calls=%async_computation.7 | async-start | bytes 262144 | tf_op jit(solution)/shard_map/all_to_all | solution.py:501
  336.1 12.3 %copy-start.31 = (bf16[1024,1024]{1,0:T(8,128)(2,1)S(1)}, bf16[1024,1024]{1,0:T(8,128)(2,1)}, u32[]{:S(2)}) copy-start(bf16[1024,1024]{1,0:T(8,128)(2,1)} %get-tuple-element.187) | copy-start | bytes 6291460
  345.6 10.9 %all-to-all-start.10 = ((f32[32,2,512]{2,1,0:T(2,128)}), f32[32,2,512]{2,1,0:T(2,128)S(1)}, u32[]{:S(2)}, u32[]{:S(2)}) async-start(f32[32,2,512]{2,1,0:T(2,128)} %get-tuple-element.186), calls=%async_computation.10 | async-start | bytes 262144 | tf_op jit(solution)/shard_map/all_to_all | solution.py:501
  348.4 52.4 %reduce-scatter.7.cloned.1.call-start = ((), (), s32[]{:S(2)}) async-start(), calls=%async_computation.29 | async-start | bytes 2359296 | tf_op jit(solution)/shard_map/reduce_scatter | solution.py:741
  357.2 9.8 %copy-start.34 = (bf16[1024,512]{1,0:T(8,128)(2,1)S(1)}, bf16[1024,512]{1,0:T(8,128)(2,1)}, u32[]{:S(2)}) copy-start(bf16[1024,512]{1,0:T(8,128)(2,1)} %get-tuple-element.193) | copy-start | bytes 3145732
  364.2 12.0 %all-to-all-start.11 = ((f32[32,2,512]{2,1,0:T(2,128)}), f32[32,2,512]{2,1,0:T(2,128)S(1)}, u32[]{:S(2)}, u32[]{:S(2)}) async-start(f32[32,2,512]{2,1,0:T(2,128)} %get-tuple-element.192), calls=%async_computation.11 | async-start | bytes 262144 | tf_op jit(solution)/shard_map/all_to_all | solution.py:501
  388.2 12.6 %all-to-all-start.12 = ((f32[32,2,512]{2,1,0:T(2,128)}), f32[32,2,512]{2,1,0:T(2,128)S(1)}, u32[]{:S(2)}, u32[]{:S(2)}) async-start(f32[32,2,512]{2,1,0:T(2,128)} %get-tuple-element.198), calls=%async_computation.12 | async-start | bytes 262144 | tf_op jit(solution)/shard_map/all_to_all | solution.py:501
  391.2 85.3 %reduce-scatter.11.cloned.1.call-start = ((), (), s32[]{:S(2)}) async-start(), calls=%async_computation.31 | async-start | bytes 5308416 | tf_op jit(solution)/shard_map/reduce_scatter | solution.py:741
  401.4 13.1 %copy-start.33 = (bf16[1024,512]{1,0:T(8,128)(2,1)S(1)}, bf16[1024,512]{1,0:T(8,128)(2,1)}, u32[]{:S(2)}) copy-start(bf16[1024,512]{1,0:T(8,128)(2,1)} %get-tuple-element.207) | copy-start | bytes 3145732
  408.8 15.9 %all-to-all-start.13 = ((f32[32,2,512]{2,1,0:T(2,128)}), f32[32,2,512]{2,1,0:T(2,128)S(1)}, u32[]{:S(2)}, u32[]{:S(2)}) async-start(f32[32,2,512]{2,1,0:T(2,128)} %get-tuple-element.206), calls=%async_computation.14 | async-start | bytes 262144 | tf_op jit(solution)/shard_map/all_to_all | solution.py:501
  436.9 12.8 %all-to-all-start.14 = ((f32[32,2,512]{2,1,0:T(2,128)}), f32[32,2,512]{2,1,0:T(2,128)S(1)}, u32[]{:S(2)}, u32[]{:S(2)}) async-start(f32[32,2,512]{2,1,0:T(2,128)} %get-tuple-element.211), calls=%async_computation.15 | async-start | bytes 262144 | tf_op jit(solution)/shard_map/all_to_all | solution.py:501
  439.5 92.0 %reduce-scatter.9.cloned.1.call-start = ((), (), s32[]{:S(2)}) async-start(), calls=%async_computation.30 | async-start | bytes 5308416 | tf_op jit(solution)/shard_map/reduce_scatter | solution.py:741
  450.3 15.2 %copy-start.1 = (bf16[1024,1024]{1,0:T(8,128)(2,1)S(1)}, bf16[1024,1024]{1,0:T(8,128)(2,1)}, u32[]{:S(2)}) copy-start(bf16[1024,1024]{1,0:T(8,128)(2,1)} %get-tuple-element.177.rest_0_) | copy-start | bytes 6291460
  460.1 16.5 %all-to-all-start.15 = ((f32[32,2,1024]{2,1,0:T(2,128)}), f32[32,2,1024]{2,1,0:T(2,128)S(1)}, u32[]{:S(2)}, u32[]{:S(2)}) async-start(f32[32,2,1024]{2,1,0:T(2,128)} %get-tuple-element.222), calls=%async_computation.18 | async-start | bytes 524288 | tf_op jit(solution)/shard_map/all_to_all | solution.py:501
  477.3 15.4 %copy-start.30 = (bf16[1024,1024]{1,0:T(8,128)(2,1)S(1)}, bf16[1024,1024]{1,0:T(8,128)(2,1)}, u32[]{:S(2)}) copy-start(bf16[1024,1024]{1,0:T(8,128)(2,1)} %get-tuple-element.228) | copy-start | bytes 6291460
  487.5 20.3 %all-to-all-start.16 = ((f32[32,2,1024]{2,1,0:T(2,128)}), f32[32,2,1024]{2,1,0:T(2,128)S(1)}, u32[]{:S(2)}, u32[]{:S(2)}) async-start(f32[32,2,1024]{2,1,0:T(2,128)} %get-tuple-element.227), calls=%async_computation.19 | async-start | bytes 524288 | tf_op jit(solution)/shard_map/all_to_all | solution.py:501
  492.6 134.9 %reduce-scatter.13.cloned.1.call-start = ((), (), s32[]{:S(2)}) async-start(), calls=%async_computation.32 | async-start | bytes 4128768 | tf_op jit(solution)/shard_map/reduce_scatter | solution.py:741
  507.9 123.8 %reduce-scatter.15.cloned.1.call-start = ((), (), s32[]{:S(2)}) async-start(), calls=%async_computation.33 | async-start | bytes 5898240 | tf_op jit(solution)/shard_map/reduce_scatter | solution.py:741
  533.9 21.9 %all-to-all-start.17 = ((bf16[4,352,512]{2,1,0:T(8,128)(2,1)}), bf16[4,352,512]{2,1,0:T(8,128)(2,1)S(1)}, u32[]{:S(2)}, u32[]{:S(2)}) async-start(bf16[4,352,512]{2,1,0:T(8,128)(2,1)} %bitcast.51), calls=%async_computation.20 | async-start | bytes 2883584 | tf_op jit(solution)/shard_map/all_to_all | solution.py:745
  556.2 7.5 %copy-start.21 = (f32[5632]{0:T(1024)S(1)}, f32[5632]{0:T(1024)}, u32[]{:S(2)}) copy-start(f32[5632]{0:T(1024)} %param.27) | copy-start | bytes 67588
  560.2 27.9 %collective-permute-start.6 = (bf16[512,1024]{1,0:T(8,128)(2,1)}, bf16[512,1024]{1,0:T(8,128)(2,1)}, u32[]{:S(2)}, u32[]{:S(2)}) collective-permute-start(bf16[512,1024]{1,0:T(8,128)(2,1)} %get-tuple-element.287), channel_id=1, source_target_pairs={{0,8},{8,0},{16,24},{24,16},{1,9},{9,1},{17,25},{25,17},{2,10},{10... | collective-permute-start | bytes 3145736 | tf_op jit(solution)/shard_map/ppermute | solution.py:468
  561.6 56.5 %collective-permute-start.7 = (bf16[512,1024]{1,0:T(8,128)(2,1)}, bf16[512,1024]{1,0:T(8,128)(2,1)}, u32[]{:S(2)}, u32[]{:S(2)}) collective-permute-start(bf16[512,1024]{1,0:T(8,128)(2,1)} %get-tuple-element.286), channel_id=1, source_target_pairs={{0,16},{8,24},{16,0},{24,8},{1,17},{9,25},{17,1},{25,9},{2,18},{10... | collective-permute-start | bytes 3145736 | tf_op jit(solution)/shard_map/ppermute | solution.py:468
  562.2 56.0 %collective-permute-start.8 = (bf16[512,1024]{1,0:T(8,128)(2,1)S(1)}, bf16[512,1024]{1,0:T(8,128)(2,1)}, u32[]{:S(2)}, u32[]{:S(2)}) collective-permute-start(bf16[512,1024]{1,0:T(8,128)(2,1)S(1)} %get-tuple-element.285), channel_id=1, source_target_pairs={{0,24},{8,16},{16,8},{24,0},{1,25},{9,17},{17,9},{25,1},{2,26},{10... | collective-permute-start | bytes 3145736 | tf_op jit(solution)/shard_map/ppermute | solution.py:468
  565.5 60.2 %all-to-all-start.18 = ((bf16[4,352,512]{2,1,0:T(8,128)(2,1)}), bf16[4,352,512]{2,1,0:T(8,128)(2,1)}, u32[]{:S(2)}, u32[]{:S(2)}) async-start(bf16[4,352,512]{2,1,0:T(8,128)(2,1)} %broadcast_in_dim.62), calls=%async_computation.23 | async-start | bytes 2883584 | tf_op jit(solution)/shard_map/all_to_all | solution.py:750
  569.9 107.4 %reduce-scatter.17.cloned.1.call-start = ((), (), s32[]{:S(2)}) async-start(), calls=%async_computation.34 | async-start | bytes 1179648 | tf_op jit(solution)/shard_map/reduce_scatter | solution.py:741
  635.1 17.2 %all-to-all-start.19 = ((bf16[4,272,512]{2,1,0:T(8,128)(2,1)}), bf16[4,272,512]{2,1,0:T(8,128)(2,1)}, u32[]{:S(2)}, u32[]{:S(2)}) async-start(bf16[4,272,512]{2,1,0:T(8,128)(2,1)} %pad_maximum_fusion.1), calls=%async_computation.24 | async-start | bytes 2228224 | tf_op jit(solution)/shard_map/all_to_all | solution.py:745
  653.9 6.7 copy-start.24
  654.9 18.2 %all-to-all-start.20 = ((bf16[4,272,512]{2,1,0:T(8,128)(2,1)}), bf16[4,272,512]{2,1,0:T(8,128)(2,1)}, u32[]{:S(2)}, u32[]{:S(2)}) async-start(bf16[4,272,512]{2,1,0:T(8,128)(2,1)} %broadcast_in_dim.63), calls=%async_computation.25 | async-start | bytes 2228224 | tf_op jit(solution)/shard_map/all_to_all | solution.py:750
  677.2 9.1 %copy-start.2 = (f32[3,64,1,512]{3,2,1,0:T(1,128)S(1)}, f32[3,64,1,512]{3,2,1,0:T(1,128)}, u32[]{:S(2)}) copy-start(f32[3,64,1,512]{3,2,1,0:T(1,128)} %reshape.181) | copy-start | bytes 1179652
  679.1 11.0 %all-to-all-start.21 = ((bf16[4,64,1024]{2,1,0:T(8,128)(2,1)}), bf16[4,64,1024]{2,1,0:T(8,128)(2,1)S(1)}, u32[]{:S(2)}, u32[]{:S(2)}) async-start(bf16[4,64,1024]{2,1,0:T(8,128)(2,1)} %broadcast_in_dim.64), calls=%async_computation.27 | async-start | bytes 1048576 | tf_op jit(solution)/shard_map/all_to_all | solution.py:750
  (24 other events, 55.3 us)
Sparse Core Ops, SparseCore 0:
  13.8 32.3 all-gather.9
  47.8 55.1 all-gather.11
  104.6 55.5 all-gather.13
  161.8 57.5 all-gather.15
  220.8 31.3 all-gather.17
  356.7 36.0 reduce-scatter.6
  400.9 60.2 reduce-scatter.10
  463.5 60.3 reduce-scatter.8
  526.3 45.0 reduce-scatter.12
  573.5 58.2 reduce-scatter.14
  634.0 31.0 reduce-scatter.16

commit v3 on v2

--- a/solution.py
+++ b/solution.py
@@ -764,9 +764,16 @@
     for b in reversed(range(blocks)):
         layer = 3 + 2 * b
         g, st_back, _ = backward(layer, "three", g, gathered, (mask_mid,), (mask_spec,))
-        own = tap_grad(1, inputs[layer], mask_mid, dz[layer], full_spread[b].shape)
-        due = (own_unite,) if b == blocks - 1 else ()
-        gathered, own = beside(st_back, own, *due)
+        if b > 0:
+            own = tap_grad(1, inputs[layer], mask_mid, dz[layer], full_spread[b].shape)
+            due = (own_unite,) if b == blocks - 1 else ()
+            gathered, own = beside(st_back, own, *due)
+        else:
+            own_shape = (fsdp, taps, *full_spread[b].shape[2:])
+            own = tap_grad(1, inputs[layer], mask_mid, dz[layer], own_shape)
+            tail = tap_grad(1, inputs[layer], mask_mid, dz[layer], (groups, half, half), taps)
+            gathered, own, tail = lax.optimization_barrier((exchange(st_back), own, tail))
+            tail_held, tail_got = deal(tail)
         own_spread[b] = scatter(own)
         layer = 2 + 2 * b
         if b > 0:
@@ -785,7 +792,7 @@
     g, st_back, _ = backward(1, "plain", g, gathered)
     split_grads = [flat_grad(inputs[1], dz[1][:, k : k + half]) for k in range(0, width, half)]
     late = [w.reshape(fsdp, -1, half) for w in (*split_grads, *narrow_grads)]
-    gathered, grad_late = beside(st_back, jnp.concatenate(late, axis=1))
+    gathered, grad_late = beside(st_back, jnp.concatenate(late, axis=1), *tail_got)
     own_late = scatter(grad_late)[0]
     dz[0], totals[0] = pl.pallas_call(
         last_norm_kernel,
@@ -831,13 +838,17 @@
         name="input_grad",
     )(dz_low, mask_back, full_down, down_rest).reshape(segment_input.shape)
 
-    *received, input_grad = lax.optimization_barrier((*rest_got, input_grad))
+    first_sums = give_back(first_part).reshape(-1, half)
+    *received, input_grad, first_sums = lax.optimization_barrier(
+        (*rest_got, input_grad, first_sums)
+    )
     rest_sum = add_parts(rest_held[0], received)
-    own_rest = scatter(rest_sum)
+    tail_sum = add_parts(tail_held[0], tail_got)
+    summed = [rest_sum[:, k : k + half] for k in range(0, width, half)] + [tail_sum]
+    summed = [part.reshape(fsdp, -1, half) for part in summed]
+    own_summed = scatter(jnp.concatenate(summed, axis=1))[0]
     *totals, rest_sum = lax.optimization_barrier((*totals, rest_sum))
     *moment, rest_sum = lax.optimization_barrier((*moment, rest_sum))
-    first_part = lax.optimization_barrier((first_part, rest_sum))[0]
-    first_sums = give_back(first_part).reshape(-1, half)
     own_late, own_direct, first_sums = lax.optimization_barrier((own_late, own_direct, first_sums))
     second = [own_late, own_direct.reshape(-1, width)]
     cut = [o.reshape(groups, -1, o.shape[-1]) for o in second]
@@ -845,20 +856,26 @@
     second_part = sum_own_part(jnp.concatenate(cut, axis=1).reshape(-1, half))
     late_rows = own_late.shape[0]
     late_own = late_rows // groups
-    sums = give_back(second_part)
-    grad_direct = sums[:, late_own:].reshape(own_direct.shape[1:])
+    second_rows = second_part.shape[0]
+    sums = give_back(jnp.concatenate([second_part, own_summed], axis=0))
+    ends = sums[:, second_rows:]
+    grad_direct = sums[:, late_own:second_rows].reshape(own_direct.shape[1:])
     late_sums = sums[:, :late_own].reshape(-1, half)
-    spread_rows = first_packed[0].shape[0]
     split_parts = late_sums[:split_rows].reshape(-1, split_rows // 2, half)
     grad_split = jnp.concatenate([split_parts[0], split_parts[1]], axis=1)
     narrow = late_sums[split_rows:].reshape(blocks + 1, narrow_rows, 1, half)
-    grad_spread = first_sums[: blocks * spread_rows]
-    grad_spread = grad_spread.reshape(blocks, 9, narrow_rows, half).transpose(0, 2, 1, 3)
-    grad_unite = first_sums[blocks * spread_rows :].reshape(own_unite.shape)[:, None]
-    grad_split, narrow, grad_spread, grad_unite, grad_direct, own_rest = lax.optimization_barrier(
-        (grad_split, narrow, grad_spread, grad_unite, grad_direct, own_rest)
+    grad_rest = jnp.concatenate(
+        [ends[:, k : k + tap_rows // 2] for k in range(0, tap_rows, tap_rows // 2)], axis=2
     )
-    grad_down = jnp.concatenate([grad_direct, give_back(own_rest)], axis=0).transpose(1, 0, 2)
+    grad_down = jnp.concatenate([grad_direct, grad_rest], axis=0).transpose(1, 0, 2)
+    at, spread = 0, []
+    for b in range(blocks):
+        size = first_packed[b].shape[0]
+        spread.append(first_sums[at : at + size].reshape(-1, narrow_rows, half))
+        at += size
+    spread[0] = jnp.concatenate([spread[0], ends[:, tap_rows:]], axis=0)
+    grad_spread = jnp.stack(spread).transpose(0, 2, 1, 3)
+    grad_unite = first_sums[at:].reshape(own_unite.shape)[:, None]
 
     means = jnp.concatenate([m[0] for m in moment])
     variances = jnp.concatenate([m[1] for m in moment])

time: 712 us -> 718 us (level)
  waiting for transfers between devices: 191 us -> 207 us
  local copies, waits for them, and re-layouts: 83.8 us -> 71.7 us
    all_to_all x3 -> x2, waiting for transfers between devices: 10.5 us -> 49.9 us  [give_back(): return lax.all_to_all(sent, 'dp', 0, 0, tiled=True).astype(F32)]
    ppermute x9 -> x12, waiting for transfers between devices: 91.1 us -> 61 us  [to_group(): return lax.ppermute(x, 'dp', [(i, i ^ k) for i in range(groups)])]
    unnamed x108 -> x110, local copies, waits for them, and re-layouts: 25 us -> 16.2 us
    reduce_scatter x6, waiting for transfers between devices: 4.25 us -> 11.9 us  [scatter(): return lax.psum_scatter(grad, 'fsdp', scatter_dimension=0, tiled=True)]
    pallas_call x4 -> x5, Pallas kernels: 40.6 us -> 43.9 us  [tap_grad(): pl.pallas_call(functools.partial(weight_grad_kernel, stride, side, first)...]
  transfers between devices with their start and end apart: 37 -> 39, of which waited for: 21 -> 19; matrix products, arithmetic and copies ran while one was open for 14% -> 12% of each run, Pallas kernels for 29% -> 29%
where the time goes in v3:
time: 718 us; the launch traced here: 706 us
  Pallas kernels  228 us (32%)
  waiting for transfers between devices  207 us (29%)
  starting transfers between devices  76.8 us (11%)
  local copies, waits for them, and re-layouts  71.7 us (10%)
  blocking collectives  66.6 us (9%)
  other arithmetic  22.5 us (3%)
  between operations  17.2 us (2%)
  matrix products  17 us (2%)
    all_to_all x5, blocking collectives, exchange(): return lax.all_to_all(st, ALL, 0, 0, tiled=True)  66.6 us
    pallas_call x7, Pallas kernels, backward(): pl.pallas_call(functools.partial(backward_kernel, kind, side, depth), gri...  66.4 us
    ppermute x12, waiting for transfers between devices, to_group(): return lax.ppermute(x, 'dp', [(i, i ^ k) for i in range(groups)])  61 us
    pallas_call x7, Pallas kernels, forward(): pl.pallas_call(functools.partial(forward_kernel, kind, side), grid=(steps...  60.8 us
    all_to_all x11, waiting for transfers between devices, exchange(): return lax.all_to_all(st, ALL, 0, 0, tiled=True)  59.6 us
    all_to_all x2, waiting for transfers between devices, give_back(): return lax.all_to_all(sent, 'dp', 0, 0, tiled=True).astype(F32)  49.9 us
    pallas_call x5, Pallas kernels, tap_grad(): pl.pallas_call(functools.partial(weight_grad_kernel, stride, side, first)...  43.9 us
    all_to_all x11, starting transfers between devices, exchange(): return lax.all_to_all(st, ALL, 0, 0, tiled=True)  40 us
  transfers between devices with their start and end apart: 39, of which 19 were waited for; matrix products, arithmetic and copies ran while one was open for 12% of the time, Pallas kernels for 29%

profile of v3, /device:TPU:0, one launch (start us, length us, event | category | flops | bytes accessed | tf_op | source)
XLA Modules:
  0.0 706.2 jit_solution(1751061726053346005)
XLA Ops:
  18.3 7.3 %all-to-all-start = ((f32[32,1,128]{2,1,0:T(1,128)}), f32[32,1,128]{2,1,0:T(1,128)S(1)}, u32[]{:S(2)}, u32[]{:S(2)}) async-start(f32[32,1,128]{2,1,0:T(1,128)} %broadcast_in_dim.47), calls=%async_computation | async-start | bytes 32768 | tf_op jit(solution)/shard_map/all_to_all | solution.py:494
  26.3 9.1 %parity_images.1 = (bf16[4,1024,512]{2,1,0:T(8,128)(2,1)}, bf16[9,1024,128]{2,1,0:T(8,128)(2,1)}, bf16[9,1024,128]{2,1,0:T(8,128)(2,1)}, bf16[9,1024,128]{2,1,0:T(8,128)(2,1)}) custom-call(s32[4,2]{1,0:T(4,128)} %copy.61.centre_ref, bf16[4,16,2,32,512]{4,3,2,1,0:T(8,128)(2,1)} %bitcast.152), custom_call_target="tpu_custom_call" | custom-call | bytes 10485760 | tf_op jit(solution)/shard_map/parity_images/pallas_call | solution.py:542
  38.2 8.0 %all-gather.10.cloned.1.call-done = bf16[8,256,512]{2,1,0:T(8,128)(2,1)} async-done(((bf16[1,256,512]{2,1,0:T(8,128)(2,1)}), bf16[8,256,512]{2,1,0:T(8,128)(2,1)}) %all-gather.10.cloned.1.call-update) | async-done | bytes 2097168 | tf_op jit(solution)/shard_map/all_gather | solution.py:447
  57.2 17.9 %collective-permute-done = bf16[8,128,512]{2,1,0:T(8,128)(2,1)} collective-permute-done((bf16[8,128,512]{2,1,0:T(8,128)(2,1)}, bf16[8,128,512]{2,1,0:T(8,128)(2,1)}, u32[]{:S(2)}, u32[]{:S(2)}) %collective-permute-start) | collective-permute-done | bytes 1048608 | tf_op jit(solution)/shard_map/ppermute | solution.py:468
  77.5 20.5 %collective-permute-done.1 = bf16[8,128,512]{2,1,0:T(8,128)(2,1)S(1)} collective-permute-done((bf16[8,128,512]{2,1,0:T(8,128)(2,1)}, bf16[8,128,512]{2,1,0:T(8,128)(2,1)S(1)}, u32[]{:S(2)}, u32[]{:S(2)}) %collective-permute-start.1) | collective-permute-done | bytes 1048608 | tf_op jit(solution)/shard_map/ppermute | solution.py:468
  103.7 16.7 %down_forward.1 = (f32[1024,1024]{1,0:T(8,128)}, f32[32,2,1024]{2,1,0:T(2,128)}) custom-call(bf16[4,1024,512]{2,1,0:T(8,128)(2,1)} %get-tuple-element.147.ph_ref.x_ref, bf16[9,1024,128]{2,1,0:T(8,128)(2,1)} %get-tuple-element.148.m_ref, f32[1024,1]{1,0:T(8,128)} %reshape.204.valid_ref, bf16[8,5,64,1024]{3,2,1,0:T(8,128)(2,1)} %bitcast.241, ...), custom_call_target="tpu_custom_call" | custom-call | flops 9663676416 | bytes 25165824 | tf_op jit(solution)/shard_map/down_forward/pallas_call | solution.py:572
  128.2 20.4 %collective-permute-done.4 = bf16[8,128,512]{2,1,0:T(8,128)(2,1)S(1)} collective-permute-done((bf16[8,128,512]{2,1,0:T(8,128)(2,1)S(1)}, bf16[8,128,512]{2,1,0:T(8,128)(2,1)S(1)}, u32[]{:S(2)}, u32[]{:S(2)}) %collective-permute-start.4) | collective-permute-done | bytes 1048608 | tf_op jit(solution)/shard_map/ppermute | solution.py:468
  155.5 8.9 %forward_plain.1 = (bf16[1024,1024]{1,0:T(8,128)(2,1)}, f32[8,1024]{1,0:T(8,128)}, f32[1024,1024]{1,0:T(8,128)}, f32[32,2,1024]{2,1,0:T(2,128)}) custom-call(f32[1024,1024]{1,0:T(8,128)} %get-tuple-element.150.z_ref.zp_ref, f32[32,2,1024]{2,1,0:T(2,128)} %copy-done.7, f32[66]{0:T(128)} %pad_maximum_fusion.5.cnt_ref, f32[1,1024]{1,0:T(1,128)} %bitcast.171, ...), custom_call_target="tpu_custom_call" | custom-call | bytes 33554432 | tf_op jit(solution)/shard_map/forward_plain/pallas_call | solution.py:624
  164.4 17.1 %all_to_all.105.s_ref = f32[32,2,1024]{2,1,0:T(2,128)} all-to-all(f32[32,2,1024]{2,1,0:T(2,128)} %get-tuple-element.159), channel_id=1, replica_groups=mesh['dp'=4,'fsdp'=8] {'dp','fsdp'}, dimensions={0} | all-to-all | bytes 524288 | tf_op jit(solution)/shard_map/all_to_all | solution.py:501
  181.5 7.6 %forward_split.1 = (bf16[1024,1024]{1,0:T(8,128)(2,1)}, f32[1024,512]{1,0:T(8,128)}, f32[8,1024]{1,0:T(8,128)}, f32[1024,512]{1,0:T(8,128)}, f32[32,2,512]{2,1,0:T(2,128)}) custom-call(f32[1024,1024]{1,0:T(8,128)} %get-tuple-element.158.z_ref.zp_ref, f32[32,2,1024]{2,1,0:T(2,128)} %all_to_all.105.s_ref, f32[66]{0:T(128)} %pad_maximum_fusion.5.cnt_ref, ...), custom_call_target="tpu_custom_call" | custom-call | bytes 33554432 | tf_op jit(solution)/shard_map/forward_split/pallas_call | solution.py:624
  189.2 6.4 all-to-all-start.3
  196.8 11.5 %all-to-all-done.3.s_ref = f32[32,2,512]{2,1,0:T(2,128)S(1)} async-done(((f32[32,2,512]{2,1,0:T(2,128)}), f32[32,2,512]{2,1,0:T(2,128)S(1)}, u32[]{:S(2)}, u32[]{:S(2)}) %all-to-all-start.3) | async-done | bytes 131104 | tf_op jit(solution)/shard_map/all_to_all | solution.py:501
  209.0 11.0 %forward_three.2 = (bf16[1024,512]{1,0:T(8,128)(2,1)}, f32[8,512]{1,0:T(8,128)}, f32[1024,512]{1,0:T(8,128)}, f32[32,2,512]{2,1,0:T(2,128)}) custom-call(f32[1024,512]{1,0:T(8,128)} %get-tuple-element.160.z_ref.zp_ref, f32[32,2,512]{2,1,0:T(2,128)} %copy-done.18, f32[66]{0:T(128)} %pad_maximum_fusion.5.cnt_ref, f32[1,512]{1,0:T(1,128)} %bitcast.211, ...), custom_call_target="tpu_custom_call" | custom-call | flops 4831838208 | bytes 25165824 | tf_op jit(solution)/shard_map/forward_three/pallas_call | solution.py:624
  220.0 11.4 %all_to_all.106.s_ref = f32[32,2,512]{2,1,0:T(2,128)} all-to-all(f32[32,2,512]{2,1,0:T(2,128)} %get-tuple-element.164), channel_id=1, replica_groups=mesh['dp'=4,'fsdp'=8] {'dp','fsdp'}, dimensions={0} | all-to-all | bytes 262144 | tf_op jit(solution)/shard_map/all_to_all | solution.py:501
  231.4 6.9 forward_resid.2
  241.2 11.3 %all-to-all-done.5.s_ref = f32[32,2,512]{2,1,0:T(2,128)S(1)} async-done(((f32[32,2,512]{2,1,0:T(2,128)}), f32[32,2,512]{2,1,0:T(2,128)S(1)}, u32[]{:S(2)}, u32[]{:S(2)}) %all-to-all-start.5) | async-done | bytes 131104 | tf_op jit(solution)/shard_map/all_to_all | solution.py:501
  253.1 11.0 %forward_three.3 = (bf16[1024,512]{1,0:T(8,128)(2,1)}, f32[8,512]{1,0:T(8,128)}, f32[1024,512]{1,0:T(8,128)}, f32[32,2,512]{2,1,0:T(2,128)}) custom-call(f32[1024,512]{1,0:T(8,128)} %get-tuple-element.166.z_ref.zp_ref, f32[32,2,512]{2,1,0:T(2,128)} %copy-done.21, f32[66]{0:T(128)} %pad_maximum_fusion.5.cnt_ref, f32[1,512]{1,0:T(1,128)} %bitcast.214, ...), custom_call_target="tpu_custom_call" | custom-call | flops 4831838208 | bytes 25165824 | tf_op jit(solution)/shard_map/forward_three/pallas_call | solution.py:624
  264.1 11.4 %all_to_all.107.s_ref = f32[32,2,512]{2,1,0:T(2,128)} all-to-all(f32[32,2,512]{2,1,0:T(2,128)} %get-tuple-element.169), channel_id=1, replica_groups=mesh['dp'=4,'fsdp'=8] {'dp','fsdp'}, dimensions={0} | all-to-all | bytes 262144 | tf_op jit(solution)/shard_map/all_to_all | solution.py:501
  275.5 6.9 forward_resid.3
  285.1 8.1 %all-to-all-done.7.s_ref = f32[32,2,512]{2,1,0:T(2,128)S(1)} async-done(((f32[32,2,512]{2,1,0:T(2,128)}), f32[32,2,512]{2,1,0:T(2,128)S(1)}, u32[]{:S(2)}, u32[]{:S(2)}) %all-to-all-start.7) | async-done | bytes 131104 | tf_op jit(solution)/shard_map/all_to_all | solution.py:501
  293.9 8.4 %forward_join.1 = (bf16[1024,1024]{1,0:T(8,128)(2,1)}, f32[8,512]{1,0:T(8,128)}, f32[1024,1024]{1,0:T(8,128)}, f32[32,2,1024]{2,1,0:T(2,128)}) custom-call(f32[1024,512]{1,0:T(8,128)} %get-tuple-element.171.z_ref.zp_ref, f32[32,2,512]{2,1,0:T(2,128)} %copy-done.12, f32[66]{0:T(128)} %pad_maximum_fusion.5.cnt_ref, f32[1,512]{1,0:T(1,128)} %bitcast.183, ...), custom_call_target="tpu_custom_call" | custom-call | bytes 25165824 | tf_op jit(solution)/shard_map/forward_join/pallas_call | solution.py:624
  302.3 13.3 %all_to_all.108.s_ref = f32[32,2,1024]{2,1,0:T(2,128)} all-to-all(f32[32,2,1024]{2,1,0:T(2,128)} %get-tuple-element.175), channel_id=1, replica_groups=mesh['dp'=4,'fsdp'=8] {'dp','fsdp'}, dimensions={0} | all-to-all | bytes 524288 | tf_op jit(solution)/shard_map/all_to_all | solution.py:501
  315.6 7.4 %top.1 = (bf16[1024,1024]{1,0:T(8,128)(2,1)}, f32[8,1024]{1,0:T(8,128)}, bf16[1024,1024]{1,0:T(8,128)(2,1)}, f32[32,2,1024]{2,1,0:T(2,128)}) custom-call(f32[1024,1024]{1,0:T(8,128)} %get-tuple-element.174.z_ref, f32[32,2,1024]{2,1,0:T(2,128)} %all_to_all.108.s_ref, f32[66]{0:T(128)} %pad_maximum_fusion.5.cnt_ref, f32[1,1024]{1,0:T(1,128)} %bitcast.177, ...), custom_call_target="tpu_custom_call" | custom-call | bytes 33554432 | tf_op jit(solution)/shard_map/top/pallas_call | solution.py:655
  323.0 13.3 %all_to_all.109.s_ref = f32[32,2,1024]{2,1,0:T(2,128)} all-to-all(f32[32,2,1024]{2,1,0:T(2,128)} %get-tuple-element.179), channel_id=1, replica_groups=mesh['dp'=4,'fsdp'=8] {'dp','fsdp'}, dimensions={0} | all-to-all | bytes 524288 | tf_op jit(solution)/shard_map/all_to_all | solution.py:501
  336.3 9.4 %backward_part.1 = (bf16[1024,1024]{1,0:T(8,128)(2,1)}, f32[8,1024]{1,0:T(8,128)}, f32[1024,512]{1,0:T(8,128)}, bf16[1024,512]{1,0:T(8,128)(2,1)}, f32[32,2,512]{2,1,0:T(2,128)}) custom-call(bf16[1024,1024]{1,0:T(8,128)(2,1)} %get-tuple-element.177.g_ref, f32[1024,1024]{1,0:T(8,128)} %get-tuple-element.174.z_ref, f32[8,1024]{1,0:T(8,128)} %get-tuple-element.273.mv_ref, ...), custom_call_target="tpu_custom_call" | custom-call | bytes 25165824 | tf_op jit(solution)/shard_map/backward_part/pallas_call | solution.py:712
  348.5 5.3 convolution_convert_fusion
  357.3 7.0 backward_keep.1
  369.9 6.4 all-to-all-done.11.s_ref
  376.9 11.4 %backward_three.2 = (bf16[1024,512]{1,0:T(8,128)(2,1)}, f32[8,512]{1,0:T(8,128)}, bf16[1024,512]{1,0:T(8,128)(2,1)}, f32[32,2,512]{2,1,0:T(2,128)}) custom-call(bf16[1024,512]{1,0:T(8,128)(2,1)} %get-tuple-element.187.g_ref, f32[1024,512]{1,0:T(8,128)} %get-tuple-element.168.z_ref.zp_ref, f32[8,512]{1,0:T(8,128)} %get-tuple-element.271.mvp_ref.mv_ref, ...), custom_call_target="tpu_custom_call" | custom-call | flops 4831838208 | bytes 25165824 | tf_op jit(solution)/shard_map/backward_three/pallas_call | solution.py:712
  391.4 9.5 %weight_grad_1.3 = bf16[8,9,64,512]{3,2,1,0:T(8,128)(2,1)} custom-call(bf16[1024,512]{1,0:T(8,128)(2,1)} %get-tuple-element.195.x_ref, bf16[9,1024,128]{2,1,0:T(8,128)(2,1)} %get-tuple-element.162.rest_0_.m_ref, bf16[1024,512]{1,0:T(8,128)(2,1)} %get-tuple-element.196.dz_ref), custom_call_target="tpu_custom_call" | custom-call | flops 4831838208 | bytes 4194304 | tf_op jit(solution)/shard_map/weight_grad_1/pallas_call | solution.py:729
  401.5 7.3 %backward_add.1 = (bf16[1024,512]{1,0:T(8,128)(2,1)}, f32[8,512]{1,0:T(8,128)}, f32[1024,512]{1,0:T(8,128)}, bf16[1024,512]{1,0:T(8,128)(2,1)}, f32[32,2,512]{2,1,0:T(2,128)}) custom-call(bf16[1024,512]{1,0:T(8,128)(2,1)} %get-tuple-element.193.g_ref, f32[1024,512]{1,0:T(8,128)} %get-tuple-element.166.z_ref.zp_ref, ...), custom_call_target="tpu_custom_call" | custom-call | bytes 25165824 | tf_op jit(solution)/shard_map/backward_add/pallas_call | solution.py:712
  408.9 5.8 all-to-all-start.13
  417.4 7.4 %all-to-all-done.13.s_ref = f32[32,2,512]{2,1,0:T(2,128)S(1)} async-done(((f32[32,2,512]{2,1,0:T(2,128)}), f32[32,2,512]{2,1,0:T(2,128)S(1)}, u32[]{:S(2)}, u32[]{:S(2)}) %all-to-all-start.13) | async-done | bytes 131104 | tf_op jit(solution)/shard_map/all_to_all | solution.py:501
  425.5 11.5 %backward_three.3 = (bf16[1024,512]{1,0:T(8,128)(2,1)}, f32[8,512]{1,0:T(8,128)}, bf16[1024,512]{1,0:T(8,128)(2,1)}, f32[32,2,512]{2,1,0:T(2,128)}) custom-call(bf16[1024,512]{1,0:T(8,128)(2,1)} %get-tuple-element.201.g_ref, f32[1024,512]{1,0:T(8,128)} %get-tuple-element.163.z_ref.zp_ref, f32[8,512]{1,0:T(8,128)} %get-tuple-element.269.mvp_ref.mv_ref, ...), custom_call_target="tpu_custom_call" | custom-call | flops 4831838208 | bytes 25165824 | tf_op jit(solution)/shard_map/backward_three/pallas_call | solution.py:712
  439.8 6.8 weight_grad_1.4
  446.5 6.0 weight_grad_1.5
  453.2 9.7 %backward_merge.1 = (bf16[1024,512]{1,0:T(8,128)(2,1)}, f32[8,512]{1,0:T(8,128)}, bf16[1024,1024]{1,0:T(8,128)(2,1)}, f32[32,2,1024]{2,1,0:T(2,128)}) custom-call(bf16[1024,512]{1,0:T(8,128)(2,1)} %get-tuple-element.212.g_ref, f32[1024,512]{1,0:T(8,128)} %get-tuple-element.160.z_ref.zp_ref, f32[8,512]{1,0:T(8,128)} %get-tuple-element.268.mvp_ref.mv_ref, ...), custom_call_target="tpu_custom_call" | custom-call | bytes 33554432 | tf_op jit(solution)/shard_map/backward_merge/pallas_call | solution.py:712
  462.9 5.8 all-to-all-start.15
  476.2 8.1 %all-to-all-done.15.s_ref = f32[32,2,1024]{2,1,0:T(2,128)S(1)} async-done(((f32[32,2,1024]{2,1,0:T(2,128)}), f32[32,2,1024]{2,1,0:T(2,128)S(1)}, u32[]{:S(2)}, u32[]{:S(2)}) %all-to-all-start.15) | async-done | bytes 262176 | tf_op jit(solution)/shard_map/all_to_all | solution.py:501
  484.9 10.1 %backward_plain.1 = (bf16[1024,1024]{1,0:T(8,128)(2,1)}, f32[8,1024]{1,0:T(8,128)}, bf16[1024,1024]{1,0:T(8,128)(2,1)}, f32[32,2,1024]{2,1,0:T(2,128)}) custom-call(bf16[1024,1024]{1,0:T(8,128)(2,1)} %get-tuple-element.217.g_ref, f32[1024,1024]{1,0:T(8,128)} %get-tuple-element.158.z_ref.zp_ref, f32[8,1024]{1,0:T(8,128)} %get-tuple-element.267.mvp_ref.mv_ref, ...), custom_call_target="tpu_custom_call" | custom-call | bytes 33554432 | tf_op jit(solution)/shard_map/backward_plain/pallas_call | solution.py:712
  511.5 5.6 down_norm.1
  517.1 11.4 %weight_grad_2.2 = bf16[8,5,64,1024]{3,2,1,0:T(8,128)(2,1)} custom-call(bf16[4,1024,512]{2,1,0:T(8,128)(2,1)} %get-tuple-element.147.ph_ref.x_ref, bf16[9,1024,128]{2,1,0:T(8,128)(2,1)} %get-tuple-element.148.m_ref, bf16[1024,1024]{1,0:T(8,128)(2,1)} %get-tuple-element.237.dz_ref), custom_call_target="tpu_custom_call" | custom-call | flops 9663676416 | bytes 8388608 | tf_op jit(solution)/shard_map/weight_grad_2/pallas_call | solution.py:729
  541.6 10.1 %weight_grad_2.3 = bf16[4,512,1024]{2,1,0:T(8,128)(2,1)} custom-call(bf16[4,1024,512]{2,1,0:T(8,128)(2,1)} %get-tuple-element.147.ph_ref.x_ref, bf16[9,1024,128]{2,1,0:T(8,128)(2,1)} %get-tuple-element.148.m_ref, bf16[1024,1024]{1,0:T(8,128)(2,1)} %get-tuple-element.237.dz_ref), custom_call_target="tpu_custom_call" | custom-call | flops 9663676416 | bytes 8388608 | tf_op jit(solution)/shard_map/weight_grad_2/pallas_call | solution.py:729
  569.0 17.9 %input_grad.1 = bf16[4,16,2,32,512]{4,3,2,1,0:T(8,128)(2,1)} custom-call(bf16[1024,1024]{1,0:T(8,128)(2,1)} %get-tuple-element.237.dz_ref, bf16[9,1024,128]{2,1,0:T(8,128)(2,1)} %get-tuple-element.238.m_ref, bf16[8,5,64,1024]{3,2,1,0:T(8,128)(2,1)} %bitcast.242, bf16[4,8,128,512]{3,2,1,0:T(8,128)(2,1)} %bitcast_dynamic-update-slice_fusion.4.wb_ref), custom_call_target="tpu_custom_call" | custom-call | flops 9663676416 | bytes 33554432 | tf_op jit(solution)/shard_map/input_grad/pallas_call | solution.py:825
  587.0 33.6 %all-to-all-done.18 = bf16[4,288,512]{2,1,0:T(8,128)(2,1)S(1)} async-done(((bf16[4,288,512]{2,1,0:T(8,128)(2,1)}), bf16[4,288,512]{2,1,0:T(8,128)(2,1)S(1)}, u32[]{:S(2)}, u32[]{:S(2)}) %all-to-all-start.18) | async-done | bytes 1179680 | tf_op jit(solution)/shard_map/all_to_all | solution.py:750
  638.4 10.8 %all-to-all-done.19 = bf16[4,272,512]{2,1,0:T(8,128)(2,1)S(1)} async-done(((bf16[4,272,512]{2,1,0:T(8,128)(2,1)}), bf16[4,272,512]{2,1,0:T(8,128)(2,1)S(1)}, u32[]{:S(2)}, u32[]{:S(2)}) %all-to-all-start.19) | async-done | bytes 1114144 | tf_op jit(solution)/shard_map/all_to_all | solution.py:745
  649.5 11.8 %reduce-scatter.17.cloned.1.call-done = bf16[1,192,512]{2,1,0:T(8,128)(2,1)} async-done(((bf16[8,192,512]{2,1,0:T(8,128)(2,1)}), bf16[1,192,512]{2,1,0:T(8,128)(2,1)}) %reduce-scatter.17.cloned.1.call-update) | async-done | bytes 196624 | tf_op jit(solution)/shard_map/reduce_scatter | solution.py:741
  671.0 16.3 %all-to-all-done.20 = bf16[4,464,512]{2,1,0:T(8,128)(2,1)S(1)} async-done(((bf16[4,464,512]{2,1,0:T(8,128)(2,1)}), bf16[4,464,512]{2,1,0:T(8,128)(2,1)S(1)}, u32[]{:S(2)}, u32[]{:S(2)}) %all-to-all-start.20) | async-done | bytes 1900576 | tf_op jit(solution)/shard_map/all_to_all | solution.py:750
  (266 shorter events, 171.8 us)
Async XLA Ops:
  7.2 39.0 %all-gather.10.cloned.1.call-start = ((), (), s32[]{:S(2)}) async-start(), calls=%async_computation.27 | async-start | bytes 2359296 | tf_op jit(solution)/shard_map/all_gather | solution.py:447
  13.6 90.1 %all-gather.12.cloned.1.call-start = ((), (), s32[]{:S(2)}) async-start(), calls=%async_computation.34 | async-start | bytes 5898240 | tf_op jit(solution)/shard_map/all_gather | solution.py:447
  14.6 11.1 %copy-start.27 = (s32[4,2]{0,1:T(2,128)S(1)}, s32[4,2]{0,1:T(2,128)}, u32[]{:S(2)}) copy-start(s32[4,2]{0,1:T(2,128)} %param.16) | copy-start | bytes 100
  14.6 182.2 %all-gather.14.cloned.1.call-start = ((), (), s32[]{:S(2)}) async-start(), calls=%async_computation.35 | async-start | bytes 5308416 | tf_op jit(solution)/shard_map/all_gather | solution.py:447
  15.8 225.3 %all-gather.16.cloned.1.call-start = ((), (), s32[]{:S(2)}) async-start(), calls=%async_computation.36 | async-start | bytes 5308416 | tf_op jit(solution)/shard_map/all_gather | solution.py:447
  18.3 17.2 %all-to-all-start = ((f32[32,1,128]{2,1,0:T(1,128)}), f32[32,1,128]{2,1,0:T(1,128)S(1)}, u32[]{:S(2)}, u32[]{:S(2)}) async-start(f32[32,1,128]{2,1,0:T(1,128)} %broadcast_in_dim.47), calls=%async_computation | async-start | bytes 32768 | tf_op jit(solution)/shard_map/all_to_all | solution.py:494
  25.6 259.4 %all-gather.18.cloned.1.call-start = ((), (), s32[]{:S(2)}) async-start(), calls=%async_computation.37 | async-start | bytes 2359296 | tf_op jit(solution)/shard_map/all_gather | solution.py:490
  48.8 26.3 %collective-permute-start = (bf16[8,128,512]{2,1,0:T(8,128)(2,1)}, bf16[8,128,512]{2,1,0:T(8,128)(2,1)}, u32[]{:S(2)}, u32[]{:S(2)}) collective-permute-start(bf16[8,128,512]{2,1,0:T(8,128)(2,1)} %get-tuple-element.284), channel_id=1, source_target_pairs={{0,8},{8,0},{16,24},{24,16},{1,9},{9,1},{17,25},{25,17},{2,10},{10... | collective-permute-start | bytes 3145736 | tf_op jit(solution)/shard_map/ppermute | solution.py:468
  50.3 47.7 %collective-permute-start.1 = (bf16[8,128,512]{2,1,0:T(8,128)(2,1)}, bf16[8,128,512]{2,1,0:T(8,128)(2,1)S(1)}, u32[]{:S(2)}, u32[]{:S(2)}) collective-permute-start(bf16[8,128,512]{2,1,0:T(8,128)(2,1)} %get-tuple-element.284), channel_id=1, source_target_pairs={{0,16},{8,24},{16,0},{24,8},{1,17},{9,25},{17,1},{25,9},{2,18},{10... | collective-permute-start | bytes 3145736 | tf_op jit(solution)/shard_map/ppermute | solution.py:468
  51.8 47.3 %collective-permute-start.2 = (bf16[8,128,512]{2,1,0:T(8,128)(2,1)}, bf16[8,128,512]{2,1,0:T(8,128)(2,1)S(1)}, u32[]{:S(2)}, u32[]{:S(2)}) collective-permute-start(bf16[8,128,512]{2,1,0:T(8,128)(2,1)} %get-tuple-element.284), channel_id=1, source_target_pairs={{0,24},{8,16},{16,8},{24,0},{1,25},{9,17},{17,9},{25,1},{2,26},{10... | collective-permute-start | bytes 3145736 | tf_op jit(solution)/shard_map/ppermute | solution.py:468
  100.2 28.0 %collective-permute-start.3 = (bf16[8,128,512]{2,1,0:T(8,128)(2,1)S(1)}, bf16[8,128,512]{2,1,0:T(8,128)(2,1)S(1)}, u32[]{:S(2)}, u32[]{:S(2)}) collective-permute-start(bf16[8,128,512]{2,1,0:T(8,128)(2,1)S(1)} %get-tuple-element.151), channel_id=1, source_target_pairs={{0,8},{8,0},{16,24},{24,16},{1,9},{9,1},{17,25},{25,17},{2,10},{10... | collective-permute-start | bytes 3145736 | tf_op jit(solution)/shard_map/ppermute | solution.py:468
  100.3 48.4 %collective-permute-start.4 = (bf16[8,128,512]{2,1,0:T(8,128)(2,1)S(1)}, bf16[8,128,512]{2,1,0:T(8,128)(2,1)S(1)}, u32[]{:S(2)}, u32[]{:S(2)}) collective-permute-start(bf16[8,128,512]{2,1,0:T(8,128)(2,1)S(1)} %get-tuple-element.151), channel_id=1, source_target_pairs={{0,16},{8,24},{16,0},{24,8},{1,17},{9,25},{17,1},{25,9},{2,18},{10... | collective-permute-start | bytes 3145736 | tf_op jit(solution)/shard_map/ppermute | solution.py:468
  102.3 48.4 %collective-permute-start.5 = (bf16[8,128,512]{2,1,0:T(8,128)(2,1)S(1)}, bf16[8,128,512]{2,1,0:T(8,128)(2,1)}, u32[]{:S(2)}, u32[]{:S(2)}) collective-permute-start(bf16[8,128,512]{2,1,0:T(8,128)(2,1)S(1)} %get-tuple-element.151), channel_id=1, source_target_pairs={{0,24},{8,16},{16,8},{24,0},{1,25},{9,17},{17,9},{25,1},{2,26},{10... | collective-permute-start | bytes 3145736 | tf_op jit(solution)/shard_map/ppermute | solution.py:468
  103.7 19.7 %copy-start.25 = (f32[5632]{0:T(1024)S(1)}, f32[5632]{0:T(1024)}, u32[]{:S(2)}) copy-start(f32[5632]{0:T(1024)} %param.24) | copy-start | bytes 67588
  103.7 20.3 %copy-start.26 = (f32[5632]{0:T(1024)S(1)}, f32[5632]{0:T(1024)}, u32[]{:S(2)}) copy-start(f32[5632]{0:T(1024)} %param.25) | copy-start | bytes 67588
  120.4 30.5 %all-to-all-start.1 = ((f32[32,2,1024]{2,1,0:T(2,128)}), f32[32,2,1024]{2,1,0:T(2,128)S(1)}, u32[]{:S(2)}, u32[]{:S(2)}) async-start(f32[32,2,1024]{2,1,0:T(2,128)} %get-tuple-element.152), calls=%async_computation.1 | async-start | bytes 524288 | tf_op jit(solution)/shard_map/all_to_all | solution.py:501
  189.2 19.1 %all-to-all-start.3 = ((f32[32,2,512]{2,1,0:T(2,128)}), f32[32,2,512]{2,1,0:T(2,128)S(1)}, u32[]{:S(2)}, u32[]{:S(2)}) async-start(f32[32,2,512]{2,1,0:T(2,128)} %get-tuple-element.161), calls=%async_computation.3 | async-start | bytes 262144 | tf_op jit(solution)/shard_map/all_to_all | solution.py:501
  238.3 14.2 %all-to-all-start.5 = ((f32[32,2,512]{2,1,0:T(2,128)}), f32[32,2,512]{2,1,0:T(2,128)S(1)}, u32[]{:S(2)}, u32[]{:S(2)}) async-start(f32[32,2,512]{2,1,0:T(2,128)} %get-tuple-element.167), calls=%async_computation.5 | async-start | bytes 262144 | tf_op jit(solution)/shard_map/all_to_all | solution.py:501
  282.4 10.8 %all-to-all-start.7 = ((f32[32,2,512]{2,1,0:T(2,128)}), f32[32,2,512]{2,1,0:T(2,128)S(1)}, u32[]{:S(2)}, u32[]{:S(2)}) async-start(f32[32,2,512]{2,1,0:T(2,128)} %get-tuple-element.172), calls=%async_computation.7 | async-start | bytes 262144 | tf_op jit(solution)/shard_map/all_to_all | solution.py:501
  336.3 12.3 %copy-start.31 = (bf16[1024,1024]{1,0:T(8,128)(2,1)S(1)}, bf16[1024,1024]{1,0:T(8,128)(2,1)}, u32[]{:S(2)}) copy-start(bf16[1024,1024]{1,0:T(8,128)(2,1)} %get-tuple-element.183) | copy-start | bytes 6291460
  345.7 11.0 %all-to-all-start.10 = ((f32[32,2,512]{2,1,0:T(2,128)}), f32[32,2,512]{2,1,0:T(2,128)S(1)}, u32[]{:S(2)}, u32[]{:S(2)}) async-start(f32[32,2,512]{2,1,0:T(2,128)} %get-tuple-element.182), calls=%async_computation.10 | async-start | bytes 262144 | tf_op jit(solution)/shard_map/all_to_all | solution.py:501
  348.5 52.4 %reduce-scatter.7.cloned.1.call-start = ((), (), s32[]{:S(2)}) async-start(), calls=%async_computation.28 | async-start | bytes 2359296 | tf_op jit(solution)/shard_map/reduce_scatter | solution.py:741
  357.3 9.8 %copy-start.34 = (bf16[1024,512]{1,0:T(8,128)(2,1)S(1)}, bf16[1024,512]{1,0:T(8,128)(2,1)}, u32[]{:S(2)}) copy-start(bf16[1024,512]{1,0:T(8,128)(2,1)} %get-tuple-element.189) | copy-start | bytes 3145732
  364.3 11.9 %all-to-all-start.11 = ((f32[32,2,512]{2,1,0:T(2,128)}), f32[32,2,512]{2,1,0:T(2,128)S(1)}, u32[]{:S(2)}, u32[]{:S(2)}) async-start(f32[32,2,512]{2,1,0:T(2,128)} %get-tuple-element.188), calls=%async_computation.11 | async-start | bytes 262144 | tf_op jit(solution)/shard_map/all_to_all | solution.py:501
  388.3 12.6 %all-to-all-start.12 = ((f32[32,2,512]{2,1,0:T(2,128)}), f32[32,2,512]{2,1,0:T(2,128)S(1)}, u32[]{:S(2)}, u32[]{:S(2)}) async-start(f32[32,2,512]{2,1,0:T(2,128)} %get-tuple-element.194), calls=%async_computation.12 | async-start | bytes 262144 | tf_op jit(solution)/shard_map/all_to_all | solution.py:501
  391.3 92.9 %reduce-scatter.11.cloned.1.call-start = ((), (), s32[]{:S(2)}) async-start(), calls=%async_computation.30 | async-start | bytes 5308416 | tf_op jit(solution)/shard_map/reduce_scatter | solution.py:741
  401.5 13.1 %copy-start.33 = (bf16[1024,512]{1,0:T(8,128)(2,1)S(1)}, bf16[1024,512]{1,0:T(8,128)(2,1)}, u32[]{:S(2)}) copy-start(bf16[1024,512]{1,0:T(8,128)(2,1)} %get-tuple-element.203) | copy-start | bytes 3145732
  408.9 15.9 %all-to-all-start.13 = ((f32[32,2,512]{2,1,0:T(2,128)}), f32[32,2,512]{2,1,0:T(2,128)S(1)}, u32[]{:S(2)}, u32[]{:S(2)}) async-start(f32[32,2,512]{2,1,0:T(2,128)} %get-tuple-element.202), calls=%async_computation.14 | async-start | bytes 262144 | tf_op jit(solution)/shard_map/all_to_all | solution.py:501
  436.9 15.6 %all-to-all-start.14 = ((f32[32,2,512]{2,1,0:T(2,128)}), f32[32,2,512]{2,1,0:T(2,128)S(1)}, u32[]{:S(2)}, u32[]{:S(2)}) async-start(f32[32,2,512]{2,1,0:T(2,128)} %get-tuple-element.207), calls=%async_computation.15 | async-start | bytes 262144 | tf_op jit(solution)/shard_map/all_to_all | solution.py:501
  439.5 96.4 %reduce-scatter.9.cloned.1.call-start = ((), (), s32[]{:S(2)}) async-start(), calls=%async_computation.29 | async-start | bytes 2949120 | tf_op jit(solution)/shard_map/reduce_scatter | solution.py:741
  462.9 11.7 %copy-start.2 = (bf16[1024,1024]{1,0:T(8,128)(2,1)S(1)}, bf16[1024,1024]{1,0:T(8,128)(2,1)}, u32[]{:S(2)}) copy-start(bf16[1024,1024]{1,0:T(8,128)(2,1)} %get-tuple-element.173.rest_0_) | copy-start | bytes 6291460
  462.9 21.3 %all-to-all-start.15 = ((f32[32,2,1024]{2,1,0:T(2,128)}), f32[32,2,1024]{2,1,0:T(2,128)S(1)}, u32[]{:S(2)}, u32[]{:S(2)}) async-start(f32[32,2,1024]{2,1,0:T(2,128)} %get-tuple-element.218), calls=%async_computation.18 | async-start | bytes 524288 | tf_op jit(solution)/shard_map/all_to_all | solution.py:501
  471.1 36.0 %collective-permute-start.6 = (bf16[512,512]{1,0:T(8,128)(2,1)}, bf16[512,512]{1,0:T(8,128)(2,1)}, u32[]{:S(2)}, u32[]{:S(2)}) collective-permute-start(bf16[512,512]{1,0:T(8,128)(2,1)} %get-tuple-element.282), channel_id=1, source_target_pairs={{0,8},{8,0},{16,24},{24,16},{1,9},{9,1},{17,25},{25,17},{2,10},{10... | collective-permute-start | bytes 1572872 | tf_op jit(solution)/shard_map/ppermute | solution.py:468
  472.9 34.2 %collective-permute-start.7 = (bf16[512,512]{1,0:T(8,128)(2,1)S(1)}, bf16[512,512]{1,0:T(8,128)(2,1)}, u32[]{:S(2)}, u32[]{:S(2)}) collective-permute-start(bf16[512,512]{1,0:T(8,128)(2,1)S(1)} %get-tuple-element.281), channel_id=1, source_target_pairs={{0,16},{8,24},{16,0},{24,8},{1,17},{9,25},{17,1},{25,9},{2,18},{10... | collective-permute-start | bytes 1572872 | tf_op jit(solution)/shard_map/ppermute | solution.py:468
  474.4 32.8 %collective-permute-start.8 = (bf16[512,512]{1,0:T(8,128)(2,1)S(1)}, bf16[512,512]{1,0:T(8,128)(2,1)}, u32[]{:S(2)}, u32[]{:S(2)}) collective-permute-start(bf16[512,512]{1,0:T(8,128)(2,1)S(1)} %get-tuple-element.280), channel_id=1, source_target_pairs={{0,24},{8,16},{16,8},{24,0},{1,25},{9,17},{17,9},{25,1},{2,26},{10... | collective-permute-start | bytes 1572872 | tf_op jit(solution)/shard_map/ppermute | solution.py:468
  495.1 15.8 %all-to-all-start.16 = ((f32[32,2,1024]{2,1,0:T(2,128)}), f32[32,2,1024]{2,1,0:T(2,128)S(1)}, u32[]{:S(2)}, u32[]{:S(2)}) async-start(f32[32,2,1024]{2,1,0:T(2,128)} %get-tuple-element.223), calls=%async_computation.19 | async-start | bytes 524288 | tf_op jit(solution)/shard_map/all_to_all | solution.py:501
  497.7 132.1 %reduce-scatter.13.cloned.1.call-start = ((), (), s32[]{:S(2)}) async-start(), calls=%async_computation.31 | async-start | bytes 4128768 | tf_op jit(solution)/shard_map/reduce_scatter | solution.py:741
  510.8 118.9 %reduce-scatter.15.cloned.1.call-start = ((), (), s32[]{:S(2)}) async-start(), calls=%async_computation.32 | async-start | bytes 5898240 | tf_op jit(solution)/shard_map/reduce_scatter | solution.py:741
  528.5 7.4 %copy-start.17 = (bf16[128,1024]{1,0:T(8,128)(2,1)S(1)}, bf16[128,1024]{1,0:T(8,128)(2,1)}, u32[]{:S(2)}) copy-start(bf16[128,1024]{1,0:T(8,128)(2,1)} %reduce-scatter.7.cloned.1.call-done) | copy-start | bytes 786436
  528.6 7.5 %copy-start.8 = (bf16[1,9,64,512]{3,2,1,0:T(8,128)(2,1)S(1)}, bf16[1,9,64,512]{3,2,1,0:T(8,128)(2,1)}, u32[]{:S(2)}) copy-start(bf16[1,9,64,512]{3,2,1,0:T(8,128)(2,1)} %reduce-scatter.11.cloned.1.call-done) | copy-start | bytes 1769476
  538.1 18.3 %all-to-all-start.17 = ((bf16[4,288,512]{2,1,0:T(8,128)(2,1)}), bf16[4,288,512]{2,1,0:T(8,128)(2,1)S(1)}, u32[]{:S(2)}, u32[]{:S(2)}) async-start(bf16[4,288,512]{2,1,0:T(8,128)(2,1)} %bitcast.54), calls=%async_computation.20 | async-start | bytes 2359296 | tf_op jit(solution)/shard_map/all_to_all | solution.py:745
  560.6 61.8 %collective-permute-start.9 = (bf16[512,1024]{1,0:T(8,128)(2,1)}, bf16[512,1024]{1,0:T(8,128)(2,1)}, u32[]{:S(2)}, u32[]{:S(2)}) collective-permute-start(bf16[512,1024]{1,0:T(8,128)(2,1)} %get-tuple-element.279), channel_id=1, source_target_pairs={{0,8},{8,0},{16,24},{24,16},{1,9},{9,1},{17,25},{25,17},{2,10},{10... | collective-permute-start | bytes 3145736 | tf_op jit(solution)/shard_map/ppermute | solution.py:468
  562.0 60.4 %collective-permute-start.10 = (bf16[512,1024]{1,0:T(8,128)(2,1)}, bf16[512,1024]{1,0:T(8,128)(2,1)}, u32[]{:S(2)}, u32[]{:S(2)}) collective-permute-start(bf16[512,1024]{1,0:T(8,128)(2,1)} %get-tuple-element.278), channel_id=1, source_target_pairs={{0,16},{8,24},{16,0},{24,8},{1,17},{9,25},{17,1},{25,9},{2,18},{10... | collective-permute-start | bytes 3145736 | tf_op jit(solution)/shard_map/ppermute | solution.py:468
  562.6 59.8 %collective-permute-start.11 = (bf16[512,1024]{1,0:T(8,128)(2,1)}, bf16[512,1024]{1,0:T(8,128)(2,1)}, u32[]{:S(2)}, u32[]{:S(2)}) collective-permute-start(bf16[512,1024]{1,0:T(8,128)(2,1)} %get-tuple-element.277), channel_id=1, source_target_pairs={{0,24},{8,16},{16,8},{24,0},{1,25},{9,17},{17,9},{25,1},{2,26},{10... | collective-permute-start | bytes 3145736 | tf_op jit(solution)/shard_map/ppermute | solution.py:468
  565.2 55.4 %all-to-all-start.18 = ((bf16[4,288,512]{2,1,0:T(8,128)(2,1)}), bf16[4,288,512]{2,1,0:T(8,128)(2,1)S(1)}, u32[]{:S(2)}, u32[]{:S(2)}) async-start(bf16[4,288,512]{2,1,0:T(8,128)(2,1)} %broadcast_in_dim.56), calls=%async_computation.21 | async-start | bytes 2359296 | tf_op jit(solution)/shard_map/all_to_all | solution.py:750
  568.7 92.6 %reduce-scatter.17.cloned.1.call-start = ((), (), s32[]{:S(2)}) async-start(), calls=%async_computation.33 | async-start | bytes 1769472 | tf_op jit(solution)/shard_map/reduce_scatter | solution.py:741
  633.2 16.0 %all-to-all-start.19 = ((bf16[4,272,512]{2,1,0:T(8,128)(2,1)}), bf16[4,272,512]{2,1,0:T(8,128)(2,1)S(1)}, u32[]{:S(2)}, u32[]{:S(2)}) async-start(bf16[4,272,512]{2,1,0:T(8,128)(2,1)} %pad_maximum_fusion.2), calls=%async_computation.24 | async-start | bytes 2228224 | tf_op jit(solution)/shard_map/all_to_all | solution.py:745
  663.7 23.5 %all-to-all-start.20 = ((bf16[4,464,512]{2,1,0:T(8,128)(2,1)}), bf16[4,464,512]{2,1,0:T(8,128)(2,1)S(1)}, u32[]{:S(2)}, u32[]{:S(2)}) async-start(bf16[4,464,512]{2,1,0:T(8,128)(2,1)} %broadcast_in_dim.57), calls=%async_computation.26 | async-start | bytes 3801088 | tf_op jit(solution)/shard_map/all_to_all | solution.py:750
  (30 other events, 58.6 us)
Sparse Core Ops, SparseCore 0:
  13.8 32.3 all-gather.9
  47.8 55.1 all-gather.11
  104.6 55.6 all-gather.13
  161.8 57.6 all-gather.15
  220.9 31.3 all-gather.17
  356.8 36.0 reduce-scatter.6
  401.0 60.2 reduce-scatter.10
  463.6 40.9 reduce-scatter.8
  511.0 43.9 reduce-scatter.12
  557.1 58.2 reduce-scatter.14
  626.8 34.5 reduce-scatter.16
